TPU v7x, 32 devices: a whole 2x2x4 slice. The times are simulated.
32 devices in a mesh: dp: 4 (over x, core), seq: 8 (over z, y).
Axes of the slice: x: 2, y: 2, z: 4, core: 2. Of those that a mesh axis runs over, the one named last changes fastest.
Arguments:
- layer_input: bfloat16 [16, 2048, 768], P('dp', 'seq'), may hold values from -6 to 6
- cotangent: bfloat16 [16, 2048, 768], P('dp', 'seq'), may hold values from -6 to 6
- first_gain: bfloat16 [768], replicated, may hold values from 0.099609375 to 1.8984375
- light_inputs: bfloat16 [768, 2304], replicated, may hold values from -0.21875 to 0.21875
- light_output: bfloat16 [768, 768], replicated, may hold values from -0.875 to 0.875
- heavy_queries: bfloat16 [768, 768], replicated, may hold values from -0.21875 to 0.21875
- heavy_keyvalue: bfloat16 [768, 1536], replicated, may hold values from -0.21875 to 0.21875
- heavy_output: bfloat16 [768, 768], replicated, may hold values from -1.75 to 1.75
- second_gain: bfloat16 [768], replicated, may hold values from 0.099609375 to 1.8984375
- router: bfloat16 [768], replicated, may hold values from -0.21875 to 0.21875
- light_gates: bfloat16 [768, 2048], replicated, may hold values from -0.21875 to 0.21875
- light_down: bfloat16 [1024, 768], replicated, may hold values from -0.25 to 0.25
- heavy_gates: bfloat16 [768, 8192], replicated, may hold values from -0.21875 to 0.21875
- heavy_down: bfloat16 [4096, 768], replicated, may hold values from -0.25 to 0.25
- query_index: int32 [16, 512], P('dp', 'seq'), may hold values from 0 to 255, as said below
- query_count: int32 [16, 8], P('dp', 'seq'), may hold values from 16 to 64, as said below
- key_index: int32 [16, 512], P('dp', 'seq'), may hold values from 0 to 255, as said below
- key_count: int32 [16, 8], P('dp'), may hold values from 16 to 64, as said below
- feed_slot: int32 [16, 2048], P('dp', 'seq'), may hold values from -1 to 191, as said below
Outputs:
- output: bfloat16 [16, 2048, 768], P('dp', 'seq')
- input_grad: float32 [16, 2048, 768], P('dp', 'seq')
- first_gain_grad: float32 [768], P(('dp', 'seq'))
- light_inputs_grad: float32 [768, 2304], P(('dp', 'seq'))
- light_output_grad: float32 [768, 768], P(('dp', 'seq'))
- heavy_queries_grad: float32 [768, 768], P(('dp', 'seq'))
- heavy_keyvalue_grad: float32 [768, 1536], P(('dp', 'seq'))
- heavy_output_grad: float32 [768, 768], P(('dp', 'seq'))
- second_gain_grad: float32 [768], P(('dp', 'seq'))
- router_grad: float32 [768], P(('dp', 'seq'))
- light_gates_grad: float32 [768, 2048], P(('dp', 'seq'))
- light_down_grad: float32 [1024, 768], P(('dp', 'seq'))
- heavy_gates_grad: float32 [768, 8192], P(('dp', 'seq'))
- heavy_down_grad: float32 [4096, 768], P(('dp', 'seq'))
Inputs may be any that keep to these rules, and one draw needn't show every extreme that they name: `query_index`: within each device's 64 slots of a row the positions are distinct. `query_count`: in every row some device has all 64 slots live. `key_index`: within each device's 64 slots of a row the positions are distinct. `key_count`: in every row some device has all 64 slots live. `feed_slot`: A device's send buffer has 8 parts of 24 rows, part j for device j of seq; slot j * 24 + m lies in part j. The slots of one device's tokens are distinct. In every index of dp some device fills every part.
All inputs are finite; a program needn't handle non-finite values.
Results may differ from a plain program's by a relative error of at most 0.018.
Values may be sent and summed in bfloat16 or wider, within the bound.
A program may use at most 320 MiB of HBM per device.

v0:
```python
import jax
import jax.numpy as jnp
from jax import lax
from jax.sharding import PartitionSpec as P

D = 768
HL = 8
LHD = 96
HH = 12
HHD = 64
RADIUS = 128
QCAP = 64
KCAP = 64


epsilon = 1e-06
precise = lax.Precision.HIGHEST


def extended(cells, sides, width):
    for axis, dim in sides:
        count = lax.axis_size(axis)
        ends = count - 1
        head = lax.slice_in_dim(cells, 0, width, axis=dim)
        tail = lax.slice_in_dim(cells, cells.shape[dim] - width, cells.shape[dim], axis=dim)
        cells = jnp.concatenate(
            [
                lax.ppermute(tail, axis, [(i, (i + 1) % count) for i in range(ends)]),
                cells,
                lax.ppermute(head, axis, [((i + 1) % count, i) for i in range(ends)]),
            ],
            axis=dim,
        )
    return cells


def norm_rows(values, scales):
    return values * lax.rsqrt(jnp.mean(values * values, axis=-1, keepdims=True) + epsilon) * scales


def glu_rows(joined):
    split_at = joined.shape[-1] // 2
    return jax.nn.gelu(joined[..., :split_at]) * joined[..., split_at:]


def pick_rows(source, places):
    return jax.vmap(lambda matrix, indices: matrix[indices])(source, places)


def put_rows(canvas, places, addend):
    return jax.vmap(lambda matrix, indices, extra: matrix.at[indices].add(extra))(
        canvas, places, addend
    )


def band_keep(seq_rank, tokens, seq_devices):
    row_pos = seq_rank * tokens + jnp.arange(tokens, dtype=jnp.int32)
    col_pos = seq_rank * tokens - RADIUS + jnp.arange(tokens + 2 * RADIUS, dtype=jnp.int32)
    inside = (col_pos[None, :] >= 0) & (col_pos[None, :] < tokens * seq_devices)
    return (jnp.abs(row_pos[:, None] - col_pos[None, :]) <= RADIUS) & inside


def masked_scores(queries, keys_all, keep_mask, factor):
    scores = (
        jnp.einsum("pqhe,pkhe->phqk", queries, keys_all, preferred_element_type=jnp.float32)
        * factor
    )
    return jnp.where(keep_mask, scores, -1e30)


def attend(queries, keys_all, values_all, keep_mask, factor):
    scores = masked_scores(queries, keys_all, keep_mask, factor)
    largest = jnp.max(scores, axis=-1, keepdims=True)
    raised = jnp.exp(scores - largest)
    summed = jnp.sum(raised, axis=-1, keepdims=True)
    probs = raised / summed
    mixture = jnp.einsum(
        "phqk,pkhe->pqhe",
        probs.astype(jnp.bfloat16),
        values_all,
        preferred_element_type=jnp.float32,
    )
    return (mixture.astype(jnp.bfloat16), largest + jnp.log(summed))


def attend_back(queries, keys_all, values_all, keep_mask, factor, log_total, grad_mixture):
    probs = jnp.exp(masked_scores(queries, keys_all, keep_mask, factor) - log_total)
    grad_probs = jnp.einsum(
        "pqhe,pkhe->phqk", grad_mixture, values_all, preferred_element_type=jnp.float32
    )
    grad_values = jnp.einsum(
        "phqk,pqhe->pkhe",
        probs.astype(jnp.bfloat16),
        grad_mixture,
        preferred_element_type=jnp.float32,
    )
    inner = jnp.sum(probs * grad_probs, axis=-1, keepdims=True)
    grad_scores = (probs * (grad_probs - inner)).astype(jnp.bfloat16)
    grad_queries = (
        jnp.einsum("phqk,pkhe->pqhe", grad_scores, keys_all, preferred_element_type=jnp.float32)
        * factor
    )
    grad_keys = (
        jnp.einsum("phqk,pqhe->pkhe", grad_scores, queries, preferred_element_type=jnp.float32)
        * factor
    )
    return (grad_queries, grad_keys, grad_values)


def per_device(
    layer_input,
    cotangent,
    first_gain,
    light_inputs,
    light_output,
    heavy_queries,
    heavy_keyvalue,
    heavy_output,
    second_gain,
    router,
    light_gates,
    light_down,
    heavy_gates,
    heavy_down,
    query_index,
    query_count,
    key_index,
    key_count,
    feed_slot,
):
    pieces, tokens = (layer_input.shape[0], layer_input.shape[1])
    seq_devices = lax.axis_size("seq")
    seq_rank = lax.axis_index("seq")
    capacity = max(2, 3 * pieces * tokens // (16 * seq_devices))
    slots_total = seq_devices * capacity
    light_factor = LHD ** (-0.5)
    heavy_factor = HHD ** (-0.5)
    inputs = layer_input.astype(jnp.float32)
    gain_first = first_gain.astype(jnp.float32)
    normed_first = norm_rows(inputs, gain_first).astype(jnp.bfloat16)
    light_query_flat = jnp.einsum(
        "ptd,de->pte", normed_first, light_inputs[:, :D], preferred_element_type=jnp.float32
    ).astype(jnp.bfloat16)
    light_local = jnp.einsum(
        "ptd,de->pte", normed_first, light_inputs[:, D:], preferred_element_type=jnp.float32
    ).astype(jnp.bfloat16)
    light_pairs = extended(light_local, (("seq", 1),), RADIUS)
    light_query = light_query_flat.reshape(pieces, tokens, HL, LHD)
    light_keys = light_pairs[..., :D].reshape(pieces, tokens + 2 * RADIUS, HL, LHD)
    light_values = light_pairs[..., D:].reshape(pieces, tokens + 2 * RADIUS, HL, LHD)
    band_mask = band_keep(seq_rank, tokens, seq_devices)
    light_mixed, light_total = attend(
        light_query, light_keys, light_values, band_mask, light_factor
    )
    light_att = light_mixed.reshape(pieces, tokens, D)
    query_rows = pick_rows(normed_first, query_index)
    key_rows = pick_rows(normed_first, key_index)
    heavy_query = (
        jnp.einsum("pqd,de->pqe", query_rows, heavy_queries, preferred_element_type=jnp.float32)
        .astype(jnp.bfloat16)
        .reshape(pieces, QCAP, HH, HHD)
    )
    heavy_local = jnp.einsum(
        "pkd,de->pke", key_rows, heavy_keyvalue, preferred_element_type=jnp.float32
    ).astype(jnp.bfloat16)
    heavy_pairs = lax.all_gather(heavy_local, "seq", axis=1, tiled=True)
    key_slots = heavy_pairs.shape[1]
    slot_range = jnp.arange(key_slots, dtype=jnp.int32)
    key_live = (slot_range % KCAP)[None, :] < jnp.repeat(key_count, KCAP, axis=1)
    key_mask = key_live[:, None, None, :]
    query_live = jnp.arange(QCAP, dtype=jnp.int32)[None, :] < query_count
    heavy_mixed, heavy_total = attend(
        heavy_query,
        heavy_pairs[..., :D].reshape(pieces, key_slots, HH, HHD),
        heavy_pairs[..., D:].reshape(pieces, key_slots, HH, HHD),
        key_mask,
        heavy_factor,
    )
    heavy_att = heavy_mixed.reshape(pieces, QCAP, D)
    heavy_rows = jnp.einsum(
        "pqe,ed->pqd", heavy_att, heavy_output, preferred_element_type=jnp.float32
    )
    light_branch = jnp.einsum(
        "pte,ed->ptd", light_att, light_output, preferred_element_type=jnp.float32
    )
    middle = put_rows(
        inputs + light_branch, query_index, jnp.where(query_live[..., None], heavy_rows, 0.0)
    )
    gain_second = second_gain.astype(jnp.float32)
    normed_second = norm_rows(middle, gain_second).astype(jnp.bfloat16)
    light_pre = jnp.einsum(
        "ptd,de->pte", normed_second, light_gates, preferred_element_type=jnp.float32
    )
    light_hidden = glu_rows(light_pre).astype(jnp.bfloat16)
    light_feed = jnp.einsum(
        "pte,ed->ptd", light_hidden, light_down, preferred_element_type=jnp.float32
    )
    gating = jax.nn.sigmoid(
        jnp.einsum("ptd,d->pt", normed_second, router, preferred_element_type=jnp.float32)
    ).reshape(-1)
    flat_rows = normed_second.reshape(pieces * tokens, D)
    flat_slot = feed_slot.reshape(-1)
    is_routed = flat_slot >= 0
    targets = jnp.where(is_routed, flat_slot, slots_total)
    fetch = jnp.clip(flat_slot, 0, slots_total - 1)
    send_rows = (
        jnp.zeros((slots_total, D), jnp.bfloat16)
        .at[targets]
        .set(flat_rows, mode="drop")
        .reshape(seq_devices, capacity, D)
    )
    arrived = lax.all_to_all(send_rows, "seq", split_axis=0, concat_axis=0, tiled=True)
    pre_rows = jnp.einsum("ncd,de->nce", arrived, heavy_gates, preferred_element_type=jnp.float32)
    hidden_rows = glu_rows(pre_rows).astype(jnp.bfloat16)
    result_rows = jnp.einsum(
        "nce,ed->ncd", hidden_rows, heavy_down, preferred_element_type=jnp.float32
    ).astype(jnp.bfloat16)
    returned_rows = lax.all_to_all(result_rows, "seq", split_axis=0, concat_axis=0, tiled=True)
    token_result = jnp.where(
        is_routed[:, None], returned_rows.reshape(slots_total, D)[fetch], 0.0
    ).astype(jnp.float32)
    heavy_feed = (gating[:, None] * token_result).reshape(pieces, tokens, D)
    output = (middle + light_feed + heavy_feed).astype(jnp.bfloat16)
    grad_out = cotangent.astype(jnp.float32)
    light_down_grad = jnp.einsum(
        "pte,ptd->ed", light_hidden, cotangent, preferred_element_type=jnp.float32
    )
    grad_light_hidden = jnp.einsum(
        "ptd,ed->pte", cotangent, light_down, preferred_element_type=jnp.float32
    )
    light_glu_pull = jax.vjp(glu_rows, light_pre)[1]
    grad_light_pre = light_glu_pull(grad_light_hidden)[0].astype(jnp.bfloat16)
    light_gates_grad = jnp.einsum(
        "ptd,pte->de", normed_second, grad_light_pre, preferred_element_type=jnp.float32
    )
    grad_second = jnp.einsum(
        "pte,de->ptd", grad_light_pre, light_gates, preferred_element_type=jnp.float32
    )
    flat_grad = grad_out.reshape(pieces * tokens, D)
    grad_gating = jnp.sum(flat_grad * token_result, axis=-1)
    grad_logit = grad_gating * gating * (1.0 - gating)
    router_grad = jnp.dot(grad_logit, flat_rows.astype(jnp.float32), precision=precise)
    grad_token = jnp.where(is_routed[:, None], gating[:, None] * flat_grad, 0.0).astype(
        jnp.bfloat16
    )
    grad_send = (
        jnp.zeros((slots_total, D), jnp.bfloat16)
        .at[targets]
        .set(grad_token, mode="drop")
        .reshape(seq_devices, capacity, D)
    )
    grad_arrived = lax.all_to_all(grad_send, "seq", split_axis=0, concat_axis=0, tiled=True)
    heavy_hidden = glu_rows(pre_rows).astype(jnp.bfloat16)
    heavy_down_grad = jnp.einsum(
        "nce,ncd->ed", heavy_hidden, grad_arrived, preferred_element_type=jnp.float32
    )
    grad_heavy_hidden = jnp.einsum(
        "ncd,ed->nce", grad_arrived, heavy_down, preferred_element_type=jnp.float32
    )
    heavy_glu_pull = jax.vjp(glu_rows, pre_rows)[1]
    grad_heavy_pre = heavy_glu_pull(grad_heavy_hidden)[0].astype(jnp.bfloat16)
    heavy_gates_grad = jnp.einsum(
        "ncd,nce->de", arrived, grad_heavy_pre, preferred_element_type=jnp.float32
    )
    grad_arrived_rows = jnp.einsum(
        "nce,de->ncd", grad_heavy_pre, heavy_gates, preferred_element_type=jnp.float32
    )
    grad_returned = lax.all_to_all(
        grad_arrived_rows.astype(jnp.bfloat16), "seq", split_axis=0, concat_axis=0, tiled=True
    ).astype(grad_arrived_rows.dtype)
    grad_routed = jnp.where(is_routed[:, None], grad_returned.reshape(slots_total, D)[fetch], 0.0)
    grad_second = grad_second + (
        grad_routed + grad_logit[:, None] * router.astype(jnp.float32)
    ).reshape(pieces, tokens, D)
    second_pull = jax.vjp(norm_rows, middle, gain_second)[1]
    grad_mid_norm, second_gain_grad = second_pull(grad_second)
    grad_middle = grad_out + grad_mid_norm
    grad_mid_low = grad_middle.astype(jnp.bfloat16)
    light_output_grad = jnp.einsum(
        "pte,ptd->ed", light_att, grad_mid_low, preferred_element_type=jnp.float32
    )
    grad_light_att = jnp.einsum(
        "ptd,ed->pte", grad_mid_low, light_output, preferred_element_type=jnp.float32
    ).astype(jnp.bfloat16)
    grad_lq, grad_lk, grad_lv = attend_back(
        light_query,
        light_keys,
        light_values,
        band_mask,
        light_factor,
        light_total,
        grad_light_att.reshape(pieces, tokens, HL, LHD),
    )
    edge_grads = jnp.concatenate(
        [
            grad_lk.reshape(pieces, tokens + 2 * RADIUS, D),
            grad_lv.reshape(pieces, tokens + 2 * RADIUS, D),
        ],
        axis=-1,
    )
    outgoing = jnp.zeros((pieces, tokens, 2 * D), jnp.float32)
    outgoing = (
        outgoing.at[:, :RADIUS]
        .set(edge_grads[:, :RADIUS])
        .at[:, tokens - RADIUS :]
        .set(edge_grads[:, tokens + RADIUS :])
    )
    incoming = extended(outgoing.astype(jnp.bfloat16), (("seq", 1),), RADIUS).astype(outgoing.dtype)
    own_grads = edge_grads[:, RADIUS : RADIUS + tokens]
    own_grads = (
        own_grads.at[:, :RADIUS]
        .add(incoming[:, :RADIUS])
        .at[:, tokens - RADIUS :]
        .add(incoming[:, tokens + RADIUS :])
    )
    grad_lq_low = grad_lq.reshape(pieces, tokens, D).astype(jnp.bfloat16)
    grad_pairs_low = own_grads.astype(jnp.bfloat16)
    light_inputs_grad = jnp.concatenate(
        [
            jnp.einsum(
                "ptd,pte->de", normed_first, grad_lq_low, preferred_element_type=jnp.float32
            ),
            jnp.einsum(
                "ptd,pte->de", normed_first, grad_pairs_low, preferred_element_type=jnp.float32
            ),
        ],
        axis=1,
    )
    grad_first = jnp.einsum(
        "pte,de->ptd", grad_lq_low, light_inputs[:, :D], preferred_element_type=jnp.float32
    )
    grad_first = grad_first + jnp.einsum(
        "pte,de->ptd", grad_pairs_low, light_inputs[:, D:], preferred_element_type=jnp.float32
    )
    back_pairs = lax.all_gather(heavy_local, "seq", axis=1, tiled=True)
    grad_query_rows = jnp.where(query_live[..., None], pick_rows(grad_mid_low, query_index), 0.0)
    heavy_output_grad = jnp.einsum(
        "pqe,pqd->ed", heavy_att, grad_query_rows, preferred_element_type=jnp.float32
    )
    grad_heavy_att = jnp.einsum(
        "pqd,ed->pqe", grad_query_rows, heavy_output, preferred_element_type=jnp.float32
    ).astype(jnp.bfloat16)
    grad_hq, grad_hk, grad_hv = attend_back(
        heavy_query,
        back_pairs[..., :D].reshape(pieces, key_slots, HH, HHD),
        back_pairs[..., D:].reshape(pieces, key_slots, HH, HHD),
        key_mask,
        heavy_factor,
        heavy_total,
        grad_heavy_att.reshape(pieces, QCAP, HH, HHD),
    )
    grad_all_pairs = jnp.concatenate(
        [grad_hk.reshape(pieces, key_slots, D), grad_hv.reshape(pieces, key_slots, D)], axis=-1
    )
    grad_key_pairs = lax.psum_scatter(
        grad_all_pairs.astype(jnp.bfloat16), "seq", scatter_dimension=1, tiled=True
    )
    heavy_keyvalue_grad = jnp.einsum(
        "pkd,pke->de", key_rows, grad_key_pairs, preferred_element_type=jnp.float32
    )
    grad_hq_low = grad_hq.reshape(pieces, QCAP, D).astype(jnp.bfloat16)
    heavy_queries_grad = jnp.einsum(
        "pqd,pqe->de", query_rows, grad_hq_low, preferred_element_type=jnp.float32
    )
    grad_first = put_rows(
        grad_first,
        query_index,
        jnp.einsum("pqe,de->pqd", grad_hq_low, heavy_queries, preferred_element_type=jnp.float32),
    )
    grad_first = put_rows(
        grad_first,
        key_index,
        jnp.einsum(
            "pke,de->pkd", grad_key_pairs, heavy_keyvalue, preferred_element_type=jnp.float32
        ),
    )
    first_pull = jax.vjp(norm_rows, inputs, gain_first)[1]
    grad_in_norm, first_gain_grad = first_pull(grad_first)
    input_grad = grad_middle + grad_in_norm
    (
        first_gain_grad,
        light_inputs_grad,
        light_output_grad,
        heavy_queries_grad,
        heavy_keyvalue_grad,
        heavy_output_grad,
        second_gain_grad,
        router_grad,
        light_gates_grad,
        light_down_grad,
        heavy_gates_grad,
        heavy_down_grad,
    ) = (
        lax.psum_scatter(first_gain_grad, ("dp", "seq"), scatter_dimension=0, tiled=True),
        lax.psum_scatter(light_inputs_grad, ("dp", "seq"), scatter_dimension=0, tiled=True),
        lax.psum_scatter(light_output_grad, ("dp", "seq"), scatter_dimension=0, tiled=True),
        lax.psum_scatter(heavy_queries_grad, ("dp", "seq"), scatter_dimension=0, tiled=True),
        lax.psum_scatter(heavy_keyvalue_grad, ("dp", "seq"), scatter_dimension=0, tiled=True),
        lax.psum_scatter(heavy_output_grad, ("dp", "seq"), scatter_dimension=0, tiled=True),
        lax.psum_scatter(second_gain_grad, ("dp", "seq"), scatter_dimension=0, tiled=True),
        lax.psum_scatter(router_grad, ("dp", "seq"), scatter_dimension=0, tiled=True),
        lax.psum_scatter(light_gates_grad, ("dp", "seq"), scatter_dimension=0, tiled=True),
        lax.psum_scatter(light_down_grad, ("dp", "seq"), scatter_dimension=0, tiled=True),
        lax.psum_scatter(heavy_gates_grad, ("dp", "seq"), scatter_dimension=0, tiled=True),
        lax.psum_scatter(heavy_down_grad, ("dp", "seq"), scatter_dimension=0, tiled=True),
    )
    return (
        output,
        input_grad,
        first_gain_grad,
        light_inputs_grad,
        light_output_grad,
        heavy_queries_grad,
        heavy_keyvalue_grad,
        heavy_output_grad,
        second_gain_grad,
        router_grad,
        light_gates_grad,
        light_down_grad,
        heavy_gates_grad,
        heavy_down_grad,
    )


def solution(mesh):
    placed = (
        P("dp", "seq", None),
        P("dp", "seq", None),
        P(),
        P(),
        P(),
        P(),
        P(),
        P(),
        P(),
        P(),
        P(),
        P(),
        P(),
        P(),
        P("dp", "seq"),
        P("dp", "seq"),
        P("dp", "seq"),
        P("dp", None),
        P("dp", "seq"),
    )
    return jax.shard_map(
        per_device,
        mesh=mesh,
        in_specs=placed,
        out_specs=(
            P("dp", "seq", None),
            P("dp", "seq", None),
            P(("dp", "seq")),
            P(("dp", "seq"), None),
            P(("dp", "seq"), None),
            P(("dp", "seq"), None),
            P(("dp", "seq"), None),
            P(("dp", "seq"), None),
            P(("dp", "seq")),
            P(("dp", "seq")),
            P(("dp", "seq"), None),
            P(("dp", "seq"), None),
            P(("dp", "seq"), None),
            P(("dp", "seq"), None),
        ),
        check_vma=False,
    )
```

profile of v0, /device:TPU:0, one launch (start us, length us, event | category | flops | bytes accessed | tf_op | source)
XLA Modules:
  0.0 1735.2 jit_solution(9546512240312141386)
XLA Ops:
  28.4 6.1 collective-permute-start
  52.9 71.1 %collective-permute-done = bf16[4,128,1536]{2,1,0:T(8,128)(2,1)} collective-permute-done((bf16[4,128,1536]{2,1,0:T(8,128)(2,1)}, bf16[4,128,1536]{2,1,0:T(8,128)(2,1)}, u32[]{:S(2)}, u32[]{:S(2)}) %collective-permute-start) | collective-permute-done | bytes 1572896 | tf_op jit(solution)/shard_map/ppermute | solution.py:28
  140.1 7.2 fusion.137
  153.4 7.2 fusion.73
  160.6 5.4 convert_add_fusion
  166.1 5.9 fusion.133
  193.4 35.9 %scatter_fusion = f32[4,256,768]{2,1,0:T(8,128)} fusion(f32[4,256,768]{2,1,0:T(8,128)} %convert_add_fusion, s32[256]{0:T(256)S(1)} %reshape.525, f32[256,768]{1,0:T(8,128)} %bitcast.270), kind=kCustom, calls=%fused_computation.7 | custom fusion | flops 196608 | bytes 2361344 | tf_op jit(solution)/shard_map/vmap()/scatter-add | solution.py:51
  233.6 5.7 scatter_custom_fusion
  239.3 17.1 all_to_all.20
  256.4 6.1 fusion.4
  266.4 5.0 fusion.81
  276.9 6.6 all-to-all-done.1
  283.5 5.2 gather_fusion
  293.2 6.3 scatter_custom_fusion.1
  303.1 7.0 fusion.53
  312.0 9.9 fusion.97
  321.9 11.4 fusion.84
  337.4 10.7 fusion.79
  349.6 6.9 gather_fusion.1
  356.6 8.3 multiply_reduce_fusion.2
  377.5 6.1 multiply_reduce_fusion.1
  386.5 5.6 multiply_convert_fusion.2
  399.5 4.9 pad_maximum_fusion.2
  405.9 5.1 convolution_bitcast_fusion.5
  425.5 8.9 convolution_bitcast_fusion.2
  439.6 13.5 multiply_reduce_fusion
  453.1 9.2 fusion.6
  462.4 6.6 copy.98
  469.0 12.3 multiply_convert_fusion
  486.5 6.6 copy.97
  507.6 8.3 multiply_convert_fusion.4
  521.2 50.8 %collective-permute-done.2 = bf16[4,128,1536]{2,1,0:T(8,128)(2,1)S(1)} collective-permute-done((bf16[4,128,1536]{2,1,0:T(8,128)(2,1)}, bf16[4,128,1536]{2,1,0:T(8,128)(2,1)S(1)}, u32[]{:S(2)}, u32[]{:S(2)}) %collective-permute-start.2) | collective-permute-done | bytes 1572896 | tf_op jit(solution)/shard_map/ppermute | solution.py:28
  584.9 6.5 convolution_bitcast_fusion.1
  597.4 13.1 convolution_bitcast_fusion
  613.9 5.7 fusion.30
  622.7 4.9 fusion.68
  627.6 23.7 %scatter_fusion.1 = f32[4,256,768]{2,1,0:T(8,128)S(1)} fusion(f32[4,256,768]{2,1,0:T(8,128)S(1)} %fusion.68, s32[256]{0:T(256)S(1)} %copy-done.11, f32[256,768]{1,0:T(8,128)} %bitcast.269), kind=kCustom, calls=%fused_computation.8 | custom fusion | flops 196608 | bytes 2361344 | tf_op jit(solution)/shard_map/vmap()/scatter-add | solution.py:51
  654.9 23.8 %scatter_fusion.2 = f32[4,256,768]{2,1,0:T(8,128)S(1)} fusion(f32[4,256,768]{2,1,0:T(8,128)S(1)} %scatter_fusion.1, s32[256]{0:T(256)S(1)} %reshape.537, f32[256,768]{1,0:T(8,128)} %bitcast.277), kind=kCustom, calls=%fused_computation.9 | custom fusion | flops 196608 | bytes 2361344 | tf_op jit(solution)/shard_map/vmap()/scatter-add | solution.py:51
  683.0 44.0 %all-reduce.7 = (f32[768]{0:T(1024)S(1)}, f32[768]{0:T(1024)S(1)}, f32[768]{0:T(1024)S(1)}) all-reduce(f32[768]{0:T(1024)S(1)} %get-tuple-element.64, f32[768]{0:T(1024)S(1)} %copy-done.79, f32[768]{0:T(1024)S(1)} %convolution_reduce_fusion), channel_id=3, replica_groups=mesh['dp'=4,'seq'=8] {'dp','seq'}, use_global_device_ids=true, to_apply=%region_18.19.clone | all-reduce | flops 2304 | bytes 18432
  728.8 6.8 fusion.39
  735.6 12.0 reduce-scatter.15.cloned.1.call-done
  747.6 104.6 %reduce-scatter.21.cloned.1.call-done = f32[24,768]{1,0:T(8,128)} async-done(((f32[768,768]{1,0:T(8,128)}), f32[24,768]{1,0:T(8,128)}) %reduce-scatter.21.cloned.1.call-update) | async-done | bytes 73744 | tf_op jit(solution)/shard_map/reduce_scatter | solution.py:399
  852.2 103.8 %reduce-scatter.17.cloned.1.call-done = f32[24,768]{1,0:T(8,128)} async-done(((f32[768,768]{1,0:T(8,128)}), f32[24,768]{1,0:T(8,128)}) %reduce-scatter.17.cloned.1.call-update) | async-done | bytes 73744 | tf_op jit(solution)/shard_map/reduce_scatter | solution.py:397
  956.0 120.8 %reduce-scatter.23.cloned.1.call-done = f32[24,2048]{1,0:T(8,128)} async-done(((f32[768,2048]{1,0:T(8,128)}), f32[24,2048]{1,0:T(8,128)}) %reduce-scatter.23.cloned.1.call-update) | async-done | bytes 196624 | tf_op jit(solution)/shard_map/reduce_scatter | solution.py:402
  1076.8 124.6 %reduce-scatter.13.cloned.1.call-done = f32[24,2304]{1,0:T(8,128)} async-done(((f32[768,2304]{1,0:T(8,128)}), f32[24,2304]{1,0:T(8,128)}) %reduce-scatter.13.cloned.1.call-update) | async-done | bytes 221200 | tf_op jit(solution)/shard_map/reduce_scatter | solution.py:395
  1201.4 162.2 %reduce-scatter.29.cloned.1.call-done = f32[128,768]{1,0:T(8,128)} async-done(((f32[4096,768]{1,0:T(8,128)}), f32[128,768]{1,0:T(8,128)}) %reduce-scatter.29.cloned.1.call-update) | async-done | bytes 393232 | tf_op jit(solution)/shard_map/reduce_scatter | solution.py:405
  1363.6 112.1 %reduce-scatter.19.cloned.1.call-done = f32[24,1536]{1,0:T(8,128)} async-done(((f32[768,1536]{1,0:T(8,128)}), f32[24,1536]{1,0:T(8,128)}) %reduce-scatter.19.cloned.1.call-update) | async-done | bytes 147472 | tf_op jit(solution)/shard_map/reduce_scatter | solution.py:398
  1475.7 252.7 %reduce-scatter.27.cloned.1.call-done = f32[24,8192]{1,0:T(8,128)} async-done(((f32[768,8192]{1,0:T(8,128)}), f32[24,8192]{1,0:T(8,128)}) %reduce-scatter.27.cloned.1.call-update) | async-done | bytes 786448 | tf_op jit(solution)/shard_map/reduce_scatter | solution.py:404
  (312 shorter events, 215.6 us)
Async XLA Ops:
  7.2 295.9 %copy-start = (bf16[768,2048]{1,0:T(8,128)(2,1)S(1)}, bf16[768,2048]{1,0:T(8,128)(2,1)}, u32[]{:S(2)}) copy-start(bf16[768,2048]{1,0:T(8,128)(2,1)} %param.37) | copy-start | bytes 9437188
  7.2 158.9 %all-gather.2.cloned.1.call-start = ((), (), s32[]{:S(2)}) async-start(), calls=%async_computation.14 | async-start | bytes 7077888 | tf_op jit(solution)/shard_map/all_gather | solution.py:166
  25.7 10.0 copy-start.80
  25.7 10.0 copy-start.71
  25.8 10.0 copy-start.81
  25.8 10.2 copy-start.82
  28.4 95.7 %collective-permute-start = (bf16[4,128,1536]{2,1,0:T(8,128)(2,1)}, bf16[4,128,1536]{2,1,0:T(8,128)(2,1)}, u32[]{:S(2)}, u32[]{:S(2)}) collective-permute-start(bf16[4,128,1536]{2,1,0:T(8,128)(2,1)} %get-tuple-element.82), channel_id=1, source_target_pairs={{0,1},{1,2},{2,3},{3,4},{4,5},{5,6},{6,7},{8,9},{9,10},{10,11},{11... | collective-permute-start | bytes 4718600 | tf_op jit(solution)/shard_map/ppermute | solution.py:28
  34.4 89.6 %collective-permute-start.1 = (bf16[4,128,1536]{2,1,0:T(8,128)(2,1)}, bf16[4,128,1536]{2,1,0:T(8,128)(2,1)}, u32[]{:S(2)}, u32[]{:S(2)}) collective-permute-start(bf16[4,128,1536]{2,1,0:T(8,128)(2,1)} %get-tuple-element.83), channel_id=1, source_target_pairs={{1,0},{2,1},{3,2},{4,3},{5,4},{6,5},{7,6},{9,8},{10,9},{11,10},{12... | collective-permute-start | bytes 4718600 | tf_op jit(solution)/shard_map/ppermute | solution.py:30
  35.7 329.1 %copy-start.57 = (f32[768]{0:T(1024)}, f32[768]{0:T(1024)S(1)}, u32[]{:S(2)}) copy-start(f32[768]{0:T(1024)S(1)} %convert_element_type.149) | copy-start | bytes 9220
  35.9 8.8 copy-start.12
  36.0 157.4 %copy-start.10 = (s32[256]{0:T(256)}, s32[256]{0:T(256)S(1)}, u32[]{:S(2)}) copy-start(s32[256]{0:T(256)S(1)} %reshape.525) | copy-start | bytes 3076
  39.9 9.2 copy-start.38
  52.0 139.1 %copy-start.83 = (pred[4,64]{1,0:T(4,128)(4,1)}, pred[4,64]{1,0:T(4,128)(4,1)S(1)}, u32[]{:S(2)}) copy-start(pred[4,64]{1,0:T(4,128)(4,1)S(1)} %iota_compare_fusion.1) | copy-start | bytes 772
  151.3 9.3 copy-start.55
  232.1 132.8 %copy-start.59 = (f32[4,256]{1,0:T(4,128)}, f32[4,256]{1,0:T(4,128)S(1)}, u32[]{:S(2)}) copy-start(f32[4,256]{1,0:T(4,128)S(1)} %fusion.112) | copy-start | bytes 12292
  266.4 8.5 copy-start.77
  271.5 12.0 all-to-all-start.1
  274.9 81.6 %copy-start.75 = (pred[4,256]{1,0:T(4,128)(4,1)}, pred[4,256]{1,0:T(4,128)(4,1)S(1)}, u32[]{:S(2)}) copy-start(pred[4,256]{1,0:T(4,128)(4,1)S(1)} %broadcast_compare_fusion.1) | copy-start | bytes 3076
  291.5 18.5 %copy-start.73 = (f32[4,256]{1,0:T(4,128)}, f32[4,256]{1,0:T(4,128)S(1)}, u32[]{:S(2)}) copy-start(f32[4,256]{1,0:T(4,128)S(1)} %get-tuple-element.70) | copy-start | bytes 12292
  291.5 65.0 %copy-start.69 = (f32[4,256]{1,0:T(4,128)}, f32[4,256]{1,0:T(4,128)S(1)}, u32[]{:S(2)}) copy-start(f32[4,256]{1,0:T(4,128)S(1)} %get-tuple-element.69) | copy-start | bytes 12292
  299.5 12.5 all-to-all-start.2
  312.0 9.9 copy-start.53
  333.4 15.4 all-to-all-start.3
  337.3 254.2 %reduce-scatter.11.cloned.1.call-start = ((), (), s32[]{:S(2)}) async-start(), calls=%async_computation.15 | async-start | bytes 7077888 | tf_op jit(solution)/shard_map/reduce_scatter | solution.py:355
  356.5 9.9 copy-start.6
  356.5 9.9 copy-start.18
  404.5 331.1 %reduce-scatter.25.cloned.1.call-start = ((), (), s32[]{:S(2)}) async-start(), calls=%async_computation.22 | async-start | bytes 3244032 | tf_op jit(solution)/shard_map/reduce_scatter | solution.py:403
  411.1 336.6 %reduce-scatter.15.cloned.1.call-start = ((), (), s32[]{:S(2)}) async-start(), calls=%async_computation.17 | async-start | bytes 2433024 | tf_op jit(solution)/shard_map/reduce_scatter | solution.py:396
  415.8 436.5 %reduce-scatter.21.cloned.1.call-start = ((), (), s32[]{:S(2)}) async-start(), calls=%async_computation.20 | async-start | bytes 2433024 | tf_op jit(solution)/shard_map/reduce_scatter | solution.py:399
  419.1 536.9 %reduce-scatter.17.cloned.1.call-start = ((), (), s32[]{:S(2)}) async-start(), calls=%async_computation.18 | async-start | bytes 2433024 | tf_op jit(solution)/shard_map/reduce_scatter | solution.py:397
  425.4 651.4 %reduce-scatter.23.cloned.1.call-start = ((), (), s32[]{:S(2)}) async-start(), calls=%async_computation.21 | async-start | bytes 6488064 | tf_op jit(solution)/shard_map/reduce_scatter | solution.py:402
  434.4 767.0 %reduce-scatter.13.cloned.1.call-start = ((), (), s32[]{:S(2)}) async-start(), calls=%async_computation.16 | async-start | bytes 7299072 | tf_op jit(solution)/shard_map/reduce_scatter | solution.py:395
  469.0 12.3 copy-start.26
  499.9 20.3 %slice-start = ((s8[6291456]{0:T(1024)(128)(4,1)}), s8[4194304]{0:T(1024)(128)(4,1)S(1)}, s32[]{:S(2)}) async-start(s8[6291456]{0:T(1024)(128)(4,1)} %bitcast.238), calls=%async_computation.25 | async-start | bytes 8388608
  501.8 70.2 %collective-permute-start.2 = (bf16[4,128,1536]{2,1,0:T(8,128)(2,1)}, bf16[4,128,1536]{2,1,0:T(8,128)(2,1)S(1)}, u32[]{:S(2)}, u32[]{:S(2)}) collective-permute-start(bf16[4,128,1536]{2,1,0:T(8,128)(2,1)} %get-tuple-element.80), channel_id=1, source_target_pairs={{0,1},{1,2},{2,3},{3,4},{4,5},{5,6},{6,7},{8,9},{9,10},{10,11},{11... | collective-permute-start | bytes 4718600 | tf_op jit(solution)/shard_map/ppermute | solution.py:28
  505.9 10.0 copy-start.14
  505.9 14.3 slice-start.1
  505.9 66.0 %collective-permute-start.3 = (bf16[4,128,1536]{2,1,0:T(8,128)(2,1)}, bf16[4,128,1536]{2,1,0:T(8,128)(2,1)}, u32[]{:S(2)}, u32[]{:S(2)}) collective-permute-start(bf16[4,128,1536]{2,1,0:T(8,128)(2,1)} %get-tuple-element.81), channel_id=1, source_target_pairs={{1,0},{2,1},{3,2},{4,3},{5,4},{6,5},{7,6},{9,8},{10,9},{11,10},{12... | collective-permute-start | bytes 4718600 | tf_op jit(solution)/shard_map/ppermute | solution.py:30
  583.5 780.1 %reduce-scatter.29.cloned.1.call-start = ((), (), s32[]{:S(2)}) async-start(), calls=%async_computation.24 | async-start | bytes 12976128 | tf_op jit(solution)/shard_map/reduce_scatter | solution.py:405
  591.4 884.3 %reduce-scatter.19.cloned.1.call-start = ((), (), s32[]{:S(2)}) async-start(), calls=%async_computation.19 | async-start | bytes 4866048 | tf_op jit(solution)/shard_map/reduce_scatter | solution.py:398
  596.5 1132.0 %reduce-scatter.27.cloned.1.call-start = ((), (), s32[]{:S(2)}) async-start(), calls=%async_computation.23 | async-start | bytes 25952256 | tf_op jit(solution)/shard_map/reduce_scatter | solution.py:404
  654.9 25.4 %copy-start.62 = (f32[768]{0:T(1024)S(1)}, f32[768]{0:T(1024)}, u32[]{:S(2)}) copy-start(f32[768]{0:T(1024)} %copy-done.61) | copy-start | bytes 9220
  654.9 25.4 %copy-start.64 = (f32[4,256]{1,0:T(4,128)S(1)}, f32[4,256]{1,0:T(4,128)}, u32[]{:S(2)}) copy-start(f32[4,256]{1,0:T(4,128)} %copy-done.63) | copy-start | bytes 12292
  680.3 48.4 %copy-start.66 = (f32[4,256]{1,0:T(4,128)S(1)}, f32[4,256]{1,0:T(4,128)}, u32[]{:S(2)}) copy-start(f32[4,256]{1,0:T(4,128)} %copy-done.65) | copy-start | bytes 12292
  680.4 48.4 %copy-start.58 = (f32[768]{0:T(1024)S(1)}, f32[768]{0:T(1024)}, u32[]{:S(2)}) copy-start(f32[768]{0:T(1024)} %copy-done.57) | copy-start | bytes 9220
  680.4 48.4 %copy-start.60 = (f32[4,256]{1,0:T(4,128)S(1)}, f32[4,256]{1,0:T(4,128)}, u32[]{:S(2)}) copy-start(f32[4,256]{1,0:T(4,128)} %copy-done.59) | copy-start | bytes 12292
  680.4 48.4 %copy-start.68 = (f32[4,256]{1,0:T(4,128)S(1)}, f32[4,256]{1,0:T(4,128)}, u32[]{:S(2)}) copy-start(f32[4,256]{1,0:T(4,128)} %copy-done.67) | copy-start | bytes 12292
  728.8 999.6 %copy-start.1 = (bf16[768,2048]{1,0:T(8,128)(2,1)S(1)}, bf16[768,2048]{1,0:T(8,128)(2,1)}, u32[]{:S(2)}) copy-start(bf16[768,2048]{1,0:T(8,128)(2,1)} %param.37) | copy-start | bytes 9437188
  (61 other events, 201.6 us)
Sparse Core Ops, SparseCore 0:
  21.1 144.3 all-gather.1
  404.6 123.9 reduce-scatter.10
  534.6 108.9 reduce-scatter.24
  649.3 98.2 reduce-scatter.14
  754.2 97.9 reduce-scatter.20
  857.9 97.9 reduce-scatter.16
  963.1 113.6 reduce-scatter.22
  1083.0 118.3 reduce-scatter.12
  1209.0 154.5 reduce-scatter.28
  1369.5 106.1 reduce-scatter.18
  1483.8 244.5 reduce-scatter.26
where the time goes:
time: 1750 us; the launch traced here: 1740 us
  waiting for transfers between devices  1120 us (64%)
  matrix products  231 us (13%)
  other arithmetic  157 us (9%)
  local copies, waits for them, and re-layouts  123 us (7%)
  blocking collectives  61.1 us (3%)
  starting transfers between devices  24.8 us (1%)
    reduce_scatter x1, waiting for transfers between devices, per_device(): lax.psum_scatter(heavy_gates_grad, ('dp', 'seq'), scatter_dimension=0, ti...  253 us
    reduce_scatter x1, waiting for transfers between devices, per_device(): lax.psum_scatter(heavy_down_grad, ('dp', 'seq'), scatter_dimension=0, til...  162 us
    reduce_scatter x1, waiting for transfers between devices, per_device(): lax.psum_scatter(light_inputs_grad, ('dp', 'seq'), scatter_dimension=0, t...  125 us
    ppermute x2, waiting for transfers between devices, extended(): lax.ppermute(tail, axis, [(i, (i + 1) % count) for i in range(ends)])  122 us
    reduce_scatter x1, waiting for transfers between devices, per_device(): lax.psum_scatter(light_gates_grad, ('dp', 'seq'), scatter_dimension=0, ti...  121 us
    reduce_scatter x1, waiting for transfers between devices, per_device(): lax.psum_scatter(heavy_keyvalue_grad, ('dp', 'seq'), scatter_dimension=0,...  112 us
    reduce_scatter x1, waiting for transfers between devices, per_device(): lax.psum_scatter(heavy_output_grad, ('dp', 'seq'), scatter_dimension=0, t...  105 us
    reduce_scatter x1, waiting for transfers between devices, per_device(): lax.psum_scatter(heavy_queries_grad, ('dp', 'seq'), scatter_dimension=0,...  104 us
  transfers between devices with their start and end apart: 18, of which 12 were waited for; matrix products, arithmetic and copies ran while one was open for 17% of the time, Pallas kernels for 0%

commit v1 on v0

v1 whole, which is shorter than its diff:
```python
import functools
import jax
import jax.numpy as jnp
from jax import lax
from jax.experimental import pallas as pl
from jax.experimental.pallas import tpu as pltpu
from jax.sharding import PartitionSpec as P
D = 768
HL = 8
LHD = 96
HH = 12
HHD = 64
RADIUS = 128
QCAP = 64
KCAP = 64
CORES = 2
DEPTH = 4
MESH = pl.DeviceIdType.MESH
epsilon = 1e-06
bf16 = jnp.bfloat16
f32 = jnp.float32


def dot(left, right, over):
    return lax.dot_general(left, right, (over, ((), ())), preferred_element_type=f32)


def mm(left, right):
    return dot(left, right, ((1,), (0,)))


def mm_nt(left, right):
    return dot(left, right, ((1,), (1,)))


def mm_tn(left, right):
    return dot(left, right, ((0,), (0,)))


class Ring:
    def __init__(self, axis, stride, count):
        self.axis, self.stride, self.count = axis, stride, count
        self.place = (lax.axis_index(axis) // stride) % count

    def shift(self, value, by):
        total = lax.axis_size(self.axis)
        pairs = []
        for i in range(total):
            c = (i // self.stride) % self.count
            pairs.append((i, i + ((c + by) % self.count - c) * self.stride))
        return lax.ppermute(value, self.axis, pairs)

    def scatter_sum(self, value, dim):
        own = lax.dynamic_index_in_dim(value, self.place, dim, keepdims=False)
        total = own.astype(f32)
        for by in range(1, self.count):
            send = lax.dynamic_index_in_dim(
                value, (self.place + by) % self.count, dim, keepdims=False
            )
            total = total + self.shift(send, by).astype(f32)
        return total

    def gather(self, value):
        return jnp.stack([value] + [self.shift(value, by) for by in range(1, self.count)])

    def return_sum(self, stacked):
        total = stacked[0].astype(f32)
        for by in range(1, self.count):
            total = total + self.shift(stacked[by], self.count - by).astype(f32)
        return total


def norm_parts(values):
    scale = lax.rsqrt(jnp.mean(values * values, axis=-1, keepdims=True) + epsilon)
    return values * scale, scale


def norm_pull(grad, values, scale, gain):
    weighted = grad * gain
    inner = jnp.mean(weighted * values, axis=-1, keepdims=True)
    return scale * weighted - values * (scale * scale * scale) * inner


def glu_rows(gate, up):
    return jax.nn.gelu(gate) * up


def head_windows():
    windows = []
    for h in range(4):
        first, end = h * LHD, (h + 1) * LHD
        windows.append((first // 128 * 128, -(-end // 128) * 128, first, end))
    return windows


def lane_mask(shape, first, end):
    lane = lax.broadcasted_iota(jnp.int32, shape, 1)
    return (lane >= first) & (lane < end)


def join_heads(parts):
    lane = lax.broadcasted_iota(jnp.int32, (parts[0].shape[0], 128), 1)
    return jnp.concatenate(
        [
            jnp.where(lane < 96, parts[0], parts[1][:, :128]),
            jnp.where(lane < 64, parts[1][:, 128:], parts[2][:, :128]),
            jnp.where(lane < 32, parts[2][:, 128:], parts[3]),
        ],
        axis=1,
    )


def light_kernel(ends_ref, own_ref, edge_ref, out_ref):
    half = RADIUS
    factor = LHD ** (-0.5)
    for block in range(2):
        rows = slice(block * half, (block + 1) * half)
        row = lax.broadcasted_iota(jnp.int32, (half, 2 * half), 0)
        col = lax.broadcasted_iota(jnp.int32, (half, 2 * half), 1)
        keep_own = col <= row + half if block == 0 else col >= row
        row, col = row[:, :half], col[:, :half]
        keep_edge = (col >= row if block == 0 else col <= row) & (ends_ref[block] > 0)
        for group in range(2):
            mixed = []
            for a, b, first, end in head_windows():
                lanes = slice(group * 384 + a, group * 384 + b)
                keys = slice(D + lanes.start, D + lanes.stop)
                values = slice(2 * D + lanes.start, 2 * D + lanes.stop)
                query = own_ref[0, rows, lanes]
                query = jnp.where(
                    lane_mask(query.shape, first - a, end - a), query, jnp.zeros_like(query)
                )
                s_own = jnp.where(keep_own, mm_nt(query, own_ref[0, :, keys]), -1e30)
                s_edge = jnp.where(keep_edge, mm_nt(query, edge_ref[0, rows, lanes]), -1e30)
                top = jnp.maximum(
                    jnp.max(s_own, axis=1, keepdims=True), jnp.max(s_edge, axis=1, keepdims=True)
                )
                e_own = jnp.exp((s_own - top) * factor)
                e_edge = jnp.exp((s_edge - top) * factor)
                total = jnp.sum(e_own, axis=1, keepdims=True) + jnp.sum(
                    e_edge, axis=1, keepdims=True
                )
                mix = mm(e_own.astype(bf16), own_ref[0, :, values])
                mix += mm(
                    e_edge.astype(bf16), edge_ref[0, rows, slice(D + lanes.start, D + lanes.stop)]
                )
                mixed.append(mix * (1.0 / total))
            out_ref[0, rows, group * 384 : (group + 1) * 384] = join_heads(mixed).astype(bf16)


def light_attention(ends, own, edge):
    pieces, tokens = own.shape[:2]
    return pl.pallas_call(
        light_kernel,
        out_shape=jax.ShapeDtypeStruct((pieces, tokens, D), bf16),
        grid_spec=pltpu.PrefetchScalarGridSpec(
            num_scalar_prefetch=1,
            grid=(pieces,),
            in_specs=[
                pl.BlockSpec((1, tokens, 3 * D), lambda p, e: (p, 0, 0)),
                pl.BlockSpec((1, 2 * RADIUS, 2 * D), lambda p, e: (p, 0, 0)),
            ],
            out_specs=pl.BlockSpec((1, tokens, D), lambda p, e: (p, 0, 0)),
        ),
        compiler_params=pltpu.CompilerParams(vmem_limit_bytes=32 << 20),
        cost_estimate=pl.CostEstimate(
            flops=pieces * HL * tokens * 384 * 256 * 4,
            bytes_accessed=pieces * (tokens * 4 * D + 2 * RADIUS * 2 * D) * 2,
            transcendentals=pieces * HL * tokens * 384,
        ),
        name="light_attention",
    )(ends, own, edge)


def light_back_kernel(ends_ref, own_ref, edge_ref, grad_ref, own_out, edge_out):
    half = RADIUS
    factor = LHD ** (-0.5)
    for group in range(2):
        dk_own, dv_own = [None] * 4, [None] * 4
        for block in range(2):
            rows = slice(block * half, (block + 1) * half)
            key = lax.broadcasted_iota(jnp.int32, (2 * half, half), 0)
            que = lax.broadcasted_iota(jnp.int32, (2 * half, half), 1)
            keep_own = key <= que + half if block == 0 else key >= que
            key, que = key[:half], que[:half]
            keep_edge = (key >= que if block == 0 else key <= que) & (ends_ref[block] > 0)
            dq, dk_edge, dv_edge = [], [], []
            for h, (a, b, first, end) in enumerate(head_windows()):
                lanes = slice(group * 384 + a, group * 384 + b)
                after = slice(D + lanes.start, D + lanes.stop)
                last = slice(2 * D + lanes.start, 2 * D + lanes.stop)
                mask = lane_mask((half, b - a), first - a, end - a)
                query = own_ref[0, rows, lanes]
                query = jnp.where(mask, query, jnp.zeros_like(query))
                grad = grad_ref[0, rows, lanes]
                grad = jnp.where(mask, grad, jnp.zeros_like(grad))
                k_own, k_edge = own_ref[0, :, after], edge_ref[0, rows, lanes]
                v_own, v_edge = own_ref[0, :, last], edge_ref[0, rows, after]
                s_own = jnp.where(keep_own, mm_nt(k_own, query), -1e30)
                s_edge = jnp.where(keep_edge, mm_nt(k_edge, query), -1e30)
                top = jnp.maximum(
                    jnp.max(s_own, axis=0, keepdims=True), jnp.max(s_edge, axis=0, keepdims=True)
                )
                e_own = jnp.exp((s_own - top) * factor)
                e_edge = jnp.exp((s_edge - top) * factor)
                total = jnp.sum(e_own, axis=0, keepdims=True) + jnp.sum(
                    e_edge, axis=0, keepdims=True
                )
                scale = 1.0 / total
                p_own, p_edge = e_own * scale, e_edge * scale
                g_own, g_edge = mm_nt(v_own, grad), mm_nt(v_edge, grad)
                inner = jnp.sum(p_own * g_own, axis=0, keepdims=True) + jnp.sum(
                    p_edge * g_edge, axis=0, keepdims=True
                )
                d_own = (p_own * (g_own - inner)).astype(bf16)
                d_edge = (p_edge * (g_edge - inner)).astype(bf16)
                dv = mm(p_own.astype(bf16), grad)
                dk = mm(d_own, query)
                dv_own[h] = dv if block == 0 else dv_own[h] + dv
                dk_own[h] = dk if block == 0 else dk_own[h] + dk
                dv_edge.append(mm(p_edge.astype(bf16), grad))
                dk_edge.append(mm(d_edge, query) * factor)
                dq.append((mm_tn(d_own, k_own) + mm_tn(d_edge, k_edge)) * factor)
            at = slice(group * 384, (group + 1) * 384)
            at_v = slice(D + at.start, D + at.stop)
            own_out[0, rows, at] = join_heads(dq).astype(bf16)
            edge_out[0, rows, at] = join_heads(dk_edge).astype(bf16)
            edge_out[0, rows, at_v] = join_heads(dv_edge).astype(bf16)
        at_w = slice(2 * D + at.start, 2 * D + at.stop)
        own_out[0, :, at_v] = (join_heads(dk_own) * factor).astype(bf16)
        own_out[0, :, at_w] = join_heads(dv_own).astype(bf16)


def light_attention_back(ends, own, edge, grad):
    pieces, tokens = own.shape[:2]
    return pl.pallas_call(
        light_back_kernel,
        out_shape=[
            jax.ShapeDtypeStruct((pieces, tokens, 3 * D), bf16),
            jax.ShapeDtypeStruct((pieces, 2 * RADIUS, 2 * D), bf16),
        ],
        grid_spec=pltpu.PrefetchScalarGridSpec(
            num_scalar_prefetch=1,
            grid=(pieces,),
            in_specs=[
                pl.BlockSpec((1, tokens, 3 * D), lambda p, e: (p, 0, 0)),
                pl.BlockSpec((1, 2 * RADIUS, 2 * D), lambda p, e: (p, 0, 0)),
                pl.BlockSpec((1, tokens, D), lambda p, e: (p, 0, 0)),
            ],
            out_specs=[
                pl.BlockSpec((1, tokens, 3 * D), lambda p, e: (p, 0, 0)),
                pl.BlockSpec((1, 2 * RADIUS, 2 * D), lambda p, e: (p, 0, 0)),
            ],
        ),
        compiler_params=pltpu.CompilerParams(vmem_limit_bytes=32 << 20),
        cost_estimate=pl.CostEstimate(
            flops=pieces * HL * tokens * 384 * 256 * 10,
            bytes_accessed=pieces * (tokens * 7 * D + 2 * RADIUS * 4 * D) * 2,
            transcendentals=pieces * HL * tokens * 384,
        ),
        name="light_attention_back",
    )(ends, own, edge, grad)


def spread_heads(value):
    tall = jnp.concatenate([value] * 4, axis=0)
    row = lax.broadcasted_iota(jnp.int32, tall.shape, 0) // QCAP
    lane = lax.broadcasted_iota(jnp.int32, tall.shape, 1) // HHD
    return jnp.where(row == lane, tall, jnp.zeros_like(tall))


def fold_heads(tall):
    lane = lax.broadcasted_iota(jnp.int32, (QCAP, 4 * HHD), 1) // HHD
    total = tall[:QCAP]
    for r in range(1, 4):
        total = jnp.where(lane == r, tall[r * QCAP : (r + 1) * QCAP], total)
    return total


def heavy_kernel(query_ref, pair_ref, live_ref, out_ref):
    factor = HHD ** (-0.5)
    keep = live_ref[0] > 0
    for group in range(HH // 4):
        lanes = slice(group * 256, (group + 1) * 256)
        query = spread_heads(query_ref[0, :, lanes])
        scores = jnp.where(keep, mm_nt(query, pair_ref[0, :, lanes]), -1e30)
        top = jnp.max(scores, axis=1, keepdims=True)
        raised = jnp.exp((scores - top) * factor)
        total = jnp.sum(raised, axis=1, keepdims=True)
        mix = mm(raised.astype(bf16), pair_ref[0, :, D + lanes.start : D + lanes.stop])
        out_ref[0, :, lanes] = fold_heads(mix * (1.0 / total)).astype(bf16)


def heavy_attention(query, pairs, live):
    pieces, slots = pairs.shape[:2]
    return pl.pallas_call(
        heavy_kernel,
        out_shape=jax.ShapeDtypeStruct((pieces, QCAP, D), bf16),
        grid=(pieces,),
        in_specs=[
            pl.BlockSpec((1, QCAP, D), lambda p: (p, 0, 0)),
            pl.BlockSpec((1, slots, 2 * D), lambda p: (p, 0, 0)),
            pl.BlockSpec((1, 1, slots), lambda p: (p, 0, 0)),
        ],
        out_specs=pl.BlockSpec((1, QCAP, D), lambda p: (p, 0, 0)),
        compiler_params=pltpu.CompilerParams(vmem_limit_bytes=32 << 20),
        cost_estimate=pl.CostEstimate(
            flops=pieces * 3 * 4 * 256 * 256 * slots,
            bytes_accessed=pieces * (slots + QCAP) * 2 * D * 2,
            transcendentals=pieces * HH * QCAP * slots,
        ),
        name="heavy_attention",
    )(query, pairs, live)


def heavy_back_kernel(query_ref, pair_ref, live_ref, grad_ref, query_out, pair_out):
    factor = HHD ** (-0.5)
    keep = live_ref[0] > 0
    for group in range(HH // 4):
        lanes = slice(group * 256, (group + 1) * 256)
        after = slice(D + lanes.start, D + lanes.stop)
        query = spread_heads(query_ref[0, :, lanes])
        grad = spread_heads(grad_ref[0, :, lanes])
        keys = pair_ref[0, :, lanes]
        scores = jnp.where(keep, mm_nt(keys, query), -1e30)
        top = jnp.max(scores, axis=0, keepdims=True)
        raised = jnp.exp((scores - top) * factor)
        probs = raised * (1.0 / jnp.sum(raised, axis=0, keepdims=True))
        grad_probs = mm_nt(pair_ref[0, :, after], grad)
        inner = jnp.sum(probs * grad_probs, axis=0, keepdims=True)
        grad_scores = (probs * (grad_probs - inner)).astype(bf16)
        pair_out[0, :, after] = mm(probs.astype(bf16), grad).astype(bf16)
        pair_out[0, :, lanes] = (mm(grad_scores, query) * factor).astype(bf16)
        query_out[0, :, lanes] = (fold_heads(mm_tn(grad_scores, keys)) * factor).astype(bf16)


def heavy_attention_back(query, pairs, live, grad):
    pieces, slots = pairs.shape[:2]
    return pl.pallas_call(
        heavy_back_kernel,
        out_shape=[
            jax.ShapeDtypeStruct((pieces, QCAP, D), bf16),
            jax.ShapeDtypeStruct((pieces, slots, 2 * D), bf16),
        ],
        grid=(pieces,),
        in_specs=[
            pl.BlockSpec((1, QCAP, D), lambda p: (p, 0, 0)),
            pl.BlockSpec((1, slots, 2 * D), lambda p: (p, 0, 0)),
            pl.BlockSpec((1, slots, 1), lambda p: (p, 0, 0)),
            pl.BlockSpec((1, QCAP, D), lambda p: (p, 0, 0)),
        ],
        out_specs=[
            pl.BlockSpec((1, QCAP, D), lambda p: (p, 0, 0)),
            pl.BlockSpec((1, slots, 2 * D), lambda p: (p, 0, 0)),
        ],
        compiler_params=pltpu.CompilerParams(vmem_limit_bytes=32 << 20),
        cost_estimate=pl.CostEstimate(
            flops=pieces * 3 * 10 * 256 * 256 * slots,
            bytes_accessed=pieces * (2 * slots + 2 * QCAP) * 2 * D * 2,
            transcendentals=pieces * HH * QCAP * slots,
        ),
        name="heavy_attention_back",
    )(query, pairs, live, grad)


def reduce_kernel(jobs, sizes, *refs):
    n_x, n_y = sizes
    count = len(jobs)
    sources, outs, scratch = refs[:count], refs[count : 2 * count], refs[2 * count :]
    names = ("own", "core", "ax", "ay", "by", "bx", "zz", "lsem", "rsem", "ssem")
    held = [
        dict(zip(names, scratch[len(names) * a : len(names) * (a + 1)])) for a in range(count)
    ]
    dp, seq = lax.axis_index("dp"), lax.axis_index("seq")
    x, c = dp // CORES, dp % CORES
    z, y = seq // n_y, seq % n_y

    def to_core():
        return (x * CORES + (1 - c), seq)

    def to_x(by):
        return (((x + by) % n_x) * CORES + c, seq)

    def to_y(by):
        return (dp, z * n_y + (y + by) % n_y)

    def to_z(by):
        return (dp, ((z + by) % DEPTH) * n_y + y)

    peers = [to_core()]
    peers += [to_x(by) for by in range(1, n_x)]
    peers += [to_y(by) for by in range(1, n_y)]
    peers += [to_z(by) for by in range(1, DEPTH)]
    barrier = pltpu.get_barrier_semaphore()
    for peer in peers:
        pl.semaphore_signal(barrier, inc=1, device_id=peer, device_id_type=MESH)
    pl.semaphore_wait(barrier, len(peers))

    def send(src, dst, a, stage, k, peer):
        h = held[a]
        pltpu.make_async_remote_copy(
            src_ref=src,
            dst_ref=dst,
            send_sem=h["ssem"].at[stage],
            recv_sem=h["rsem"].at[stage, k],
            device_id=peer,
            device_id_type=MESH,
        ).start()

    def arrived(buffer, a, stage, k):
        h = held[a]
        pltpu.make_async_remote_copy(
            src_ref=buffer,
            dst_ref=buffer,
            send_sem=h["ssem"].at[stage],
            recv_sem=h["rsem"].at[stage, k],
            device_id=to_core(),
            device_id_type=MESH,
        ).wait_recv()

    def columns(a, k):
        width = jobs[a][0]
        return pl.ds(k * width, width)

    def local(a, k):
        h = held[a]
        return pltpu.make_async_copy(
            sources[a].at[:, c, :, :, :, columns(a, k)], h["own"].at[k], h["lsem"].at[k]
        )

    def stage_core_start(a, k):
        local(a, k).start()
        send(
            sources[a].at[:, 1 - c, :, :, :, columns(a, k)],
            held[a]["core"].at[k],
            a,
            0,
            k,
            to_core(),
        )

    def add_blocks(total, index_of, pieces):
        @pl.loop(0, total)
        def _(i):
            for target, addend in pieces:
                at = index_of(i)
                target[at] = target[at] + addend[at]

    def stage_core(a, k):
        h = held[a]
        local(a, k).wait()
        arrived(h["core"].at[k], a, 0, k)
        own, other = h["own"], h["core"]

        @pl.loop(0, n_x * DEPTH)
        def _(i):
            for j in range(n_y):
                at = (k, i // DEPTH, i % DEPTH, j)
                own[at] = own[at] + other[at]

        half = k // 2
        if k % 2 == 0:
            for by in range(1, n_x):
                send(own.at[k, (x + by) % n_x], h["ax"].at[half, by - 1], a, 1, k, to_x(by))
        else:
            for by in range(1, n_y):
                send(own.at[k, :, :, (y + by) % n_y], h["by"].at[half, by - 1], a, 2, k, to_y(by))

    def stage_second(a, k):
        h = held[a]
        own, half = h["own"], k // 2
        if k % 2 == 0:
            arrived(h["ax"].at[half], a, 1, k)

            @pl.loop(0, DEPTH)
            def _(i):
                for j in range(n_y):
                    for s in range(n_x - 1):
                        at = (k, x, i, j)
                        own[at] = own[at] + h["ax"][half, s, i, j]

            for by in range(1, n_y):
                send(
                    own.at[k, x, :, (y + by) % n_y], h["ay"].at[half, by - 1], a, 2, k, to_y(by)
                )
        else:
            arrived(h["by"].at[half], a, 2, k)

            @pl.loop(0, DEPTH)
            def _(i):
                for j in range(n_x):
                    for s in range(n_y - 1):
                        at = (k, j, i, y)
                        own[at] = own[at] + h["by"][half, s, j, i]

            for by in range(1, n_x):
                send(
                    own.at[k, (x + by) % n_x, :, y], h["bx"].at[half, by - 1], a, 1, k, to_x(by)
                )

    def stage_third(a, k):
        h = held[a]
        own, half = h["own"], k // 2
        name, stage, others = ("ay", 2, n_y - 1) if k % 2 == 0 else ("bx", 1, n_x - 1)
        arrived(h[name].at[half], a, stage, k)

        @pl.loop(0, DEPTH)
        def _(i):
            for s in range(others):
                at = (k, x, i, y)
                own[at] = own[at] + h[name][half, s, i]

        for by in range(1, DEPTH):
            send(own.at[k, x, (z + by) % DEPTH, y], h["zz"].at[k, by - 1], a, 3, k, to_z(by))

    def stage_last(a, k):
        h = held[a]
        width = jobs[a][0]
        arrived(h["zz"].at[k], a, 3, k)
        total = h["own"][k, x, z, y].astype(f32)
        for s in range(DEPTH - 1):
            total = total + h["zz"][k, s].astype(f32)
        outs[a][:, k * width : (k + 1) * width] = total

    order = [(a, k) for a in range(count) for k in range(jobs[a][1])]
    for a, k in order:
        stage_core_start(a, k)
    lags = [(stage_core, 0), (stage_second, 4), (stage_third, 8), (stage_last, 12)]
    for step in range(len(order) + lags[-1][1]):
        for stage, lag in lags:
            if 0 <= step - lag < len(order):
                stage(*order[step - lag])

    for a in range(count):
        h = held[a]

        def sent(buffer, stage):
            pltpu.make_async_remote_copy(
                src_ref=buffer,
                dst_ref=buffer,
                send_sem=h["ssem"].at[stage],
                recv_sem=h["rsem"].at[stage, 0],
                device_id=to_core(),
                device_id_type=MESH,
            ).wait_send()

        sent(h["core"], 0)
        sent(h["ax"], 1)
        sent(h["bx"], 1)
        sent(h["by"], 2)
        sent(h["ay"], 2)
        sent(h["zz"], 3)


def reduce_all(values, widths, n_x, n_y, collective_id):
    jobs, operands, out_shape, scratch = [], [], [], []
    devices = n_x * CORES * DEPTH * n_y
    for value, width in zip(values, widths):
        height, columns = value.shape
        chunk = height // devices
        k = columns // width
        jobs.append((width, k))
        operands.append(value.reshape(n_x, CORES, DEPTH, n_y, chunk, columns))
        out_shape.append(jax.ShapeDtypeStruct((chunk, columns), f32))
        tile = (chunk, width)
        scratch += [
            pltpu.VMEM((k, n_x, DEPTH, n_y) + tile, bf16),
            pltpu.VMEM((k, n_x, DEPTH, n_y) + tile, bf16),
            pltpu.VMEM((k // 2, n_x - 1, DEPTH, n_y) + tile, bf16),
            pltpu.VMEM((k // 2, n_y - 1, DEPTH) + tile, bf16),
            pltpu.VMEM((k // 2, n_y - 1, n_x, DEPTH) + tile, bf16),
            pltpu.VMEM((k // 2, n_x - 1, DEPTH) + tile, bf16),
            pltpu.VMEM((k, DEPTH - 1) + tile, bf16),
            pltpu.SemaphoreType.DMA((k,)),
            pltpu.SemaphoreType.DMA((4, k)),
            pltpu.SemaphoreType.DMA((4,)),
        ]
    total = sum(v.size for v in values)
    return pl.pallas_call(
        functools.partial(reduce_kernel, tuple(jobs), (n_x, n_y)),
        out_shape=out_shape,
        in_specs=[pl.BlockSpec(memory_space=pl.ANY)] * len(values),
        out_specs=[pl.BlockSpec(memory_space=pltpu.VMEM)] * len(values),
        scratch_shapes=scratch,
        compiler_params=pltpu.CompilerParams(
            collective_id=collective_id, has_side_effects=True, vmem_limit_bytes=60 << 20
        ),
        cost_estimate=pl.CostEstimate(flops=2 * total, bytes_accessed=4 * total, transcendentals=0),
        name="reduce_gradients",
    )(*operands)


def per_device(
    layer_input,
    cotangent,
    first_gain,
    light_inputs,
    light_output,
    heavy_queries,
    heavy_keyvalue,
    heavy_output,
    second_gain,
    router,
    light_gates,
    light_down,
    heavy_gates,
    heavy_down,
    query_index,
    query_count,
    key_index,
    key_count,
    feed_slot,
):
    pieces, tokens = layer_input.shape[:2]
    rows = pieces * tokens
    n_dp, n_seq = lax.axis_size("dp"), lax.axis_size("seq")
    n_x, n_y = n_dp // CORES, n_seq // DEPTH
    seq_rank = lax.axis_index("seq")
    core = Ring("dp", 1, CORES)
    ring_x = Ring("dp", CORES, n_x)
    ring_y = Ring("seq", 1, n_y)
    ring_z = Ring("seq", n_y, DEPTH)
    capacity = max(2, 3 * rows // (16 * n_seq))
    slots = n_seq * capacity
    light_factor = LHD ** (-0.5)
    heavy_factor = HHD ** (-0.5)

    def reduce_grad(value, first, second):
        height, width = value.shape
        chunk = height // (n_dp * n_seq)
        parts = value.reshape(n_x, CORES, DEPTH, n_y, chunk, width)
        parts = core.scatter_sum(parts, 1).astype(bf16)
        dims = ["x", "z", "y"]
        rings = {"x": ring_x, "y": ring_y, "z": ring_z}
        order = [first, second, [d for d in dims if d not in (first, second)][0]]
        for i, d in enumerate(order):
            at = dims.index(d)
            parts = rings[d].scatter_sum(parts, at)
            if i < 2:
                parts = parts.astype(bf16)
            dims.remove(d)
        return parts

    def reduce_split(value):
        half = value.shape[1] // 2
        return jnp.concatenate(
            [
                reduce_grad(value[:, :half], "x", "y"),
                reduce_grad(value[:, half:], "y", "x"),
            ],
            axis=1,
        )

    def reduce_vectors(value):
        count, width = value.shape
        chunk = width // (n_dp * n_seq)
        parts = value.reshape(count, n_x, CORES, DEPTH, n_y, chunk)
        parts = core.scatter_sum(parts, 2)
        parts = ring_x.scatter_sum(parts, 1)
        parts = ring_z.scatter_sum(parts, 1)
        return ring_y.scatter_sum(parts, 1)

    ends = n_seq - 1
    left_rows = lax.ppermute(
        layer_input[:, tokens - RADIUS :], "seq", [(i, i + 1) for i in range(ends)]
    )
    right_rows = lax.ppermute(layer_input[:, :RADIUS], "seq", [(i + 1, i) for i in range(ends)])
    position = jnp.arange(tokens, dtype=jnp.int32)
    key_pick = (key_index[:, :, None] == position[None, None, :]).astype(bf16)
    query_live = jnp.arange(QCAP, dtype=jnp.int32)[None, :] < query_count
    query_pick = (query_index[:, :, None] == position[None, None, :]).astype(bf16)
    live_pick = query_pick * query_live[:, :, None].astype(bf16)
    key_raw = jnp.einsum("pkt,ptd->pkd", key_pick, layer_input, preferred_element_type=f32).astype(
        bf16
    )
    key_all = ring_y.gather(ring_z.gather(key_raw))

    gain_first = first_gain.astype(f32)
    inputs = layer_input.astype(f32)
    unit_first, scale_first = norm_parts(inputs)
    normed_first = (unit_first * gain_first).astype(bf16)
    normed_flat = normed_first.reshape(rows, D)
    own_proj = mm(normed_flat, light_inputs).astype(bf16).reshape(pieces, tokens, 3 * D)
    edge_rows = jnp.concatenate([left_rows, right_rows], axis=1)
    normed_edge = (norm_parts(edge_rows.astype(f32))[0] * gain_first).astype(bf16)
    edge_flat = normed_edge.reshape(pieces * 2 * RADIUS, D)
    edge_proj = mm(edge_flat, light_inputs[:, D:]).astype(bf16)
    edge_proj = edge_proj.reshape(pieces, 2 * RADIUS, 2 * D)

    reach = jnp.stack([seq_rank > 0, seq_rank < n_seq - 1]).astype(jnp.int32)
    light_att = light_attention(reach, own_proj, edge_proj).reshape(rows, D)

    key_slots = n_seq * KCAP
    key_rows_all = key_all.transpose(2, 0, 1, 3, 4).reshape(pieces * key_slots, D)
    normed_keys = (norm_parts(key_rows_all.astype(f32))[0] * gain_first).astype(bf16)
    heavy_pairs = mm(normed_keys, heavy_keyvalue).astype(bf16).reshape(pieces, key_slots, 2 * D)
    from_z = (ring_z.place - jnp.arange(DEPTH, dtype=jnp.int32)) % DEPTH
    from_y = (ring_y.place - jnp.arange(n_y, dtype=jnp.int32)) % n_y
    sources = (from_z[None, :] * n_y + from_y[:, None]).reshape(-1)
    counts_here = jnp.sum(
        jnp.where(
            sources[None, :, None] == jnp.arange(n_seq, dtype=jnp.int32)[None, None, :],
            key_count[:, None, :],
            0,
        ),
        axis=-1,
    )
    key_live = jnp.arange(KCAP, dtype=jnp.int32)[None, None, :] < counts_here[:, :, None]
    key_live = key_live.reshape(pieces, 1, key_slots).astype(f32)
    query_rows = (
        jnp.einsum("pqt,ptd->pqd", query_pick, normed_first, preferred_element_type=f32)
        .astype(bf16)
        .reshape(pieces * QCAP, D)
    )
    heavy_query = mm(query_rows, heavy_queries).astype(bf16).reshape(pieces, QCAP, D)
    heavy_att = heavy_attention(heavy_query, heavy_pairs, key_live)
    heavy_spread = (
        jnp.einsum("pqt,pqd->ptd", live_pick, heavy_att, preferred_element_type=f32)
        .astype(bf16)
        .reshape(rows, D)
    )

    middle = (
        inputs.reshape(rows, D) + mm(light_att, light_output) + mm(heavy_spread, heavy_output)
    )
    gain_second = second_gain.astype(f32)
    unit_second, scale_second = norm_parts(middle)
    normed_second = (unit_second * gain_second).astype(bf16)

    slot_of = feed_slot.reshape(1, rows)
    pick = (jnp.arange(slots, dtype=jnp.int32)[:, None] == slot_of).astype(bf16)
    routed = feed_slot.reshape(rows, 1) >= 0
    cot = cotangent.reshape(rows, D)
    gating = jax.nn.sigmoid(
        jnp.sum(normed_second.astype(f32) * router.astype(f32), axis=-1, keepdims=True)
    )
    grad_token = (gating * cot.astype(f32)).astype(bf16)
    feed_in = mm(pick, normed_second).astype(bf16)
    grad_in = mm(pick, grad_token).astype(bf16)

    hidden = light_gates.shape[1] // 2
    light_gate = mm(normed_second, light_gates[:, :hidden])
    light_up = mm(normed_second, light_gates[:, hidden:])
    light_act, light_pull = jax.vjp(glu_rows, light_gate, light_up)
    light_act = light_act.astype(bf16)
    light_feed = mm(light_act, light_down)
    grad_light_gate, grad_light_up = light_pull(mm_nt(cot, light_down))
    grad_light_pre = jnp.concatenate([grad_light_gate.astype(bf16), grad_light_up.astype(bf16)], 1)

    wide_hidden = heavy_gates.shape[1] // 2
    heavy_gate = mm(feed_in, heavy_gates[:, :wide_hidden])
    heavy_up = mm(feed_in, heavy_gates[:, wide_hidden:])
    heavy_act, heavy_pull = jax.vjp(glu_rows, heavy_gate, heavy_up)
    heavy_act = heavy_act.astype(bf16)
    heavy_result = mm(heavy_act, heavy_down).astype(bf16)
    grad_heavy_gate, grad_heavy_up = heavy_pull(mm_nt(grad_in, heavy_down))
    grad_heavy_pre = jnp.concatenate([grad_heavy_gate.astype(bf16), grad_heavy_up.astype(bf16)], 1)
    grad_feed_in = mm_nt(grad_heavy_pre, heavy_gates).astype(bf16)
    heavy_down_grad = mm_tn(heavy_act, grad_in).astype(bf16)
    heavy_gates_grad = mm_tn(feed_in, grad_heavy_pre).astype(bf16)
    light_down_grad = mm_tn(light_act, cot).astype(bf16)
    light_gates_grad = mm_tn(normed_second, grad_light_pre).astype(bf16)

    token_result = mm_tn(pick, heavy_result)
    output = (middle + light_feed + gating * token_result).astype(bf16).reshape(layer_input.shape)
    grad_gating = jnp.sum(cot.astype(f32) * token_result, axis=-1, keepdims=True)
    grad_logit = grad_gating * gating * (1.0 - gating)
    grad_second = (
        mm_nt(grad_light_pre, light_gates)
        + mm_tn(pick, grad_feed_in)
        + grad_logit * router.astype(f32)
    )
    router_grad = jnp.sum(grad_logit * normed_second.astype(f32), axis=0)
    second_gain_grad = jnp.sum(grad_second * unit_second, axis=0)
    grad_middle = cot.astype(f32) + norm_pull(grad_second, middle, scale_second, gain_second)
    grad_mid_low = grad_middle.astype(bf16)

    light_output_grad = mm_tn(light_att, grad_mid_low).astype(bf16)
    grad_light_att = mm_nt(grad_mid_low, light_output).astype(bf16)
    grad_query_rows = (
        jnp.einsum(
            "pqt,ptd->pqd",
            live_pick,
            grad_mid_low.reshape(pieces, tokens, D),
            preferred_element_type=f32,
        )
        .astype(bf16)
        .reshape(pieces * QCAP, D)
    )
    heavy_output_grad = mm_tn(heavy_att.reshape(pieces * QCAP, D), grad_query_rows).astype(bf16)
    grad_heavy_att = mm_nt(grad_query_rows, heavy_output).astype(bf16)

    grad_hq_low, grad_hkv_low = heavy_attention_back(
        heavy_query,
        heavy_pairs,
        key_live.reshape(pieces, key_slots, 1),
        grad_heavy_att.reshape(pieces, QCAP, D),
    )
    grad_hq_low = grad_hq_low.reshape(pieces * QCAP, D)
    grad_hkv_low = grad_hkv_low.reshape(pieces * key_slots, 2 * D)
    grad_key_rows = mm_nt(grad_hkv_low, heavy_keyvalue).astype(bf16)
    grad_key_rows = grad_key_rows.reshape(pieces, n_y, DEPTH, KCAP, D).transpose(1, 2, 0, 3, 4)
    grad_key_own = ring_z.return_sum(ring_y.return_sum(grad_key_rows).astype(bf16))
    heavy_keyvalue_grad = mm_tn(normed_keys, grad_hkv_low).astype(bf16)
    heavy_queries_grad = mm_tn(query_rows, grad_hq_low).astype(bf16)

    grad_own, grad_edge = light_attention_back(
        reach, own_proj, edge_proj, grad_light_att.reshape(pieces, tokens, D)
    )
    grad_own = grad_own.reshape(rows, 3 * D)
    grad_edge = grad_edge.reshape(pieces * 2 * RADIUS, 2 * D)
    grad_edge_rows = mm_nt(grad_edge, light_inputs[:, D:]).astype(bf16)
    grad_edge_rows = grad_edge_rows.reshape(pieces, 2 * RADIUS, D)
    from_right = lax.ppermute(
        grad_edge_rows[:, :RADIUS], "seq", [(i + 1, i) for i in range(ends)]
    )
    from_left = lax.ppermute(
        grad_edge_rows[:, RADIUS:], "seq", [(i, i + 1) for i in range(ends)]
    )
    light_inputs_grad = jnp.concatenate(
        [
            mm_tn(normed_flat, grad_own[:, :D]),
            mm_tn(normed_flat, grad_own[:, D:]) + mm_tn(edge_flat, grad_edge),
        ],
        axis=1,
    ).astype(bf16)

    grad_hq_rows = mm_nt(grad_hq_low, heavy_queries).astype(bf16).reshape(pieces, QCAP, D)
    grad_first = mm_nt(grad_own, light_inputs).reshape(pieces, tokens, D)
    grad_first = (
        grad_first
        + jnp.einsum("pqt,pqd->ptd", query_pick, grad_hq_rows, preferred_element_type=f32)
        + jnp.einsum("pkt,pkd->ptd", key_pick, grad_key_own.astype(bf16), preferred_element_type=f32)
        + jnp.concatenate([from_left, from_right], axis=1).astype(f32)
    )
    first_gain_grad = jnp.sum(grad_first * unit_first, axis=(0, 1))
    input_grad = grad_middle.reshape(pieces, tokens, D) + norm_pull(
        grad_first, inputs, scale_first, gain_first
    )
    vectors = jnp.stack([first_gain_grad, second_gain_grad, router_grad])
    devices = n_dp * n_seq
    feed_grads = [heavy_gates_grad, heavy_down_grad, light_gates_grad, light_down_grad]
    late_grads = [
        light_inputs_grad,
        light_output_grad,
        heavy_queries_grad,
        heavy_keyvalue_grad,
        heavy_output_grad,
    ]
    if D // devices % 8 == 0:
        each = D // devices
        lines = vectors.reshape(3, devices, each).transpose(1, 0, 2)
        lines = jnp.pad(lines, ((0, 0), (0, 5), (0, 256 - each))).reshape(devices * 8, 256)
        feed_grads = reduce_all(feed_grads, (512, 128, 512, 384), n_x, n_y, 0)
        *late_grads, lines = reduce_all(
            late_grads + [lines.astype(bf16)], (384,) * 5 + (128,), n_x, n_y, 1
        )
        vectors = lines[:3, :each]
    else:
        feed_grads = [reduce_split(v) for v in feed_grads]
        late_grads = [reduce_split(v) for v in late_grads]
        vectors = reduce_vectors(vectors)
    return (
        output,
        input_grad,
        vectors[0],
        *late_grads,
        vectors[1],
        vectors[2],
        feed_grads[2],
        feed_grads[3],
        feed_grads[0],
        feed_grads[1],
    )


def solution(mesh):
    rows = P(("dp", "seq"), None)
    line = P(("dp", "seq"))
    tokens = P("dp", "seq", None)
    slots = P("dp", "seq")
    return jax.shard_map(
        per_device,
        mesh=mesh,
        in_specs=(tokens, tokens) + (P(),) * 12 + (slots, slots, slots, P("dp", None), slots),
        out_specs=(tokens, tokens, line) + (rows,) * 5 + (line, line) + (rows,) * 4,
        check_vma=False,
    )
```

time: 1750 us -> 530 us (0.30)
  waiting for transfers between devices: 1120 us -> 49.5 us
  Pallas kernels: 0 us -> 221 us
  other arithmetic: 157 us -> 30.6 us
  local copies, waits for them, and re-layouts: 123 us -> 35.9 us
  matrix products: 231 us -> 149 us
  blocking collectives: 61.1 us -> 0 us
    reduce_scatter x10 -> x0, waiting for transfers between devices: 993 us -> none  [the longest x1 253 us: per_device(): lax.psum_scatter(heavy_gates_grad, ('dp', 'seq'), scatter_dimension=0, ti...]
    pallas_call x0 -> x6, Pallas kernels: none -> 221 us  [the longest x2 165 us: reduce_all(): pl.pallas_call(functools.partial(reduce_kernel, tuple(jobs), (n_x, n_y)),...]
    scatter-add x6 -> x0, other arithmetic: 86.1 us -> none  [the longest x4 83.4 us: put_rows(): matrix.at[indices].add(extra)]
    dot_general x44 -> x42, matrix products: 231 us -> 149 us  [the longest x36 135 us: dot(): lax.dot_general(left, right, (over, ((), ())), preferred_element_type=f32)]
    ppermute x4 -> x12, waiting for transfers between devices: 122 us -> 49.5 us  [the longest x8 49.5 us: shift(): return lax.ppermute(value, self.axis, pairs)]
    unnamed x1 -> x0, blocking collectives: 44 us -> none
    slice x8 -> x2, local copies, waits for them, and re-layouts: 31.7 us -> 3.86 us  [the longest x1 2.61 us: per_device(): layer_input[:, tokens - RADIUS:]]
    ppermute x4 -> x12, starting transfers between devices: 13.2 us -> 39 us  [the longest x8 27.7 us: shift(): return lax.ppermute(value, self.axis, pairs)]
  transfers between devices with their start and end apart: 18 -> 12, of which waited for: 12 -> 2; matrix products, arithmetic and copies ran while one was open for 17% -> 13% of each run, Pallas kernels for 0% -> 24%
where the time goes in v1:
time: 530 us; the launch traced here: 527 us
  Pallas kernels  221 us (42%)
  matrix products  149 us (28%)
  waiting for transfers between devices  49.5 us (9%)
  starting transfers between devices  39 us (7%)
  local copies, waits for them, and re-layouts  35.9 us (7%)
  other arithmetic  30.6 us (6%)
    pallas_call x2, Pallas kernels, reduce_all(): pl.pallas_call(functools.partial(reduce_kernel, tuple(jobs), (n_x, n_y)),...  165 us
    dot_general x36, matrix products, dot(): lax.dot_general(left, right, (over, ((), ())), preferred_element_type=f32)  135 us
    ppermute x8, waiting for transfers between devices, shift(): return lax.ppermute(value, self.axis, pairs)  49.5 us
    ppermute x8, starting transfers between devices, shift(): return lax.ppermute(value, self.axis, pairs)  27.7 us
    pallas_call x1, Pallas kernels, light_attention_back(): pl.pallas_call(light_back_kernel, out_shape=[jax.ShapeDtypeStruct((pieces...  27.5 us
    unnamed x178, local copies, waits for them, and re-layouts  17.9 us
    pallas_call x1, Pallas kernels, light_attention(): pl.pallas_call(light_kernel, out_shape=jax.ShapeDtypeStruct((pieces, toke...  15.6 us
  transfers between devices with their start and end apart: 12, of which 2 were waited for; matrix products, arithmetic and copies ran while one was open for 13% of the time, Pallas kernels for 24%

profile of v1, /device:TPU:0, one launch (start us, length us, event | category | flops | bytes accessed | tf_op | source)
XLA Modules:
  0.0 526.9 jit_solution(17218832211960406723)
XLA Ops:
  0.7 2.8 convolution_convert_fusion.15
  3.4 5.1 collective-permute-start.4
  9.6 2.6 fusion.97
  12.2 3.5 collective-permute-start
  23.9 2.3 compare_convert_fusion.live_ref
  28.9 2.7 copy.65
  33.7 6.5 %convolution_convert_fusion.3 = bf16[1024,2304]{1,0:T(8,128)(2,1)S(1)} fusion(bf16[1024,768]{1,0:T(8,128)(2,1)} %bitcast.210, bf16[768,2304]{1,0:T(8,128)(2,1)} %param.22), kind=kOutput, calls=%fused_computation.15 | convolution fusion | flops 3626237952 | bytes 9830400 | tf_op jit(solution)/shard_map/dot_general | solution.py:25
  40.9 3.9 fusion.99
  46.4 3.1 collective-permute-start.5
  55.3 2.8 convolution_convert_fusion.4
  58.2 15.6 %light_attention.1 = bf16[4,256,768]{2,1,0:T(8,128)(2,1)S(1)} custom-call(s32[2]{0:T(128)S(1)} %add_convert_fusion.1.ends_ref, bf16[4,256,2304]{2,1,0:T(8,128)(2,1)S(1)} %bitcast.197, bf16[4,256,1536]{2,1,0:T(8,128)(2,1)S(1)} %bitcast.201), custom_call_target="tpu_custom_call" | custom-call | flops 3221225472 | bytes 9437184 | tf_op jit(solution)/shard_map/light_attention/pallas_call | solution.py:153
  73.8 3.1 fusion.98
  76.9 9.3 %collective-permute-done.5 = bf16[4,4,64,768]{3,2,1,0:T(8,128)(2,1)S(1)} collective-permute-done((bf16[4,4,64,768]{3,2,1,0:T(8,128)(2,1)S(1)}, bf16[4,4,64,768]{3,2,1,0:T(8,128)(2,1)S(1)}, u32[]{:S(2)}, u32[]{:S(2)}) %collective-permute-start.5) | collective-permute-done | bytes 1572896 | tf_op jit(solution)/shard_map/ppermute | solution.py:51
  86.9 2.5 multiply_convert_fusion
  89.4 3.0 convert_bitcast_fusion
  92.5 3.2 copy.60
  96.3 5.2 convolution_convert_fusion.1
  101.6 3.9 heavy_attention.1
  113.4 6.2 %fusion.13 = (bf16[1024,1024]{0,1:T(8,128)(2,1)S(1)}, bf16[1024,1024]{0,1:T(8,128)(2,1)S(1)}, bf16[1024,1024]{0,1:T(8,128)(2,1)}) fusion(f32[1024,1024]{0,1:T(8,128)S(1)} %copy-done.71, f32[1024,1024]{0,1:T(8,128)S(1)} %fusion.46, bf16[1024,768]{1,0:T(8,128)(2,1)S(1)} %get-tuple-element.49, bf16[768,2048]{1,0:T(8,128)(2,1)S(1)} %copy-done.65), kind=kOutput, calls=%fused_computation.29 | convolution fusion | flops 1637875712 | bytes 17825792 | tf_op jit(solution)/shard_map/dot_general | solution.py:25
  121.0 6.8 %convolution_convert_fusion.5 = bf16[768,2048]{1,0:T(8,128)(2,1)} fusion(bf16[1024,768]{1,0:T(8,128)(2,1)S(1)} %get-tuple-element.49, bf16[1024,1024]{0,1:T(8,128)(2,1)S(1)} %get-tuple-element.51, bf16[1024,1024]{0,1:T(8,128)(2,1)S(1)} %get-tuple-element.50), kind=kOutput, calls=%fused_computation.40 | convolution fusion | flops 3231186944 | bytes 8912896 | tf_op jit(solution)/shard_map/dot_general | solution.py:25
  127.8 6.9 %fusion.33 = f32[1024,768]{1,0:T(8,128)} fusion(bf16[768,2048]{1,0:T(8,128)(2,1)S(1)} %copy-done.65, bf16[1024,1024]{0,1:T(8,128)(2,1)} %copy-done.73, bf16[1024,1024]{0,1:T(8,128)(2,1)S(1)} %get-tuple-element.50), kind=kOutput, calls=%fused_computation.84 | convolution fusion | flops 3229614080 | bytes 10485760 | tf_op jit(solution)/shard_map/dot_general | solution.py:25
  139.8 4.9 fusion.24
  144.7 9.6 %fusion.56 = bf16[192,768]{1,0:T(8,128)(2,1)} fusion(bf16[768,8192]{1,0:T(8,128)(2,1)} %param.31, bf16[192,4096]{1,0:T(8,128)(2,1)S(1)} %get-tuple-element.54, bf16[192,4096]{1,0:T(8,128)(2,1)S(1)} %get-tuple-element.53), kind=kOutput, calls=%fused_computation.121 | convolution fusion | flops 2422358016 | bytes 16023552 | tf_op jit(solution)/shard_map/dot_general | solution.py:25
  154.3 6.9 %convolution_convert_fusion = bf16[768,8192]{1,0:T(8,128)(2,1)} fusion(bf16[192,768]{1,0:T(8,128)(2,1)S(1)} %convolution_convert_fusion.19, bf16[192,4096]{1,0:T(8,128)(2,1)S(1)} %get-tuple-element.54, bf16[192,4096]{1,0:T(8,128)(2,1)S(1)} %get-tuple-element.53), kind=kOutput, calls=%fused_computation | convolution fusion | flops 2428502016 | bytes 16023552 | tf_op jit(solution)/shard_map/dot_general | solution.py:25
  163.2 7.5 %fusion.26 = (f32[1024]{0:T(1024)S(1)}, f32[1024,768]{1,0:T(8,128)}) fusion(bf16[4,256,768]{2,1,0:T(8,128)(2,1)} %param.20, bf16[192,4096]{1,0:T(8,128)(2,1)} %get-tuple-element.55, bf16[4096,768]{1,0:T(8,128)(2,1)} %param.32, s32[1024]{0:T(1024)S(1)} %bitcast.242), kind=kOutput, calls=%fused_computation.53 | convolution fusion | flops 1512651776 | bytes 12591104 | tf_op jit(solution)/shard_map/dot_general | solution.py:25
  170.8 5.2 convolution_convert_fusion.9
  176.0 3.1 add_convert_fusion
  180.7 2.4 fusion.95
  187.0 8.8 %heavy_attention_back.1 = (bf16[4,64,768]{2,1,0:T(8,128)(2,1)S(1)}, bf16[4,512,1536]{2,1,0:T(8,128)(2,1)S(1)}) custom-call(bf16[4,64,768]{2,1,0:T(8,128)(2,1)S(1)} %bitcast.192, bf16[4,512,1536]{2,1,0:T(8,128)(2,1)S(1)} %bitcast.188, f32[4,512,1]{2,1,0:T(8,128)S(1)} %copy-done.2, bf16[4,64,768]{2,1,0:T(8,128)(2,1)S(1)} %bitcast.194), custom_call_target="tpu_custom_call" | custom-call | flops 4026531840 | bytes 14155776 | tf_op jit(solution)/shard_map/heavy_attention_back/pallas_call | solution.py:339
  195.9 5.3 %convolution_convert_fusion.7 = bf16[2048,768]{1,0:T(8,128)(2,1)S(1)} fusion(bf16[2048,1536]{1,0:T(8,128)(2,1)S(1)} %bitcast.195, bf16[768,1536]{1,0:T(8,128)(2,1)S(1)} %copy-done), kind=kOutput, calls=%fused_computation.42 | convolution fusion | flops 4833411072 | bytes 11796480 | tf_op jit(solution)/shard_map/dot_general | solution.py:25
  205.8 27.5 %light_attention_back.1 = (bf16[4,256,2304]{2,1,0:T(8,128)(2,1)S(1)}, bf16[4,256,1536]{2,1,0:T(8,128)(2,1)S(1)}) custom-call(s32[2]{0:T(128)S(1)} %add_convert_fusion.1.ends_ref, bf16[4,256,2304]{2,1,0:T(8,128)(2,1)S(1)} %bitcast.200, bf16[4,256,1536]{2,1,0:T(8,128)(2,1)S(1)} %bitcast.202, bf16[4,256,768]{2,1,0:T(8,128)(2,1)S(1)} %bitcast.206), custom_call_target="tpu_custom_call" | custom-call | flops 8053063680 | bytes 17301504 | tf_op jit(solution)/shard_map/light_attention_back/pallas_call | solution.py:236
  233.3 7.7 %fusion.14 = f32[4,256,768]{2,1,0:T(8,128)} fusion(bf16[4,256,2304]{2,1,0:T(8,128)(2,1)S(1)} %get-tuple-element.28, bf16[768,2304]{1,0:T(8,128)(2,1)} %param.22), kind=kOutput, calls=%fused_computation.38 | convolution fusion | flops 3623878656 | bytes 11403264 | tf_op jit(solution)/shard_map/dot_general | solution.py:25
  241.0 2.7 fusion.27
  245.7 2.6 fusion.38
  249.6 5.3 %collective-permute-start.10 = (bf16[4,128,768]{2,1,0:T(8,128)(2,1)}, bf16[4,128,768]{2,1,0:T(8,128)(2,1)}, u32[]{:S(2)}, u32[]{:S(2)}) collective-permute-start(bf16[4,128,768]{2,1,0:T(8,128)(2,1)} %get-tuple-element.59), channel_id=1, source_target_pairs={{0,1},{1,2},{2,3},{3,4},{4,5},{5,6},{6,7},{8,9},{9,10},{10,11},{11... | collective-permute-start | bytes 2359304 | tf_op jit(solution)/shard_map/ppermute | solution.py:817
  256.1 5.1 collective-permute-start.6
  261.2 2.3 fusion.68
  263.5 4.8 fusion.6
  270.4 4.4 convolution_convert_fusion.2
  274.9 6.6 %convolution_convert_fusion.6 = bf16[768,1536]{1,0:T(8,128)(2,1)} fusion(bf16[2048,768]{1,0:T(8,128)(2,1)S(1)} %bitcast.225, bf16[2048,1536]{1,0:T(8,128)(2,1)S(1)} %bitcast.196), kind=kOutput, calls=%fused_computation.41 | convolution fusion | flops 4833017856 | bytes 11796480 | tf_op jit(solution)/shard_map/dot_general | solution.py:25
  281.5 40.2 %collective-permute-done.6 = bf16[4,4,64,768]{3,2,1,0:T(8,128)(2,1)S(1)} collective-permute-done((bf16[4,4,64,768]{3,2,1,0:T(8,128)(2,1)S(1)}, bf16[4,4,64,768]{3,2,1,0:T(8,128)(2,1)S(1)}, u32[]{:S(2)}, u32[]{:S(2)}) %collective-permute-start.6) | collective-permute-done | bytes 1572896 | tf_op jit(solution)/shard_map/ppermute | solution.py:51
  324.3 5.1 collective-permute-start.7
  331.5 6.2 %collective-permute-start.8 = (bf16[4,64,768]{2,1,0:T(8,128)(2,1)}, bf16[4,64,768]{2,1,0:T(8,128)(2,1)}, u32[]{:S(2)}, u32[]{:S(2)}) collective-permute-start(bf16[4,64,768]{2,1,0:T(8,128)(2,1)} %get-tuple-element.58), channel_id=1, source_target_pairs={{0,4},{1,5},{2,6},{3,7},{4,0},{5,1},{6,2},{7,3},{8,12},{9,13},{10,... | collective-permute-start | bytes 1179656 | tf_op jit(solution)/shard_map/ppermute | solution.py:51
  338.4 111.9 %reduce_gradients.3 = (f32[24,8192]{1,0:T(8,128)}, f32[128,768]{1,0:T(8,128)}, f32[24,2048]{1,0:T(8,128)}, f32[32,768]{1,0:T(8,128)}) custom-call(bf16[2,2,4,2,24,8192]{5,4,3,2,1,0:T(8,128)(2,1)} %bitcast.207, bf16[2,2,4,2,128,768]{5,4,3,2,1,0:T(8,128)(2,1)} %bitcast.208, bf16[2,2,4,2,24,2048]{5,4,3,2,1,0:T(8,128)(2,1)} %bitcast.227, ...), custom_call_target="tpu_custom_call" | custom-call | flops 23592960 | bytes 47185920 | tf_op jit(solution)/shard_map/reduce_gradients/pallas_call | solution.py:579
  450.3 4.0 convolution_convert_fusion.11
  454.4 6.3 %multiply_reduce_fusion.2 = (bf16[768]{0:T(1024)(128)(2,1)S(1)}, f32[4,256]{1,0:T(4,128)S(1)}, f32[4,256,768]{2,1,0:T(8,128)}) fusion(bf16[4,256,768]{2,1,0:T(8,128)(2,1)S(1)} %copy-done.10, f32[4,256]{1,0:T(4,128)S(1)} %copy-done.49, f32[768]{0:T(1024)S(1)} %convert_element_type.230, bf16[4,128,768]{2,1,0:T(8,128)(2,1)} %collective-permute-done.11, ...), kind=kOutput, calls=%fused_computation.67 | convolution fusion | flops 113309952 | bytes 14169600 | tf_op jit(solution)/shard_map/pkt,pkd->ptd/dot_general | solution.py:833
  461.5 52.9 %reduce_gradients.2 = (f32[24,2304]{1,0:T(8,128)}, f32[24,768]{1,0:T(8,128)}, f32[24,768]{1,0:T(8,128)}, f32[24,1536]{1,0:T(8,128)}, f32[24,768]{1,0:T(8,128)}, /*index=5*/f32[8,256]{1,0:T(8,128)}) custom-call(bf16[2,2,4,2,24,2304]{5,4,3,2,1,0:T(8,128)(2,1)} %pad_maximum_fusion.1.refs_0_, bf16[2,2,4,2,24,768]{5,4,3,2,1,0:T(8,128)(2,1)} %bitcast.238, ...), custom_call_target="tpu_custom_call" | custom-call | flops 9568256 | bytes 19136512 | tf_op jit(solution)/shard_map/reduce_gradients/pallas_call | solution.py:579
  515.9 4.6 subtract_add_fusion
  (264 shorter events, 69.9 us)
Async XLA Ops:
  0.6 95.7 %copy-start = (bf16[768,1536]{1,0:T(8,128)(2,1)S(1)}, bf16[768,1536]{1,0:T(8,128)(2,1)}, u32[]{:S(2)}) copy-start(bf16[768,1536]{1,0:T(8,128)(2,1)} %param.25) | copy-start | bytes 7077892
  0.7 18.4 %copy-start.62 = (s32[4,8]{1,0:T(4,128)S(1)}, s32[4,8]{1,0:T(4,128)}, u32[]{:S(2)}) copy-start(s32[4,8]{1,0:T(4,128)} %param.36) | copy-start | bytes 388
  3.4 17.9 %copy-start.59 = (bf16[768]{0:T(1024)(128)(2,1)S(1)}, bf16[768]{0:T(1024)(128)(2,1)}, u32[]{:S(2)}) copy-start(bf16[768]{0:T(1024)(128)(2,1)} %param.21) | copy-start | bytes 4612
  3.4 17.9 %copy-start.60 = (bf16[768]{0:T(1024)(128)(2,1)S(1)}, bf16[768]{0:T(1024)(128)(2,1)}, u32[]{:S(2)}) copy-start(bf16[768]{0:T(1024)(128)(2,1)} %param.27) | copy-start | bytes 4612
  3.4 18.5 %copy-start.61 = (bf16[768]{0:T(1024)(128)(2,1)S(1)}, bf16[768]{0:T(1024)(128)(2,1)}, u32[]{:S(2)}) copy-start(bf16[768]{0:T(1024)(128)(2,1)} %param.28) | copy-start | bytes 4612
  3.4 19.1 %copy-start.58 = (s32[4,256]{1,0:T(4,128)S(1)}, s32[4,256]{1,0:T(4,128)}, u32[]{:S(2)}) copy-start(s32[4,256]{1,0:T(4,128)} %param.37) | copy-start | bytes 12292
  3.4 41.3 %collective-permute-start.4 = (bf16[4,64,768]{2,1,0:T(8,128)(2,1)}, bf16[4,64,768]{2,1,0:T(8,128)(2,1)}, u32[]{:S(2)}, u32[]{:S(2)}) collective-permute-start(bf16[4,64,768]{2,1,0:T(8,128)(2,1)} %convolution_convert_fusion.15), channel_id=1, source_target_pairs={{0,6},{1,7},{2,0},{3,1},{4,2},{5,3},{6,4},{7,5},{8,14},{9,15},{10,... | collective-permute-start | bytes 1179656 | tf_op jit(solution)/shard_map/ppermute | solution.py:51
  8.5 36.2 %collective-permute-start.3 = (bf16[4,64,768]{2,1,0:T(8,128)(2,1)}, bf16[4,64,768]{2,1,0:T(8,128)(2,1)}, u32[]{:S(2)}, u32[]{:S(2)}) collective-permute-start(bf16[4,64,768]{2,1,0:T(8,128)(2,1)} %convolution_convert_fusion.15), channel_id=1, source_target_pairs={{0,4},{1,5},{2,6},{3,7},{4,0},{5,1},{6,2},{7,3},{8,12},{9,13},{10,... | collective-permute-start | bytes 1179656 | tf_op jit(solution)/shard_map/ppermute | solution.py:51
  8.6 36.2 %collective-permute-start.2 = (bf16[4,64,768]{2,1,0:T(8,128)(2,1)}, bf16[4,64,768]{2,1,0:T(8,128)(2,1)}, u32[]{:S(2)}, u32[]{:S(2)}) collective-permute-start(bf16[4,64,768]{2,1,0:T(8,128)(2,1)} %convolution_convert_fusion.15), channel_id=1, source_target_pairs={{0,2},{1,3},{2,4},{3,5},{4,6},{5,7},{6,0},{7,1},{8,10},{9,11},{10,... | collective-permute-start | bytes 1179656 | tf_op jit(solution)/shard_map/ppermute | solution.py:51
  12.2 37.3 %collective-permute-start = (bf16[4,128,768]{2,1,0:T(8,128)(2,1)}, bf16[4,128,768]{2,1,0:T(8,128)(2,1)S(1)}, u32[]{:S(2)}, u32[]{:S(2)}) collective-permute-start(bf16[4,128,768]{2,1,0:T(8,128)(2,1)} %get-tuple-element.63), channel_id=1, source_target_pairs={{0,1},{1,2},{2,3},{3,4},{4,5},{5,6},{6,7},{8,9},{9,10},{10,11},{11... | collective-permute-start | bytes 2359304 | tf_op jit(solution)/shard_map/ppermute | solution.py:664
  15.6 33.8 %collective-permute-start.1 = (bf16[4,128,768]{2,1,0:T(8,128)(2,1)}, bf16[4,128,768]{2,1,0:T(8,128)(2,1)}, u32[]{:S(2)}, u32[]{:S(2)}) collective-permute-start(bf16[4,128,768]{2,1,0:T(8,128)(2,1)} %get-tuple-element.64), channel_id=1, source_target_pairs={{1,0},{2,1},{3,2},{4,3},{5,4},{6,5},{7,6},{9,8},{10,9},{11,10},{12... | collective-permute-start | bytes 2359304 | tf_op jit(solution)/shard_map/ppermute | solution.py:667
  19.4 8.4 %copy-start.52 = (s32[4,64]{1,0:T(4,128)S(1)}, s32[4,64]{1,0:T(4,128)}, u32[]{:S(2)}) copy-start(s32[4,64]{1,0:T(4,128)} %param.33) | copy-start | bytes 3076
  33.6 6.5 %copy-start.70 = (s32[4,1]{0,1:T(1,128)S(1)}, s32[4,1]{0,1:T(1,128)}, u32[]{:S(2)}) copy-start(s32[4,1]{0,1:T(1,128)} %param.34) | copy-start | bytes 52
  33.7 7.2 %copy-start.23 = (bf16[4,256,768]{2,1,0:T(8,128)(2,1)S(1)}, bf16[4,256,768]{2,1,0:T(8,128)(2,1)}, u32[]{:S(2)}) copy-start(bf16[4,256,768]{2,1,0:T(8,128)(2,1)} %param.20) | copy-start | bytes 4718596
  33.7 7.2 %copy-start.66 = (bf16[1024,768]{1,0:T(8,128)(2,1)S(1)}, bf16[1024,768]{1,0:T(8,128)(2,1)}, u32[]{:S(2)}) copy-start(bf16[1024,768]{1,0:T(8,128)(2,1)} %param.30) | copy-start | bytes 4718596
  40.1 18.0 %copy-start.3 = (bf16[1024,2304]{1,0:T(8,128)(2,1)}, bf16[1024,2304]{1,0:T(8,128)(2,1)S(1)}, u32[]{:S(2)}) copy-start(bf16[1024,2304]{1,0:T(8,128)(2,1)S(1)} %convolution_convert_fusion.3) | copy-start | bytes 14155780
  46.4 39.8 %collective-permute-start.5 = (bf16[4,4,64,768]{3,2,1,0:T(8,128)(2,1)S(1)}, bf16[4,4,64,768]{3,2,1,0:T(8,128)(2,1)S(1)}, u32[]{:S(2)}, u32[]{:S(2)}) collective-permute-start(bf16[4,4,64,768]{3,2,1,0:T(8,128)(2,1)S(1)} %get-tuple-element.62), channel_id=1, source_target_pairs={{0,1},{1,0},{2,3},{3,2},{4,5},{5,4},{6,7},{7,6},{8,9},{9,8},{10,11... | collective-permute-start | bytes 4718600 | tf_op jit(solution)/shard_map/ppermute | solution.py:51
  58.1 15.7 %copy-start.4 = (bf16[1024,1536]{1,0:T(8,128)(2,1)}, bf16[1024,1536]{1,0:T(8,128)(2,1)S(1)}, u32[]{:S(2)}) copy-start(bf16[1024,1536]{1,0:T(8,128)(2,1)S(1)} %convolution_convert_fusion.4) | copy-start | bytes 9437188
  58.2 15.7 %copy-start.68 = (bf16[768,768]{1,0:T(8,128)(2,1)S(1)}, bf16[768,768]{1,0:T(8,128)(2,1)}, u32[]{:S(2)}) copy-start(bf16[768,768]{1,0:T(8,128)(2,1)} %param.23) | copy-start | bytes 3538948
  110.6 24.2 %copy-start.21 = (bf16[1024,768]{1,0:T(8,128)(2,1)}, bf16[1024,768]{1,0:T(8,128)(2,1)S(1)}, u32[]{:S(2)}) copy-start(bf16[1024,768]{1,0:T(8,128)(2,1)S(1)} %get-tuple-element.49) | copy-start | bytes 4718596
  119.7 16.4 %slice-start.4 = ((s8[6291456]{0:T(1024)(128)(4,1)}), s8[4194304]{0:T(1024)(128)(4,1)S(1)}, s32[]{:S(2)}) async-start(s8[6291456]{0:T(1024)(128)(4,1)} %bitcast.212), calls=%async_computation.4 | async-start | bytes 8388608
  121.0 15.1 %slice-start.5 = ((s8[6291456]{0:T(1024)(128)(4,1)}), s8[2097152]{0:T(1024)(128)(4,1)S(1)}, s32[]{:S(2)}) async-start(s8[6291456]{0:T(1024)(128)(4,1)} %bitcast.212), calls=%async_computation.5 | async-start | bytes 4194304
  127.8 7.0 %copy-start.51 = (s32[1,2,4,128]{3,1,2,0:T(2,128)S(1)}, s32[1,2,4,128]{3,1,2,0:T(2,128)}, u32[]{:S(2)}) copy-start(s32[1,2,4,128]{3,1,2,0:T(2,128)} %copy.73) | copy-start | bytes 12292
  127.8 7.5 %copy-start.24 = (bf16[4,256,768]{2,1,0:T(8,128)(2,1)S(1)}, bf16[4,256,768]{2,1,0:T(8,128)(2,1)}, u32[]{:S(2)}) copy-start(bf16[4,256,768]{2,1,0:T(8,128)(2,1)} %param.20) | copy-start | bytes 4718596
  127.8 10.4 %slice-start.6 = ((s8[12582912]{0:T(1024)(128)(4,1)}), s8[4194304]{0:T(1024)(128)(4,1)S(1)}, s32[]{:S(2)}) async-start(s8[12582912]{0:T(1024)(128)(4,1)} %bitcast.246), calls=%async_computation.6 | async-start | bytes 8388608
  127.8 10.4 %slice-start.7 = ((s8[12582912]{0:T(1024)(128)(4,1)}), s8[4194304]{0:T(1024)(128)(4,1)S(1)}, s32[]{:S(2)}) async-start(s8[12582912]{0:T(1024)(128)(4,1)} %bitcast.246), calls=%async_computation.7 | async-start | bytes 8388608
  154.3 6.9 %copy-start.17 = (bf16[4,2,4,64,768]{4,3,0,2,1:T(8,128)(2,1)S(1)}, bf16[4,2,4,64,768]{4,3,0,2,1:T(8,128)(2,1)}, u32[]{:S(2)}) copy-start(bf16[4,2,4,64,768]{4,3,0,2,1:T(8,128)(2,1)} %multiply_convert_fusion) | copy-start | bytes 9437188
  180.7 6.3 %slice-start = ((s8[6291456]{0:T(1024)(128)(4,1)}), s8[4194304]{0:T(1024)(128)(4,1)S(1)}, s32[]{:S(2)}) async-start(s8[6291456]{0:T(1024)(128)(4,1)} %bitcast.186), calls=%async_computation | async-start | bytes 8388608
  233.3 7.7 %copy-start.15 = (bf16[4,256,768]{2,1,0:T(8,128)(2,1)S(1)}, bf16[4,256,768]{2,1,0:T(8,128)(2,1)}, u32[]{:S(2)}) copy-start(bf16[4,256,768]{2,1,0:T(8,128)(2,1)} %copy-done.14) | copy-start | bytes 4718596
  248.3 15.2 %copy-start.30 = (bf16[4,128,768]{2,1,0:T(8,128)(2,1)S(1)}, bf16[4,128,768]{2,1,0:T(8,128)(2,1)}, u32[]{:S(2)}) copy-start(bf16[4,128,768]{2,1,0:T(8,128)(2,1)} %copy-done.29) | copy-start | bytes 2359300
  248.3 15.2 %copy-start.57 = (f32[4,256]{1,0:T(4,128)S(1)}, f32[4,256]{1,0:T(4,128)}, u32[]{:S(2)}) copy-start(f32[4,256]{1,0:T(4,128)} %get-tuple-element.68) | copy-start | bytes 12292
  249.6 204.8 %collective-permute-start.10 = (bf16[4,128,768]{2,1,0:T(8,128)(2,1)}, bf16[4,128,768]{2,1,0:T(8,128)(2,1)}, u32[]{:S(2)}, u32[]{:S(2)}) collective-permute-start(bf16[4,128,768]{2,1,0:T(8,128)(2,1)} %get-tuple-element.59), channel_id=1, source_target_pairs={{0,1},{1,2},{2,3},{3,4},{4,5},{5,6},{6,7},{8,9},{9,10},{10,11},{11... | collective-permute-start | bytes 2359304 | tf_op jit(solution)/shard_map/ppermute | solution.py:817
  254.9 199.5 %collective-permute-start.11 = (bf16[4,128,768]{2,1,0:T(8,128)(2,1)}, bf16[4,128,768]{2,1,0:T(8,128)(2,1)}, u32[]{:S(2)}, u32[]{:S(2)}) collective-permute-start(bf16[4,128,768]{2,1,0:T(8,128)(2,1)} %get-tuple-element.60), channel_id=1, source_target_pairs={{1,0},{2,1},{3,2},{4,3},{5,4},{6,5},{7,6},{9,8},{10,9},{11,10},{12... | collective-permute-start | bytes 2359304 | tf_op jit(solution)/shard_map/ppermute | solution.py:814
  256.1 65.5 %collective-permute-start.6 = (bf16[4,4,64,768]{3,2,1,0:T(8,128)(2,1)S(1)}, bf16[4,4,64,768]{3,2,1,0:T(8,128)(2,1)S(1)}, u32[]{:S(2)}, u32[]{:S(2)}) collective-permute-start(bf16[4,4,64,768]{3,2,1,0:T(8,128)(2,1)S(1)} %slice_bitcast_fusion.2), channel_id=1, source_target_pairs={{0,1},{1,0},{2,3},{3,2},{4,5},{5,4},{6,7},{7,6},{8,9},{9,8},{10,11... | collective-permute-start | bytes 4718600 | tf_op jit(solution)/shard_map/ppermute | solution.py:51
  281.5 56.3 %copy-start.22 = (bf16[1024,768]{1,0:T(8,128)(2,1)S(1)}, bf16[1024,768]{1,0:T(8,128)(2,1)}, u32[]{:S(2)}) copy-start(bf16[1024,768]{1,0:T(8,128)(2,1)} %copy-done.21) | copy-start | bytes 4718596
  324.3 130.0 %collective-permute-start.7 = (bf16[4,64,768]{2,1,0:T(8,128)(2,1)}, bf16[4,64,768]{2,1,0:T(8,128)(2,1)}, u32[]{:S(2)}, u32[]{:S(2)}) collective-permute-start(bf16[4,64,768]{2,1,0:T(8,128)(2,1)} %get-tuple-element.56), channel_id=1, source_target_pairs={{0,6},{1,7},{2,0},{3,1},{4,2},{5,3},{6,4},{7,5},{8,14},{9,15},{10,... | collective-permute-start | bytes 1179656 | tf_op jit(solution)/shard_map/ppermute | solution.py:51
  329.4 124.9 %collective-permute-start.9 = (bf16[4,64,768]{2,1,0:T(8,128)(2,1)}, bf16[4,64,768]{2,1,0:T(8,128)(2,1)}, u32[]{:S(2)}, u32[]{:S(2)}) collective-permute-start(bf16[4,64,768]{2,1,0:T(8,128)(2,1)} %get-tuple-element.57), channel_id=1, source_target_pairs={{0,2},{1,3},{2,4},{3,5},{4,6},{5,7},{6,0},{7,1},{8,10},{9,11},{10,... | collective-permute-start | bytes 1179656 | tf_op jit(solution)/shard_map/ppermute | solution.py:51
  331.5 122.8 %collective-permute-start.8 = (bf16[4,64,768]{2,1,0:T(8,128)(2,1)}, bf16[4,64,768]{2,1,0:T(8,128)(2,1)}, u32[]{:S(2)}, u32[]{:S(2)}) collective-permute-start(bf16[4,64,768]{2,1,0:T(8,128)(2,1)} %get-tuple-element.58), channel_id=1, source_target_pairs={{0,4},{1,5},{2,6},{3,7},{4,0},{5,1},{6,2},{7,3},{8,12},{9,13},{10,... | collective-permute-start | bytes 1179656 | tf_op jit(solution)/shard_map/ppermute | solution.py:51
  338.3 111.9 %copy-start.7 = (bf16[4,256,768]{2,1,0:T(8,128)(2,1)S(1)}, bf16[4,256,768]{2,1,0:T(8,128)(2,1)}, u32[]{:S(2)}) copy-start(bf16[4,256,768]{2,1,0:T(8,128)(2,1)} %copy-done.6) | copy-start | bytes 4718596
  461.5 54.3 %copy-start.11 = (bf16[4,256,768]{2,1,0:T(8,128)(2,1)S(1)}, bf16[4,256,768]{2,1,0:T(8,128)(2,1)}, u32[]{:S(2)}) copy-start(bf16[4,256,768]{2,1,0:T(8,128)(2,1)} %param.19) | copy-start | bytes 4718596
  461.5 54.3 %copy-start.54 = (f32[4,256]{1,0:T(4,128)S(1)}, f32[4,256]{1,0:T(4,128)}, u32[]{:S(2)}) copy-start(f32[4,256]{1,0:T(4,128)} %get-tuple-element.70) | copy-start | bytes 12292
  515.8 5.9 %copy-start.45 = (f32[24,768]{1,0:T(8,128)S(1)}, f32[24,768]{1,0:T(8,128)}, u32[]{:S(2)}) copy-start(f32[24,768]{1,0:T(8,128)} %get-tuple-element.99) | copy-start | bytes 221188
  515.8 6.6 %copy-start.42 = (f32[24,1536]{1,0:T(8,128)S(1)}, f32[24,1536]{1,0:T(8,128)}, u32[]{:S(2)}) copy-start(f32[24,1536]{1,0:T(8,128)} %get-tuple-element.100) | copy-start | bytes 442372
  515.8 7.2 %copy-start.44 = (f32[24,768]{1,0:T(8,128)S(1)}, f32[24,768]{1,0:T(8,128)}, u32[]{:S(2)}) copy-start(f32[24,768]{1,0:T(8,128)} %get-tuple-element.101) | copy-start | bytes 221188
  515.8 7.8 %copy-start.41 = (f32[24,2048]{1,0:T(8,128)S(1)}, f32[24,2048]{1,0:T(8,128)}, u32[]{:S(2)}) copy-start(f32[24,2048]{1,0:T(8,128)} %get-tuple-element.104) | copy-start | bytes 589828
  515.8 8.5 %copy-start.43 = (f32[32,768]{1,0:T(8,128)S(1)}, f32[32,768]{1,0:T(8,128)}, u32[]{:S(2)}) copy-start(f32[32,768]{1,0:T(8,128)} %get-tuple-element.105) | copy-start | bytes 294916
  515.8 9.1 %copy-start.37 = (f32[24,8192]{1,0:T(8,128)S(1)}, f32[24,8192]{1,0:T(8,128)}, u32[]{:S(2)}) copy-start(f32[24,8192]{1,0:T(8,128)} %get-tuple-element.106) | copy-start | bytes 2359300
  520.4 5.5 %copy-start.38 = (f32[128,768]{1,0:T(8,128)S(1)}, f32[128,768]{1,0:T(8,128)}, u32[]{:S(2)}) copy-start(f32[128,768]{1,0:T(8,128)} %get-tuple-element.107) | copy-start | bytes 1179652
  (47 other events, 152.3 us)

commit v2 on v1

--- a/solution.py
+++ b/solution.py
@@ -1,4 +1,5 @@
 import functools
+import math
 import jax
 import jax.numpy as jnp
 from jax import lax
@@ -60,13 +61,15 @@
             total = total + self.shift(send, by).astype(f32)
         return total
 
-    def gather(self, value):
-        return jnp.stack([value] + [self.shift(value, by) for by in range(1, self.count)])
-
-    def return_sum(self, stacked):
-        total = stacked[0].astype(f32)
+    def gather(self, value, dim):
+        parts = [value] + [self.shift(value, by) for by in range(1, self.count)]
+        return jnp.concatenate(parts, axis=dim)
+
+    def return_sum(self, joined, dim):
+        parts = jnp.split(joined, self.count, axis=dim)
+        total = parts[0].astype(f32)
         for by in range(1, self.count):
-            total = total + self.shift(stacked[by], self.count - by).astype(f32)
+            total = total + self.shift(parts[by], self.count - by).astype(f32)
         return total
 
 
@@ -172,10 +175,10 @@
     )(ends, own, edge)
 
 
-def light_back_kernel(ends_ref, own_ref, edge_ref, grad_ref, own_out, edge_out):
+def light_back_unit(reach, groups, own_ref, edge_ref, grad_ref, own_out, edge_out):
     half = RADIUS
     factor = LHD ** (-0.5)
-    for group in range(2):
+    for group in groups:
         dk_own, dv_own = [None] * 4, [None] * 4
         for block in range(2):
             rows = slice(block * half, (block + 1) * half)
@@ -183,7 +186,7 @@
             que = lax.broadcasted_iota(jnp.int32, (2 * half, half), 1)
             keep_own = key <= que + half if block == 0 else key >= que
             key, que = key[:half], que[:half]
-            keep_edge = (key >= que if block == 0 else key <= que) & (ends_ref[block] > 0)
+            keep_edge = (key >= que if block == 0 else key <= que) & reach[block]
             dq, dk_edge, dv_edge = [], [], []
             for h, (a, b, first, end) in enumerate(head_windows()):
                 lanes = slice(group * 384 + a, group * 384 + b)
@@ -231,6 +234,10 @@
         own_out[0, :, at_w] = join_heads(dv_own).astype(bf16)
 
 
+def light_back_kernel(ends_ref, *refs):
+    light_back_unit((ends_ref[0] > 0, ends_ref[1] > 0), range(2), *refs)
+
+
 def light_attention_back(ends, own, edge, grad):
     pieces, tokens = own.shape[:2]
     return pl.pallas_call(
@@ -315,7 +322,8 @@
 
 def heavy_back_kernel(query_ref, pair_ref, live_ref, grad_ref, query_out, pair_out):
     factor = HHD ** (-0.5)
-    keep = live_ref[0] > 0
+    slots = pair_ref.shape[1]
+    keep = jnp.broadcast_to(live_ref[0], (128, slots)).T[:, :1] > 0
     for group in range(HH // 4):
         lanes = slice(group * 256, (group + 1) * 256)
         after = slice(D + lanes.start, D + lanes.stop)
@@ -346,7 +354,7 @@
         in_specs=[
             pl.BlockSpec((1, QCAP, D), lambda p: (p, 0, 0)),
             pl.BlockSpec((1, slots, 2 * D), lambda p: (p, 0, 0)),
-            pl.BlockSpec((1, slots, 1), lambda p: (p, 0, 0)),
+            pl.BlockSpec((1, 1, slots), lambda p: (p, 0, 0)),
             pl.BlockSpec((1, QCAP, D), lambda p: (p, 0, 0)),
         ],
         out_specs=[
@@ -363,18 +371,25 @@
     )(query, pairs, live, grad)
 
 
-def reduce_kernel(jobs, sizes, *refs):
+def reduce_kernel(jobs, arrays, sizes, work, *refs):
     n_x, n_y = sizes
-    count = len(jobs)
-    sources, outs, scratch = refs[:count], refs[count : 2 * count], refs[2 * count :]
-    names = ("own", "core", "ax", "ay", "by", "bx", "zz", "lsem", "rsem", "ssem")
-    held = [
-        dict(zip(names, scratch[len(names) * a : len(names) * (a + 1)])) for a in range(count)
-    ]
+    n_dp = n_x * CORES
+    given, made = (3, 2) if work else (0, 0)
+    sources, outs = refs[:arrays], refs[arrays + given : 2 * arrays + given]
+    operands = refs[arrays : arrays + given] + refs[2 * arrays + given :][:made]
+    scratch = list(refs[2 * arrays + given + made :])
+    held = []
+    for job in jobs:
+        names = SCRATCH[job[1]]
+        held.append(dict(zip(names, scratch[: len(names)])))
+        del scratch[: len(names)]
     dp, seq = lax.axis_index("dp"), lax.axis_index("seq")
     x, c = dp // CORES, dp % CORES
     z, y = seq // n_y, seq % n_y
 
+    def to_dp(by):
+        return (lax.rem(dp + by, n_dp), seq)
+
     def to_core():
         return (x * CORES + (1 - c), seq)
 
@@ -387,8 +402,7 @@
     def to_z(by):
         return (dp, ((z + by) % DEPTH) * n_y + y)
 
-    peers = [to_core()]
-    peers += [to_x(by) for by in range(1, n_x)]
+    peers = [to_dp(by) for by in range(1, n_dp)]
     peers += [to_y(by) for by in range(1, n_y)]
     peers += [to_z(by) for by in range(1, DEPTH)]
     barrier = pltpu.get_barrier_semaphore()
@@ -396,198 +410,278 @@
         pl.semaphore_signal(barrier, inc=1, device_id=peer, device_id_type=MESH)
     pl.semaphore_wait(barrier, len(peers))
 
-    def send(src, dst, a, stage, k, peer):
+    def copy(src, dst, a, stage, k, peer):
         h = held[a]
-        pltpu.make_async_remote_copy(
+        return pltpu.make_async_remote_copy(
             src_ref=src,
             dst_ref=dst,
             send_sem=h["ssem"].at[stage],
             recv_sem=h["rsem"].at[stage, k],
             device_id=peer,
             device_id_type=MESH,
-        ).start()
-
-    def arrived(buffer, a, stage, k):
+        )
+
+    def arrived(name, a, stage, k):
+        buffer = held[a][name].at[k]
+        copy(buffer, buffer, a, stage, k, to_core()).wait_recv()
+
+    def columns(a, k):
+        _, _, start, width, _ = jobs[a]
+        return pl.ds(start + k * width, width)
+
+    def source(a):
+        return sources[jobs[a][0]]
+
+    def local(a, k):
+        h, cols = held[a], columns(a, k)
+        whole = source(a)
+        part = whole.at[:, c, :, :, :, cols] if "core" in h else whole.at[..., cols]
+        return pltpu.make_async_copy(part, h["own"].at[k], h["lsem"].at[k])
+
+    def add_all(target, pairs):
+        for at, addend, place in pairs:
+            target[at] = target[at] + addend[place]
+
+    def begin(a, k):
         h = held[a]
-        pltpu.make_async_remote_copy(
-            src_ref=buffer,
-            dst_ref=buffer,
-            send_sem=h["ssem"].at[stage],
-            recv_sem=h["rsem"].at[stage, k],
-            device_id=to_core(),
-            device_id_type=MESH,
-        ).wait_recv()
-
-    def columns(a, k):
-        width = jobs[a][0]
-        return pl.ds(k * width, width)
-
-    def local(a, k):
-        h = held[a]
-        return pltpu.make_async_copy(
-            sources[a].at[:, c, :, :, :, columns(a, k)], h["own"].at[k], h["lsem"].at[k]
-        )
-
-    def stage_core_start(a, k):
         local(a, k).start()
-        send(
-            sources[a].at[:, 1 - c, :, :, :, columns(a, k)],
-            held[a]["core"].at[k],
-            a,
-            0,
-            k,
-            to_core(),
-        )
-
-    def add_blocks(total, index_of, pieces):
-        @pl.loop(0, total)
-        def _(i):
-            for target, addend in pieces:
-                at = index_of(i)
-                target[at] = target[at] + addend[at]
-
-    def stage_core(a, k):
-        h = held[a]
+        if "core" in h:
+            src = source(a).at[:, 1 - c, :, :, :, columns(a, k)]
+            copy(src, h["core"].at[k], a, 0, k, to_core()).start()
+        else:
+            for by in range(1, n_y):
+                src = source(a).at[:, :, (y + by) % n_y, :, columns(a, k)]
+                copy(src, h["yy"].at[k, by - 1], a, 2, k, to_y(by)).start()
+
+    def first(a, k):
+        h, kind = held[a], jobs[a][1]
         local(a, k).wait()
-        arrived(h["core"].at[k], a, 0, k)
-        own, other = h["own"], h["core"]
+        if "core" not in h:
+            return
+        own = h["own"]
+        arrived("core", a, 0, k)
 
         @pl.loop(0, n_x * DEPTH)
         def _(i):
             for j in range(n_y):
                 at = (k, i // DEPTH, i % DEPTH, j)
-                own[at] = own[at] + other[at]
-
-        half = k // 2
-        if k % 2 == 0:
+                own[at] = own[at] + h["core"][at]
+
+        if kind == "xy":
             for by in range(1, n_x):
-                send(own.at[k, (x + by) % n_x], h["ax"].at[half, by - 1], a, 1, k, to_x(by))
+                src = own.at[k, (x + by) % n_x]
+                copy(src, h["xx"].at[k, by - 1], a, 1, k, to_x(by)).start()
         else:
             for by in range(1, n_y):
-                send(own.at[k, :, :, (y + by) % n_y], h["by"].at[half, by - 1], a, 2, k, to_y(by))
-
-    def stage_second(a, k):
-        h = held[a]
-        own, half = h["own"], k // 2
-        if k % 2 == 0:
-            arrived(h["ax"].at[half], a, 1, k)
+                src = own.at[k, :, :, (y + by) % n_y]
+                copy(src, h["yy"].at[k, by - 1], a, 2, k, to_y(by)).start()
+
+    def second(a, k):
+        h, kind = held[a], jobs[a][1]
+        own = h.get("own")
+        if kind == "xy":
+            arrived("xx", a, 1, k)
 
             @pl.loop(0, DEPTH)
             def _(i):
                 for j in range(n_y):
                     for s in range(n_x - 1):
                         at = (k, x, i, j)
-                        own[at] = own[at] + h["ax"][half, s, i, j]
+                        own[at] = own[at] + h["xx"][k, s, i, j]
 
             for by in range(1, n_y):
-                send(
-                    own.at[k, x, :, (y + by) % n_y], h["ay"].at[half, by - 1], a, 2, k, to_y(by)
-                )
-        else:
-            arrived(h["by"].at[half], a, 2, k)
+                src = own.at[k, x, :, (y + by) % n_y]
+                copy(src, h["yy"].at[k, by - 1], a, 2, k, to_y(by)).start()
+        elif kind == "yx":
+            arrived("yy", a, 2, k)
 
             @pl.loop(0, DEPTH)
             def _(i):
                 for j in range(n_x):
                     for s in range(n_y - 1):
                         at = (k, j, i, y)
-                        own[at] = own[at] + h["by"][half, s, j, i]
+                        own[at] = own[at] + h["yy"][k, s, j, i]
 
             for by in range(1, n_x):
-                send(
-                    own.at[k, (x + by) % n_x, :, y], h["bx"].at[half, by - 1], a, 1, k, to_x(by)
-                )
-
-    def stage_third(a, k):
+                src = own.at[k, (x + by) % n_x, :, y]
+                copy(src, h["xx"].at[k, by - 1], a, 1, k, to_x(by)).start()
+
+    def third(a, k):
+        h, kind = held[a], jobs[a][1]
+        own = h.get("own")
+        if kind in ("xy", "yx"):
+            name, stage, others = ("yy", 2, n_y - 1) if kind == "xy" else ("xx", 1, n_x - 1)
+            arrived(name, a, stage, k)
+
+            @pl.loop(0, DEPTH)
+            def _(i):
+                for s in range(others):
+                    at = (k, x, i, y)
+                    own[at] = own[at] + h[name][k, s, i]
+
+            for by in range(1, DEPTH):
+                src = own.at[k, x, (z + by) % DEPTH, y]
+                copy(src, h["zz"].at[k, by - 1], a, 3, k, to_z(by)).start()
+        else:
+            arrived("yy", a, 2, k)
+
+            @pl.loop(0, DEPTH)
+            def _(i):
+                for g in range(own.shape[1]):
+                    for s in range(n_y - 1):
+                        at = (k, g, i, y)
+                        own[at] = own[at] + h["yy"][k, s, g, i]
+
+            for by in range(1, DEPTH):
+                src = own.at[k, :, (z + by) % DEPTH, y]
+                copy(src, h["zz"].at[k, by - 1], a, 3, k, to_z(by)).start()
+
+    def fourth(a, k):
         h = held[a]
-        own, half = h["own"], k // 2
-        name, stage, others = ("ay", 2, n_y - 1) if k % 2 == 0 else ("bx", 1, n_x - 1)
-        arrived(h[name].at[half], a, stage, k)
-
-        @pl.loop(0, DEPTH)
-        def _(i):
-            for s in range(others):
-                at = (k, x, i, y)
-                own[at] = own[at] + h[name][half, s, i]
-
-        for by in range(1, DEPTH):
-            send(own.at[k, x, (z + by) % DEPTH, y], h["zz"].at[k, by - 1], a, 3, k, to_z(by))
-
-    def stage_last(a, k):
+        array, kind, start, width, chunks = jobs[a]
+        arrived("zz", a, 3, k)
+        if kind != "gates":
+            here = h["own"].at[k, 0, z, y] if kind == "seq" else h["own"].at[k, x, z, y]
+            total = here[...].astype(f32)
+            for s in range(DEPTH - 1):
+                block = h["zz"][k, s, 0] if kind == "seq" else h["zz"][k, s]
+                total = total + block.astype(f32)
+            outs[array][:, start + k * width : start + (k + 1) * width] = total
+        else:
+
+            @pl.loop(0, n_dp)
+            def _(g):
+                total = h["own"][k, g, z, y].astype(f32)
+                for s in range(DEPTH - 1):
+                    total = total + h["zz"][k, s, g].astype(f32)
+                h["sum"][k, g] = total.astype(bf16)
+
+            h["dd"][k, dp] = h["sum"][k, dp]
+            for by in range(1, n_dp):
+                peer = lax.rem(dp + by, n_dp)
+                copy(h["sum"].at[k, peer], h["dd"].at[k, dp], a, 0, k, to_dp(by)).start()
+
+    def last(a, k):
         h = held[a]
-        width = jobs[a][0]
-        arrived(h["zz"].at[k], a, 3, k)
-        total = h["own"][k, x, z, y].astype(f32)
-        for s in range(DEPTH - 1):
-            total = total + h["zz"][k, s].astype(f32)
-        outs[a][:, k * width : (k + 1) * width] = total
-
-    order = [(a, k) for a in range(count) for k in range(jobs[a][1])]
-    for a, k in order:
-        stage_core_start(a, k)
-    lags = [(stage_core, 0), (stage_second, 4), (stage_third, 8), (stage_last, 12)]
-    for step in range(len(order) + lags[-1][1]):
-        for stage, lag in lags:
-            if 0 <= step - lag < len(order):
-                stage(*order[step - lag])
-
-    for a in range(count):
+        array, kind, start, width, chunks = jobs[a]
+        if kind == "gates":
+            part = h["dd"].at[k, pl.ds(0, n_dp - 1)]
+            copy(part, part, a, 0, k, to_core()).wait_recv()
+            half = chunks // 2
+            for g in range(n_dp):
+                to = (((k // half) * n_dp + g) * half + k % half) * width
+                outs[array][:, to : to + width] = h["dd"][k, g].astype(f32)
+
+    lists = {"all": [], "rest": []}
+    for a, job in enumerate(jobs):
+        group = "all" if "core" in held[a] else "rest"
+        lists[group].append([(a, k) for k in range(job[4])])
+    events = []
+    for group, parts in lists.items():
+        order = interleave(parts)
+        pace = max(len(interleave(p)) for p in lists.values()) / max(1, len(order))
+        for i, (a, k) in enumerate(order):
+            for stage, lag in zip((begin, first, second, third, fourth, last), LAGS[group]):
+                events.append((i * pace + lag, len(events), stage, (a, k)))
+    if work:
+        reach = (seq > 0, seq < DEPTH * n_y - 1)
+
+        def unit(p, g):
+            light_back_unit(reach, (g,), *[ref.at[pl.ds(p, 1)] for ref in operands])
+
+        for p in range(operands[0].shape[0]):
+            for g in range(2):
+                events.append(((2 * p + g) * 1.5, len(events), unit, (p, g)))
+    for _, _, stage, what in sorted(events, key=lambda e: e[:2]):
+        stage(*what)
+
+    for a, job in enumerate(jobs):
         h = held[a]
-
-        def sent(buffer, stage):
-            pltpu.make_async_remote_copy(
-                src_ref=buffer,
-                dst_ref=buffer,
-                send_sem=h["ssem"].at[stage],
-                recv_sem=h["rsem"].at[stage, 0],
-                device_id=to_core(),
-                device_id_type=MESH,
-            ).wait_send()
-
-        sent(h["core"], 0)
-        sent(h["ax"], 1)
-        sent(h["bx"], 1)
-        sent(h["by"], 2)
-        sent(h["ay"], 2)
-        sent(h["zz"], 3)
-
-
-def reduce_all(values, widths, n_x, n_y, collective_id):
-    jobs, operands, out_shape, scratch = [], [], [], []
-    devices = n_x * CORES * DEPTH * n_y
-    for value, width in zip(values, widths):
+        for name, stage in (("core", 0), ("xx", 1), ("yy", 2), ("zz", 3)):
+            if name in h:
+                copy(h[name], h[name], a, stage, 0, to_core()).wait_send()
+        if job[1] == "gates":
+            part = h["dd"].at[:, pl.ds(0, n_dp - 1)]
+            copy(part, part, a, 0, 0, to_core()).wait_send()
+
+
+def interleave(parts):
+    keyed = [((i + 0.5) / len(p), n, v) for n, p in enumerate(parts) for i, v in enumerate(p)]
+    return [v for _, _, v in sorted(keyed)]
+
+
+LAGS = {"all": (-4, 0, 2, 4, 6.5, 9), "rest": (-2, -1, -1, 1, 3.5, 6)}
+SCRATCH = {
+    "xy": ("own", "core", "xx", "yy", "zz", "lsem", "rsem", "ssem"),
+    "yx": ("own", "core", "xx", "yy", "zz", "lsem", "rsem", "ssem"),
+    "seq": ("own", "yy", "zz", "lsem", "rsem", "ssem"),
+    "gates": ("own", "yy", "zz", "sum", "dd", "lsem", "rsem", "ssem"),
+}
+
+
+def copy_kernel(*refs):
+    count = len(refs) // 2
+    for i in range(count):
+        refs[count + i][...] = refs[i][...]
+
+
+def copy_all(values):
+    count = len(values)
+    return pl.pallas_call(
+        copy_kernel,
+        out_shape=[jax.ShapeDtypeStruct(v.shape, v.dtype) for v in values],
+        in_specs=[pl.BlockSpec(memory_space=pltpu.VMEM)] * count,
+        out_specs=[pl.BlockSpec(memory_space=pltpu.VMEM)] * count,
+        name="copy_outputs",
+    )(*values)
+
+
+def reduce_all(values, jobs, n_x, n_y, collective_id, work=()):
+    n_dp = n_x * CORES
+    kinds = {array: kind for array, kind, _, _, _ in jobs}
+    operands, out_shape, scratch = [], [], []
+    for array, value in enumerate(values):
         height, columns = value.shape
-        chunk = height // devices
-        k = columns // width
-        jobs.append((width, k))
-        operands.append(value.reshape(n_x, CORES, DEPTH, n_y, chunk, columns))
+        groups = {"seq": (1,), "gates": (n_dp,)}.get(kinds[array], (n_x, CORES))
+        chunk = height // (n_y * DEPTH * math.prod(groups))
+        operands.append(value.reshape(groups + (DEPTH, n_y, chunk, columns)))
+        columns *= n_dp if kinds[array] == "gates" else 1
         out_shape.append(jax.ShapeDtypeStruct((chunk, columns), f32))
-        tile = (chunk, width)
+    for array, kind, _, width, k in jobs:
+        tile = (out_shape[array].shape[0], width)
+        lead = {"seq": (1,), "gates": (n_dp,)}.get(kind, (n_x,))
+        shapes = [(k,) + lead + (DEPTH, n_y)]
+        if kind == "xy":
+            shapes += shapes + [(k, n_x - 1, DEPTH, n_y), (k, n_y - 1, DEPTH), (k, DEPTH - 1)]
+        elif kind == "yx":
+            shapes += shapes + [(k, n_x - 1, DEPTH), (k, n_y - 1, n_x, DEPTH), (k, DEPTH - 1)]
+        else:
+            shapes += [(k, n_y - 1) + lead + (DEPTH,), (k, DEPTH - 1) + lead]
+        if kind == "gates":
+            shapes += [(k, n_dp)] * 2
+        scratch += [pltpu.VMEM(shape + tile, bf16) for shape in shapes]
         scratch += [
-            pltpu.VMEM((k, n_x, DEPTH, n_y) + tile, bf16),
-            pltpu.VMEM((k, n_x, DEPTH, n_y) + tile, bf16),
-            pltpu.VMEM((k // 2, n_x - 1, DEPTH, n_y) + tile, bf16),
-            pltpu.VMEM((k // 2, n_y - 1, DEPTH) + tile, bf16),
-            pltpu.VMEM((k // 2, n_y - 1, n_x, DEPTH) + tile, bf16),
-            pltpu.VMEM((k // 2, n_x - 1, DEPTH) + tile, bf16),
-            pltpu.VMEM((k, DEPTH - 1) + tile, bf16),
             pltpu.SemaphoreType.DMA((k,)),
             pltpu.SemaphoreType.DMA((4, k)),
             pltpu.SemaphoreType.DMA((4,)),
         ]
     total = sum(v.size for v in values)
+    out_shape += [jax.ShapeDtypeStruct(v.shape, bf16) for v in work[:2]]
+    here = pl.BlockSpec(memory_space=pltpu.VMEM)
     return pl.pallas_call(
-        functools.partial(reduce_kernel, tuple(jobs), (n_x, n_y)),
+        functools.partial(reduce_kernel, tuple(jobs), len(values), (n_x, n_y), bool(work)),
         out_shape=out_shape,
-        in_specs=[pl.BlockSpec(memory_space=pl.ANY)] * len(values),
-        out_specs=[pl.BlockSpec(memory_space=pltpu.VMEM)] * len(values),
+        in_specs=[pl.BlockSpec(memory_space=pl.ANY)] * len(values) + [here] * len(work),
+        out_specs=[here] * len(out_shape),
         scratch_shapes=scratch,
         compiler_params=pltpu.CompilerParams(
             collective_id=collective_id, has_side_effects=True, vmem_limit_bytes=60 << 20
         ),
-        cost_estimate=pl.CostEstimate(flops=2 * total, bytes_accessed=4 * total, transcendentals=0),
+        cost_estimate=pl.CostEstimate(
+            flops=2 * total, bytes_accessed=32 * total, transcendentals=0
+        ),
         name="reduce_gradients",
-    )(*operands)
+    )(*operands, *work)
 
 
 def per_device(
@@ -651,6 +745,11 @@
             axis=1,
         )
 
+    def reduce_seq(value):
+        parts = value.reshape(1, DEPTH, n_y, value.shape[0] // n_seq, value.shape[1])
+        parts = ring_z.scatter_sum(parts, 1).astype(bf16)
+        return ring_y.scatter_sum(parts, 1)[0]
+
     def reduce_vectors(value):
         count, width = value.shape
         chunk = width // (n_dp * n_seq)
@@ -673,7 +772,7 @@
     key_raw = jnp.einsum("pkt,ptd->pkd", key_pick, layer_input, preferred_element_type=f32).astype(
         bf16
     )
-    key_all = ring_y.gather(ring_z.gather(key_raw))
+    key_all = lax.all_gather(key_raw, "seq", axis=1, tiled=True)
 
     gain_first = first_gain.astype(f32)
     inputs = layer_input.astype(f32)
@@ -691,21 +790,10 @@
     light_att = light_attention(reach, own_proj, edge_proj).reshape(rows, D)
 
     key_slots = n_seq * KCAP
-    key_rows_all = key_all.transpose(2, 0, 1, 3, 4).reshape(pieces * key_slots, D)
+    key_rows_all = key_all.reshape(pieces * key_slots, D)
     normed_keys = (norm_parts(key_rows_all.astype(f32))[0] * gain_first).astype(bf16)
     heavy_pairs = mm(normed_keys, heavy_keyvalue).astype(bf16).reshape(pieces, key_slots, 2 * D)
-    from_z = (ring_z.place - jnp.arange(DEPTH, dtype=jnp.int32)) % DEPTH
-    from_y = (ring_y.place - jnp.arange(n_y, dtype=jnp.int32)) % n_y
-    sources = (from_z[None, :] * n_y + from_y[:, None]).reshape(-1)
-    counts_here = jnp.sum(
-        jnp.where(
-            sources[None, :, None] == jnp.arange(n_seq, dtype=jnp.int32)[None, None, :],
-            key_count[:, None, :],
-            0,
-        ),
-        axis=-1,
-    )
-    key_live = jnp.arange(KCAP, dtype=jnp.int32)[None, None, :] < counts_here[:, :, None]
+    key_live = jnp.arange(KCAP, dtype=jnp.int32)[None, None, :] < key_count[:, :, None]
     key_live = key_live.reshape(pieces, 1, key_slots).astype(f32)
     query_rows = (
         jnp.einsum("pqt,ptd->pqd", query_pick, normed_first, preferred_element_type=f32)
@@ -747,19 +835,40 @@
     grad_light_gate, grad_light_up = light_pull(mm_nt(cot, light_down))
     grad_light_pre = jnp.concatenate([grad_light_gate.astype(bf16), grad_light_up.astype(bf16)], 1)
 
-    wide_hidden = heavy_gates.shape[1] // 2
-    heavy_gate = mm(feed_in, heavy_gates[:, :wide_hidden])
-    heavy_up = mm(feed_in, heavy_gates[:, wide_hidden:])
+    dp_rank = lax.axis_index("dp")
+    share = heavy_gates.shape[1] // (2 * n_dp)
+    gates_here = [
+        lax.dynamic_slice_in_dim(heavy_gates, (part * n_dp + dp_rank) * share, share, 1)
+        for part in range(2)
+    ]
+    down_here = lax.dynamic_slice_in_dim(heavy_down, dp_rank * share, share, 0)
+    feed_all = core.gather(ring_x.gather(jnp.stack([feed_in, grad_in]), 1), 1)
+    feed_all, light_act, grad_light_pre = lax.optimization_barrier(
+        (feed_all, light_act, grad_light_pre)
+    )
+    feed_rows, grad_rows = feed_all[0], feed_all[1]
+    heavy_gate = mm(feed_rows, gates_here[0])
+    heavy_up = mm(feed_rows, gates_here[1])
     heavy_act, heavy_pull = jax.vjp(glu_rows, heavy_gate, heavy_up)
     heavy_act = heavy_act.astype(bf16)
-    heavy_result = mm(heavy_act, heavy_down).astype(bf16)
-    grad_heavy_gate, grad_heavy_up = heavy_pull(mm_nt(grad_in, heavy_down))
-    grad_heavy_pre = jnp.concatenate([grad_heavy_gate.astype(bf16), grad_heavy_up.astype(bf16)], 1)
-    grad_feed_in = mm_nt(grad_heavy_pre, heavy_gates).astype(bf16)
-    heavy_down_grad = mm_tn(heavy_act, grad_in).astype(bf16)
-    heavy_gates_grad = mm_tn(feed_in, grad_heavy_pre).astype(bf16)
-    light_down_grad = mm_tn(light_act, cot).astype(bf16)
-    light_gates_grad = mm_tn(normed_second, grad_light_pre).astype(bf16)
+    heavy_part = mm(heavy_act, down_here).astype(bf16)
+    grad_heavy_gate, grad_heavy_up = heavy_pull(mm_nt(grad_rows, down_here))
+    grad_heavy_pre = [grad_heavy_gate.astype(bf16), grad_heavy_up.astype(bf16)]
+    grad_part = (
+        mm_nt(grad_heavy_pre[0], gates_here[0]) + mm_nt(grad_heavy_pre[1], gates_here[1])
+    ).astype(bf16)
+    back = core.return_sum(jnp.stack([heavy_part, grad_part]), 1).astype(bf16)
+    back, light_act_late, grad_light_late = lax.optimization_barrier(
+        (back, light_act, grad_light_pre)
+    )
+    back = ring_x.return_sum(back, 1).astype(bf16)
+    heavy_result, grad_feed_in = back[0], back[1]
+    heavy_down_grad = mm_tn(heavy_act, grad_rows).astype(bf16)
+    heavy_gates_grad = jnp.concatenate(
+        [mm_tn(feed_rows, grad_heavy_pre[0]), mm_tn(feed_rows, grad_heavy_pre[1])], axis=1
+    ).astype(bf16)
+    light_down_grad = mm_tn(light_act_late, cot).astype(bf16)
+    light_gates_grad = mm_tn(normed_second, grad_light_late).astype(bf16)
 
     token_result = mm_tn(pick, heavy_result)
     output = (middle + light_feed + gating * token_result).astype(bf16).reshape(layer_input.shape)
@@ -793,20 +902,50 @@
     grad_hq_low, grad_hkv_low = heavy_attention_back(
         heavy_query,
         heavy_pairs,
-        key_live.reshape(pieces, key_slots, 1),
+        key_live,
         grad_heavy_att.reshape(pieces, QCAP, D),
     )
     grad_hq_low = grad_hq_low.reshape(pieces * QCAP, D)
     grad_hkv_low = grad_hkv_low.reshape(pieces * key_slots, 2 * D)
     grad_key_rows = mm_nt(grad_hkv_low, heavy_keyvalue).astype(bf16)
-    grad_key_rows = grad_key_rows.reshape(pieces, n_y, DEPTH, KCAP, D).transpose(1, 2, 0, 3, 4)
-    grad_key_own = ring_z.return_sum(ring_y.return_sum(grad_key_rows).astype(bf16))
     heavy_keyvalue_grad = mm_tn(normed_keys, grad_hkv_low).astype(bf16)
     heavy_queries_grad = mm_tn(query_rows, grad_hq_low).astype(bf16)
 
-    grad_own, grad_edge = light_attention_back(
-        reach, own_proj, edge_proj, grad_light_att.reshape(pieces, tokens, D)
-    )
+    grad_light_att, grad_key_rows = lax.optimization_barrier((grad_light_att, grad_key_rows))
+    grad_key_own = lax.psum_scatter(
+        grad_key_rows.reshape(pieces, key_slots, D), "seq", scatter_dimension=1, tiled=True
+    )
+    grad_light_att = grad_light_att.reshape(pieces, tokens, D)
+    each = D // (n_dp * n_seq)
+    early = [
+        light_gates_grad,
+        light_down_grad,
+        light_output_grad,
+        heavy_output_grad,
+        heavy_gates_grad,
+        heavy_down_grad,
+    ]
+    if each % 8 == 0:
+        jobs = [
+            (0, "xy", 0, 512, light_gates_grad.shape[1] // 512),
+            (1, "xy", 0, 384, D // 384),
+            (2, "xy", 0, 384, D // 384),
+            (3, "xy", 0, 384, D // 384),
+            (4, "gates", 0, 256, heavy_gates_grad.shape[1] // 256),
+            (5, "seq", 0, 128, D // 128),
+        ]
+        *early, grad_own, grad_edge = reduce_all(
+            early, jobs, n_x, n_y, 0, (own_proj, edge_proj, grad_light_att)
+        )
+    else:
+        grad_own, grad_edge = light_attention_back(reach, own_proj, edge_proj, grad_light_att)
+        parts = heavy_gates_grad.reshape(n_dp, DEPTH, n_y, each, -1)
+        parts = ring_z.scatter_sum(parts, 1).astype(bf16)
+        parts = ring_y.scatter_sum(parts, 1).astype(bf16)
+        parts = lax.all_to_all(parts, "dp", split_axis=0, concat_axis=0, tiled=True)
+        parts = parts.reshape(n_dp, each, 2, -1).transpose(1, 2, 0, 3)
+        early = [reduce_split(v) for v in early[:4]]
+        early += [parts.reshape(each, -1).astype(f32), reduce_seq(heavy_down_grad)]
     grad_own = grad_own.reshape(rows, 3 * D)
     grad_edge = grad_edge.reshape(pieces * 2 * RADIUS, 2 * D)
     grad_edge_rows = mm_nt(grad_edge, light_inputs[:, D:]).astype(bf16)
@@ -839,38 +978,38 @@
     )
     vectors = jnp.stack([first_gain_grad, second_gain_grad, router_grad])
     devices = n_dp * n_seq
-    feed_grads = [heavy_gates_grad, heavy_down_grad, light_gates_grad, light_down_grad]
-    late_grads = [
-        light_inputs_grad,
-        light_output_grad,
-        heavy_queries_grad,
-        heavy_keyvalue_grad,
-        heavy_output_grad,
-    ]
-    if D // devices % 8 == 0:
-        each = D // devices
+    late = [light_inputs_grad, heavy_queries_grad, heavy_keyvalue_grad]
+    if each % 8 == 0:
         lines = vectors.reshape(3, devices, each).transpose(1, 0, 2)
         lines = jnp.pad(lines, ((0, 0), (0, 5), (0, 256 - each))).reshape(devices * 8, 256)
-        feed_grads = reduce_all(feed_grads, (512, 128, 512, 384), n_x, n_y, 0)
-        *late_grads, lines = reduce_all(
-            late_grads + [lines.astype(bf16)], (384,) * 5 + (128,), n_x, n_y, 1
-        )
+        jobs = []
+        for array, value in enumerate(late):
+            half = value.shape[1] // 2
+            jobs += [(array, "xy", 0, 384, half // 384), (array, "yx", half, 384, half // 384)]
+        jobs.append((len(late), "xy", 0, 256, 1))
+        sums = reduce_all(late + [lines.astype(bf16)], jobs, n_x, n_y, 1)
+        *sums, lines = copy_all([*early, *sums])
+        early, late = sums[: len(early)], sums[len(early) :]
         vectors = lines[:3, :each]
     else:
-        feed_grads = [reduce_split(v) for v in feed_grads]
-        late_grads = [reduce_split(v) for v in late_grads]
+        late = [reduce_split(v) for v in late]
         vectors = reduce_vectors(vectors)
+    light_gates_grad, light_down_grad, light_output_grad, heavy_output_grad = early[:4]
     return (
         output,
         input_grad,
         vectors[0],
-        *late_grads,
+        late[0],
+        light_output_grad,
+        late[1],
+        late[2],
+        heavy_output_grad,
         vectors[1],
         vectors[2],
-        feed_grads[2],
-        feed_grads[3],
-        feed_grads[0],
-        feed_grads[1],
+        light_gates_grad,
+        light_down_grad,
+        early[4],
+        early[5],
     )
 
 

time: 530 us -> 475 us (0.90)
  starting transfers between devices: 39 us -> 17.2 us
  Pallas kernels: 221 us -> 205 us
  local copies, waits for them, and re-layouts: 35.9 us -> 21 us
  between operations: 2.19 us -> 15.5 us
  matrix products: 149 us -> 137 us
  waiting for transfers between devices: 49.5 us -> 43.5 us
    ppermute x8 -> x4, waiting for transfers between devices: 49.5 us -> 8.34 us  [shift(): return lax.ppermute(value, self.axis, pairs)]
    ppermute x1, waiting for transfers between devices: 0.01 us -> 24.8 us  [per_device(): lax.ppermute(layer_input[:, tokens - RADIUS:], 'seq', [(i, i + 1) for i i...]
    ppermute x8 -> x4, starting transfers between devices: 27.7 us -> 3.61 us  [shift(): return lax.ppermute(value, self.axis, pairs)]
    pallas_call x3, Pallas kernels: 192 us -> 176 us  [the longest x2 174 us: reduce_all(): pl.pallas_call(functools.partial(reduce_kernel, tuple(jobs), len(values),...]
    dot_general x36 -> x39, matrix products: 135 us -> 123 us  [dot(): lax.dot_general(left, right, (over, ((), ())), preferred_element_type=f32)]
    all_gather x0 -> x1, waiting for transfers between devices: none -> 10.4 us  [per_device(): key_all = lax.all_gather(key_raw, 'seq', axis=1, tiled=True)]
    unnamed x178 -> x142, local copies, waits for them, and re-layouts: 17.9 us -> 8.11 us
    concatenate x0 -> x4, other arithmetic: none -> 6.73 us  [the longest x1 2.39 us: per_device(): jnp.concatenate([grad_light_gate.astype(bf16), grad_light_up.astype(bf16)...]
  transfers between devices with their start and end apart: 12 -> 10, of which waited for: 2 -> 4; matrix products, arithmetic and copies ran while one was open for 13% -> 21% of each run, Pallas kernels for 24% -> 30%
where the time goes in v2:
time: 475 us; the launch traced here: 472 us
  Pallas kernels  205 us (43%)
  matrix products  137 us (29%)
  waiting for transfers between devices  43.5 us (9%)
  other arithmetic  33 us (7%)
  local copies, waits for them, and re-layouts  21 us (4%)
  starting transfers between devices  17.2 us (4%)
  between operations  15.5 us (3%)
    pallas_call x2, Pallas kernels, reduce_all(): pl.pallas_call(functools.partial(reduce_kernel, tuple(jobs), len(values),...  174 us
    dot_general x39, matrix products, dot(): lax.dot_general(left, right, (over, ((), ())), preferred_element_type=f32)  123 us
    ppermute x1, waiting for transfers between devices, per_device(): lax.ppermute(layer_input[:, tokens - RADIUS:], 'seq', [(i, i + 1) for i i...  24.8 us
    pallas_call x1, Pallas kernels, light_attention(): pl.pallas_call(light_kernel, out_shape=jax.ShapeDtypeStruct((pieces, toke...  15.9 us
    all_gather x1, waiting for transfers between devices, per_device(): key_all = lax.all_gather(key_raw, 'seq', axis=1, tiled=True)  10.4 us
  transfers between devices with their start and end apart: 10, of which 4 were waited for; matrix products, arithmetic and copies ran while one was open for 21% of the time, Pallas kernels for 30%

profile of v2, /device:TPU:0, one launch (start us, length us, event | category | flops | bytes accessed | tf_op | source)
XLA Modules:
  0.0 472.0 jit_solution(6378945208736012336)
XLA Ops:
  7.3 2.7 convolution_convert_fusion.16
  10.1 2.6 fusion.113
  12.7 5.0 %collective-permute-start = (bf16[4,128,768]{2,1,0:T(8,128)(2,1)}, bf16[4,128,768]{2,1,0:T(8,128)(2,1)S(1)}, u32[]{:S(2)}, u32[]{:S(2)}) collective-permute-start(bf16[4,128,768]{2,1,0:T(8,128)(2,1)} %get-tuple-element.94), channel_id=1, source_target_pairs={{0,1},{1,2},{2,3},{3,4},{4,5},{5,6},{6,7},{8,9},{9,10},{10,11},{11... | collective-permute-start | bytes 2359304 | tf_op jit(solution)/shard_map/ppermute | solution.py:763
  26.9 4.2 convolution_convert_fusion.1
  31.1 24.8 %collective-permute-done = bf16[4,128,768]{2,1,0:T(8,128)(2,1)S(1)} collective-permute-done((bf16[4,128,768]{2,1,0:T(8,128)(2,1)}, bf16[4,128,768]{2,1,0:T(8,128)(2,1)S(1)}, u32[]{:S(2)}, u32[]{:S(2)}) %collective-permute-start) | collective-permute-done | bytes 786464 | tf_op jit(solution)/shard_map/ppermute | solution.py:763
  60.1 2.8 convolution_convert_fusion.2
  62.9 15.9 %light_attention.1 = bf16[4,256,768]{2,1,0:T(8,128)(2,1)S(1)} custom-call(s32[2]{0:T(128)S(1)} %add_convert_fusion.4.ends_ref, bf16[4,256,2304]{2,1,0:T(8,128)(2,1)S(1)} %bitcast.194, bf16[4,256,1536]{2,1,0:T(8,128)(2,1)S(1)} %bitcast.196), custom_call_target="tpu_custom_call" | custom-call | flops 3221225472 | bytes 9437184 | tf_op jit(solution)/shard_map/light_attention/pallas_call | solution.py:156
  80.0 3.1 fusion.114
  83.0 10.4 %all-gather.2.cloned.1.call-done = bf16[4,512,768]{2,1,0:T(8,128)(2,1)} async-done(((bf16[4,64,768]{2,1,0:T(8,128)(2,1)}), bf16[4,512,768]{2,1,0:T(8,128)(2,1)}) %all-gather.2.cloned.1.call-update) | async-done | bytes 3145744 | tf_op jit(solution)/shard_map/all_gather | solution.py:775
  93.4 2.7 multiply_reduce_fusion
  97.6 5.2 %convolution_convert_fusion = bf16[2048,1536]{1,0:T(8,128)(2,1)S(1)} fusion(bf16[2048,768]{1,0:T(8,128)(2,1)S(1)} %fusion.1, bf16[768,1536]{1,0:T(8,128)(2,1)S(1)} %copy-done), kind=kOutput, calls=%fused_computation | convolution fusion | flops 4834983936 | bytes 11796480 | tf_op jit(solution)/shard_map/dot_general | solution.py:26
  102.9 4.1 heavy_attention.1
  115.8 3.8 fusion.115
  119.6 2.6 copy.39
  122.2 3.9 fusion.44
  126.1 2.8 collective-permute-done.2
  130.2 6.2 %fusion.9 = (bf16[1024,1024]{0,1:T(8,128)(2,1)S(1)}, bf16[1024,1024]{0,1:T(8,128)(2,1)S(1)}, bf16[1024,1024]{0,1:T(8,128)(2,1)}) fusion(f32[1024,1024]{0,1:T(8,128)S(1)} %copy-done.61, f32[1024,1024]{0,1:T(8,128)S(1)} %fusion.44, bf16[1024,768]{1,0:T(8,128)(2,1)S(1)} %copy-done.17, bf16[768,2048]{1,0:T(8,128)(2,1)S(1)} %copy-done.54), kind=kOutput, calls=%fused_computation.23 | convolution fusion | flops 1637875712 | bytes 17825792 | tf_op jit(solution)/shard_map/dot_general | solution.py:26
  136.4 2.4 pad_maximum_fusion
  142.5 2.8 copy.38
  145.3 3.3 fusion.52
  148.7 2.8 fusion.60
  151.5 5.3 %multiply_convert_fusion.6 = (bf16[768,1024]{1,0:T(8,128)(2,1)S(1)}, bf16[768,1024]{1,0:T(8,128)(2,1)S(1)}, bf16[768,1024]{1,0:T(8,128)(2,1)S(1)}) fusion(f32[768,1024]{1,0:T(8,128)S(1)} %fusion.60, f32[768,1024]{1,0:T(8,128)S(1)} %fusion.52, bf16[768,8192]{1,0:T(8,128)(2,1)} %param.31, s32[]{:T(128)S(6)} %select_n.10, bf16[2,768,768]{2,1,0:T(8,128)(2,1)S(1)} %copy-done.21), kind=kOutput, calls=%fused_computation.68 | convolution fusion | flops 1228406784 | bytes 13762564 | tf_op jit(solution)/shard_map/dot_general | solution.py:26
  156.8 2.8 fusion.50
  159.6 2.8 fusion.58
  162.5 2.9 fusion.51
  171.4 2.6 convolution_convert_fusion.7
  176.7 5.1 %convolution_convert_fusion.3 = bf16[768,2048]{1,0:T(8,128)(2,1)} fusion(bf16[1024,768]{1,0:T(8,128)(2,1)S(1)} %copy-done.18, bf16[1024,2048]{0,1:T(8,128)(2,1)S(1)} %copy-done.26), kind=kOutput, calls=%fused_computation.34 | convolution fusion | flops 3222798336 | bytes 8912896 | tf_op jit(solution)/shard_map/dot_general | solution.py:26
  181.7 3.0 convolution_convert_fusion.10
  184.7 5.5 %collective-permute-done.5 = bf16[2,192,768]{2,1,0:T(8,128)(2,1)S(1)} collective-permute-done((bf16[2,192,768]{2,1,0:T(8,128)(2,1)S(1)}, bf16[2,192,768]{2,1,0:T(8,128)(2,1)S(1)}, u32[]{:S(2)}, u32[]{:S(2)}) %collective-permute-start.5) | collective-permute-done | bytes 589856 | tf_op jit(solution)/shard_map/ppermute | solution.py:52
  191.2 2.5 fusion.22
  193.8 4.8 %multiply_reduce_fusion.1 = (bf16[768]{0:T(1024)(128)(2,1)S(1)}, f32[1024]{0:T(1024)S(1)}, f32[1024,768]{1,0:T(8,128)S(1)}) fusion(f32[1024,768]{1,0:T(8,128)S(1)} %copy-done.9, f32[1024]{0:T(1024)S(1)} %get-tuple-element.106, f32[768]{0:T(1024)S(1)} %convert_element_type.228, f32[768]{0:T(1024)S(1)} %copy-done.42, f32[1024]{0:T(1024)S(1)} %subtract_multiply_fusion, ...), kind=kOutput, calls=%fused_computation.56 | convolution fusion | flops 3228301568 | bytes 16797184 | tf_op jit(solution)/shard_map/dot_general | solution.py:26
  198.6 2.6 fusion.111
  201.2 2.5 convolution_convert_fusion.11
  203.7 2.6 convolution_convert_fusion.6
  208.8 8.7 %heavy_attention_back.1 = (bf16[4,64,768]{2,1,0:T(8,128)(2,1)S(1)}, bf16[4,512,1536]{2,1,0:T(8,128)(2,1)S(1)}) custom-call(bf16[4,64,768]{2,1,0:T(8,128)(2,1)S(1)} %bitcast.199, bf16[4,512,1536]{2,1,0:T(8,128)(2,1)S(1)} %bitcast.193, f32[4,1,512]{2,1,0:T(1,128)S(1)} %compare_convert_fusion.live_ref, bf16[4,64,768]{2,1,0:T(8,128)(2,1)S(1)} %bitcast.201), custom_call_target="tpu_custom_call" | custom-call | flops 4026531840 | bytes 14155776 | tf_op jit(solution)/shard_map/heavy_attention_back/pallas_call | solution.py:347
  217.5 6.4 %convolution_convert_fusion.4 = bf16[2048,768]{1,0:T(8,128)(2,1)} fusion(bf16[2048,1536]{1,0:T(8,128)(2,1)S(1)} %bitcast.202, bf16[768,1536]{1,0:T(8,128)(2,1)S(1)} %copy-done), kind=kOutput, calls=%fused_computation.35 | convolution fusion | flops 4833411072 | bytes 11796480 | tf_op jit(solution)/shard_map/dot_general | solution.py:26
  224.0 123.8 %reduce_gradients.2 = (f32[24,2048]{1,0:T(8,128)}, f32[32,768]{1,0:T(8,128)}, f32[24,768]{1,0:T(8,128)}, f32[24,768]{1,0:T(8,128)}, f32[24,8192]{1,0:T(8,128)}, ...) custom-call(bf16[2,2,4,2,24,2048]{5,4,3,2,1,0:T(8,128)(2,1)} %bitcast.217, ...), custom_call_target="tpu_custom_call" | custom-call | flops 11796480 | bytes 188743680 | tf_op jit(solution)/shard_map/reduce_gradients/pallas_call | solution.py:671
  347.7 5.3 %fusion.34 = bf16[1024,768]{1,0:T(8,128)(2,1)S(1)} fusion(bf16[1024,1536]{1,0:T(8,128)(2,1)} %bitcast.245, bf16[768,2304]{1,0:T(8,128)(2,1)} %param.22), kind=kOutput, calls=%fused_computation.87 | convolution fusion | flops 2416705536 | bytes 7077888 | tf_op jit(solution)/shard_map/dot_general | solution.py:26
  354.3 5.9 %collective-permute-start.6 = (bf16[4,128,768]{2,1,0:T(8,128)(2,1)}, bf16[4,128,768]{2,1,0:T(8,128)(2,1)}, u32[]{:S(2)}, u32[]{:S(2)}) collective-permute-start(bf16[4,128,768]{2,1,0:T(8,128)(2,1)} %get-tuple-element.92), channel_id=1, source_target_pairs={{0,1},{1,2},{2,3},{3,4},{4,5},{5,6},{6,7},{8,9},{9,10},{10,11},{11... | collective-permute-start | bytes 2359304 | tf_op jit(solution)/shard_map/ppermute | solution.py:956
  367.4 2.7 fusion.23
  370.1 4.8 %fusion.2 = bf16[768,1536]{1,0:T(8,128)(2,1)S(1)} fusion(f32[768,1536]{1,0:T(8,128)S(1)} %fusion.23, bf16[4,256,1536]{2,1,0:T(8,128)(2,1)S(1)} %copy-done.56, f32[4,256]{1,0:T(4,128)S(1)} %copy-done.46, f32[768]{0:T(1024)S(1)} %convert_element_type.209, bf16[4,128,768]{2,1,0:T(8,128)(2,1)} %collective-permute-done.1, bf16[4,128,768]{2,1,0:T(8,128)(2,1)S(1)} %copy-done.28), kind=kOutput, calls=%fused_computation.14 | convolution fusion | flops 2423783424 | bytes 11803648 | tf_op jit(solution)/shard_map/dot_general | solution.py:26
  378.2 5.6 %fusion.10 = f32[4,256,768]{2,1,0:T(8,128)} fusion(bf16[4,256,2304]{2,1,0:T(8,128)(2,1)S(1)} %bitcast.221, bf16[768,2304]{1,0:T(8,128)(2,1)S(1)} %copy-done.53), kind=kOutput, calls=%fused_computation.32 | convolution fusion | flops 3623878656 | bytes 11403264 | tf_op jit(solution)/shard_map/dot_general | solution.py:26
  383.9 6.6 %bitcast_convert_fusion = bf16[768,1536]{1,0:T(8,128)(2,1)} fusion(bf16[4,512,1536]{2,1,0:T(8,128)(2,1)S(1)} %bitcast.204, bf16[4,512,768]{2,1,0:T(8,128)(2,1)S(1)} %copy-done.13, f32[768]{0:T(1024)S(1)} %convert_element_type.209, f32[4,512]{1,0:T(4,128)S(1)} %copy-done.44), kind=kOutput, calls=%fused_computation.12 | convolution fusion | flops 4839309312 | bytes 11807744 | tf_op jit(solution)/shard_map/dot_general | solution.py:26
  391.1 7.0 %add_convert_fusion = bf16[1024,768]{1,0:T(8,128)(2,1)} fusion(f32[1024,768]{1,0:T(8,128)} %get-tuple-element.110, f32[1024,768]{1,0:T(8,128)} %copy-done.8, bf16[1024,1024]{0,1:T(8,128)(2,1)} %get-tuple-element.51, bf16[1024,768]{1,0:T(8,128)(2,1)} %param.30, f32[1024]{0:T(1024)S(1)} %add_divide_fusion), kind=kOutput, calls=%fused_computation.66 | convolution fusion | flops 1613758464 | bytes 11538432 | tf_op jit(solution)/shard_map/dot_general | solution.py:26
  398.1 7.1 %multiply_reduce_fusion.2 = (bf16[768]{0:T(1024)(128)(2,1)S(1)}, f32[4,256]{1,0:T(4,128)S(1)}, f32[4,256,768]{2,1,0:T(8,128)}) fusion(bf16[4,256,768]{2,1,0:T(8,128)(2,1)} %param.19, f32[4,256]{1,0:T(4,128)S(1)} %copy-done.37, f32[768]{0:T(1024)S(1)} %convert_element_type.209, bf16[4,128,768]{2,1,0:T(8,128)(2,1)} %collective-permute-done.7, ...), kind=kOutput, calls=%fused_computation.57 | convolution fusion | flops 111737088 | bytes 12989952 | tf_op jit(solution)/shard_map/pkt,pkd->ptd/dot_general | solution.py:972
  406.0 49.8 %reduce_gradients.3 = (f32[24,2304]{1,0:T(8,128)}, f32[24,768]{1,0:T(8,128)}, f32[24,1536]{1,0:T(8,128)}, f32[8,256]{1,0:T(8,128)}) custom-call(bf16[2,2,4,2,24,2304]{5,4,3,2,1,0:T(8,128)(2,1)} %pad_maximum_fusion.1.refs_0_, bf16[2,2,4,2,24,768]{5,4,3,2,1,0:T(8,128)(2,1)} %bitcast.232, bf16[2,2,4,2,24,1536]{5,4,3,2,1,0:T(8,128)(2,1)} %bitcast.218, ...), custom_call_target="tpu_custom_call" | custom-call | flops 7208960 | bytes 115343360 | tf_op jit(solution)/shard_map/reduce_gradients/pallas_call | solution.py:671
  455.9 2.8 copy_outputs.1
  460.0 4.9 %subtract_add_fusion = f32[4,256,768]{2,1,0:T(8,128)} fusion(f32[4,256,768]{2,1,0:T(8,128)} %bitcast.210, bf16[4,256,768]{2,1,0:T(8,128)(2,1)} %param.19, f32[4,256,768]{2,1,0:T(8,128)} %get-tuple-element.112, f32[4,256]{1,0:T(4,128)S(1)} %broadcast_multiply_fusion.1, f32[4,256]{1,0:T(4,128)S(1)} %copy-done.41, f32[768]{0:T(1024)S(1)} %convert_element_type.209, ...), kind=kLoop, calls=%fused_computation.61 | loop fusion | flops 5505024 | bytes 11025408 | tf_op jit(solution)/shard_map/add | solution.py:976
  (220 shorter events, 56.1 us)
Async XLA Ops:
  7.2 90.4 %copy-start = (bf16[768,1536]{1,0:T(8,128)(2,1)S(1)}, bf16[768,1536]{1,0:T(8,128)(2,1)}, u32[]{:S(2)}) copy-start(bf16[768,1536]{1,0:T(8,128)(2,1)} %param.25) | copy-start | bytes 7077892
  7.2 11.9 %copy-start.48 = (bf16[768]{0:T(1024)(128)(2,1)S(1)}, bf16[768]{0:T(1024)(128)(2,1)}, u32[]{:S(2)}) copy-start(bf16[768]{0:T(1024)(128)(2,1)} %param.21) | copy-start | bytes 4612
  7.2 11.9 %copy-start.49 = (bf16[768]{0:T(1024)(128)(2,1)S(1)}, bf16[768]{0:T(1024)(128)(2,1)}, u32[]{:S(2)}) copy-start(bf16[768]{0:T(1024)(128)(2,1)} %param.27) | copy-start | bytes 4612
  7.2 11.9 %copy-start.50 = (bf16[768]{0:T(1024)(128)(2,1)S(1)}, bf16[768]{0:T(1024)(128)(2,1)}, u32[]{:S(2)}) copy-start(bf16[768]{0:T(1024)(128)(2,1)} %param.28) | copy-start | bytes 4612
  7.2 12.5 %copy-start.47 = (s32[4,256]{1,0:T(4,128)S(1)}, s32[4,256]{1,0:T(4,128)}, u32[]{:S(2)}) copy-start(s32[4,256]{1,0:T(4,128)} %param.37) | copy-start | bytes 12292
  7.2 13.2 %copy-start.51 = (s32[4,8]{1,0:T(4,128)S(1)}, s32[4,8]{1,0:T(4,128)}, u32[]{:S(2)}) copy-start(s32[4,8]{1,0:T(4,128)} %param.36) | copy-start | bytes 388
  7.2 15.4 %copy-start.60 = (s32[4,1]{0,1:T(1,128)S(1)}, s32[4,1]{0,1:T(1,128)}, u32[]{:S(2)}) copy-start(s32[4,1]{0,1:T(1,128)} %param.34) | copy-start | bytes 52
  7.3 86.2 %all-gather.2.cloned.1.call-start = ((), (), s32[]{:S(2)}) async-start(), calls=%async_computation.1 | async-start | bytes 3538944 | tf_op jit(solution)/shard_map/all_gather | solution.py:775
  10.1 388.0 %reduce-scatter.2.cloned.1.call-start = ((), (), s32[]{:S(2)}) async-start(), calls=%async_computation.2 | async-start | bytes 3538944 | tf_op jit(solution)/shard_map/reduce_scatter | solution.py:915
  12.7 13.2 %copy-start.39 = (s32[4,64]{1,0:T(4,128)S(1)}, s32[4,64]{1,0:T(4,128)}, u32[]{:S(2)}) copy-start(s32[4,64]{1,0:T(4,128)} %param.33) | copy-start | bytes 3076
  12.7 43.2 %collective-permute-start = (bf16[4,128,768]{2,1,0:T(8,128)(2,1)}, bf16[4,128,768]{2,1,0:T(8,128)(2,1)S(1)}, u32[]{:S(2)}, u32[]{:S(2)}) collective-permute-start(bf16[4,128,768]{2,1,0:T(8,128)(2,1)} %get-tuple-element.94), channel_id=1, source_target_pairs={{0,1},{1,2},{2,3},{3,4},{4,5},{5,6},{6,7},{8,9},{9,10},{10,11},{11... | collective-permute-start | bytes 2359304 | tf_op jit(solution)/shard_map/ppermute | solution.py:763
  17.8 38.1 %collective-permute-start.1 = (bf16[4,128,768]{2,1,0:T(8,128)(2,1)}, bf16[4,128,768]{2,1,0:T(8,128)(2,1)}, u32[]{:S(2)}, u32[]{:S(2)}) collective-permute-start(bf16[4,128,768]{2,1,0:T(8,128)(2,1)} %get-tuple-element.95), channel_id=1, source_target_pairs={{1,0},{2,1},{3,2},{4,3},{5,4},{6,5},{7,6},{9,8},{10,9},{11,10},{12... | collective-permute-start | bytes 2359304 | tf_op jit(solution)/shard_map/ppermute | solution.py:766
  20.7 5.7 %copy-start.24 = (bf16[768,768]{1,0:T(8,128)(2,1)S(1)}, bf16[768,768]{1,0:T(8,128)(2,1)}, u32[]{:S(2)}) copy-start(bf16[768,768]{1,0:T(8,128)(2,1)} %param.24) | copy-start | bytes 3538948
  25.9 5.2 %copy-start.10 = (bf16[4,256,768]{2,1,0:T(8,128)(2,1)}, bf16[4,256,768]{2,1,0:T(8,128)(2,1)S(1)}, u32[]{:S(2)}) copy-start(bf16[4,256,768]{2,1,0:T(8,128)(2,1)S(1)} %multiply_convert_fusion.8) | copy-start | bytes 4718596
  26.4 4.8 %copy-start.33 = (bf16[4,64,768]{2,1,0:T(8,128)(2,1)}, bf16[4,64,768]{2,1,0:T(8,128)(2,1)S(1)}, u32[]{:S(2)}) copy-start(bf16[4,64,768]{2,1,0:T(8,128)(2,1)S(1)} %convolution_convert_fusion.18) | copy-start | bytes 1179652
  31.1 31.8 %copy-start.2 = (bf16[1024,2304]{1,0:T(8,128)(2,1)}, bf16[1024,2304]{1,0:T(8,128)(2,1)S(1)}, u32[]{:S(2)}) copy-start(bf16[1024,2304]{1,0:T(8,128)(2,1)S(1)} %convolution_convert_fusion.1) | copy-start | bytes 14155780
  62.9 15.9 %copy-start.3 = (bf16[1024,1536]{1,0:T(8,128)(2,1)}, bf16[1024,1536]{1,0:T(8,128)(2,1)S(1)}, u32[]{:S(2)}) copy-start(bf16[1024,1536]{1,0:T(8,128)(2,1)S(1)} %convolution_convert_fusion.2) | copy-start | bytes 9437188
  62.9 17.0 %copy-start.58 = (bf16[768,768]{1,0:T(8,128)(2,1)S(1)}, bf16[768,768]{1,0:T(8,128)(2,1)}, u32[]{:S(2)}) copy-start(bf16[768,768]{1,0:T(8,128)(2,1)} %param.23) | copy-start | bytes 3538948
  102.8 4.9 %copy-start.7 = (bf16[4,256,768]{2,1,0:T(8,128)(2,1)S(1)}, bf16[4,256,768]{2,1,0:T(8,128)(2,1)}, u32[]{:S(2)}) copy-start(bf16[4,256,768]{2,1,0:T(8,128)(2,1)} %param.19) | copy-start | bytes 4718596
  102.8 4.9 %copy-start.22 = (bf16[768,768]{1,0:T(8,128)(2,1)S(1)}, bf16[768,768]{1,0:T(8,128)(2,1)}, u32[]{:S(2)}) copy-start(bf16[768,768]{1,0:T(8,128)(2,1)} %param.26) | copy-start | bytes 3538948
  102.9 5.0 %copy-start.29 = (f32[1024,768]{1,0:T(8,128)S(1)}, f32[1024,768]{1,0:T(8,128)}, u32[]{:S(2)}) copy-start(f32[1024,768]{1,0:T(8,128)} %fusion.114) | copy-start | bytes 9437188
  110.2 5.6 %copy-start.57 = (bf16[1024,768]{1,0:T(8,128)(2,1)S(1)}, bf16[1024,768]{1,0:T(8,128)(2,1)}, u32[]{:S(2)}) copy-start(bf16[1024,768]{1,0:T(8,128)(2,1)} %param.30) | copy-start | bytes 4718596
  114.4 14.5 %collective-permute-start.2 = (bf16[2,192,768]{2,1,0:T(8,128)(2,1)}, bf16[2,192,768]{2,1,0:T(8,128)(2,1)}, u32[]{:S(2)}, u32[]{:S(2)}) collective-permute-start(bf16[2,192,768]{2,1,0:T(8,128)(2,1)} %pad_maximum_fusion.6), channel_id=1, source_target_pairs={{0,16},{8,24},{16,0},{24,8},{1,17},{9,25},{17,1},{25,9},{2,18},{10... | collective-permute-start | bytes 1769480 | tf_op jit(solution)/shard_map/ppermute | solution.py:52
  122.2 6.7 %copy-start.31 = (bf16[1,192,768]{2,1,0:T(8,128)(2,1)S(1)}, bf16[1,192,768]{2,1,0:T(8,128)(2,1)}, u32[]{:S(2)}) copy-start(bf16[1,192,768]{2,1,0:T(8,128)(2,1)} %copy-done.30) | copy-start | bytes 884740
  122.2 7.9 %copy-start.17 = (bf16[1024,768]{1,0:T(8,128)(2,1)S(1)}, bf16[1024,768]{1,0:T(8,128)(2,1)}, u32[]{:S(2)}) copy-start(bf16[1024,768]{1,0:T(8,128)(2,1)} %copy-done.16) | copy-start | bytes 4718596
  122.2 8.0 %copy-start.54 = (bf16[768,2048]{1,0:T(8,128)(2,1)S(1)}, bf16[768,2048]{1,0:T(8,128)(2,1)}, u32[]{:S(2)}) copy-start(bf16[768,2048]{1,0:T(8,128)(2,1)} %param.29) | copy-start | bytes 9437188
  122.2 8.0 %copy-start.61 = (f32[1024,1024]{0,1:T(8,128)S(1)}, f32[1024,1024]{0,1:T(8,128)}, u32[]{:S(2)}) copy-start(f32[1024,1024]{0,1:T(8,128)} %fusion.115) | copy-start | bytes 12582916
  130.1 8.7 %collective-permute-start.3 = (bf16[2,384,768]{2,1,0:T(8,128)(2,1)S(1)}, bf16[2,384,768]{2,1,0:T(8,128)(2,1)S(1)}, u32[]{:S(2)}, u32[]{:S(2)}) collective-permute-start(bf16[2,384,768]{2,1,0:T(8,128)(2,1)S(1)} %pad_maximum_fusion.5), channel_id=1, source_target_pairs={{0,8},{8,0},{16,24},{24,16},{1,9},{9,1},{17,25},{25,17},{2,10},{10... | collective-permute-start | bytes 3538952 | tf_op jit(solution)/shard_map/ppermute | solution.py:52
  165.4 8.6 %collective-permute-start.4 = (bf16[2,384,768]{2,1,0:T(8,128)(2,1)S(1)}, bf16[2,384,768]{2,1,0:T(8,128)(2,1)S(1)}, u32[]{:S(2)}, u32[]{:S(2)}) collective-permute-start(bf16[2,384,768]{2,1,0:T(8,128)(2,1)S(1)} %pad_maximum_fusion.4), channel_id=1, source_target_pairs={{0,8},{8,0},{16,24},{24,16},{1,9},{9,1},{17,25},{25,17},{2,10},{10... | collective-permute-start | bytes 3538952 | tf_op jit(solution)/shard_map/ppermute | solution.py:52
  174.4 7.3 %copy-start.15 = (bf16[4,256,768]{2,1,0:T(8,128)(2,1)S(1)}, bf16[4,256,768]{2,1,0:T(8,128)(2,1)}, u32[]{:S(2)}) copy-start(bf16[4,256,768]{2,1,0:T(8,128)(2,1)} %param.20) | copy-start | bytes 4718596
  174.4 7.3 %copy-start.62 = (bf16[1024,1024]{0,1:T(8,128)(2,1)S(1)}, bf16[1024,1024]{0,1:T(8,128)(2,1)}, u32[]{:S(2)}) copy-start(bf16[1024,1024]{0,1:T(8,128)(2,1)} %get-tuple-element.51) | copy-start | bytes 6291460
  174.4 15.8 %collective-permute-start.5 = (bf16[2,192,768]{2,1,0:T(8,128)(2,1)S(1)}, bf16[2,192,768]{2,1,0:T(8,128)(2,1)S(1)}, u32[]{:S(2)}, u32[]{:S(2)}) collective-permute-start(bf16[2,192,768]{2,1,0:T(8,128)(2,1)S(1)} %split.15), channel_id=1, source_target_pairs={{0,16},{8,24},{16,0},{24,8},{1,17},{9,25},{17,1},{25,9},{2,18},{10... | collective-permute-start | bytes 1769480 | tf_op jit(solution)/shard_map/ppermute | solution.py:52
  201.2 7.5 %slice-start = ((s8[6291456]{0:T(1024)(128)(4,1)}), s8[4194304]{0:T(1024)(128)(4,1)S(1)}, s32[]{:S(2)}) async-start(s8[6291456]{0:T(1024)(128)(4,1)} %bitcast.191), calls=%async_computation.3 | async-start | bytes 8388608
  203.7 5.1 %slice-start.1 = ((s8[6291456]{0:T(1024)(128)(4,1)}), s8[2097152]{0:T(1024)(128)(4,1)S(1)}, s32[]{:S(2)}) async-start(s8[6291456]{0:T(1024)(128)(4,1)} %bitcast.191), calls=%async_computation.4 | async-start | bytes 4194304
  217.5 6.5 %copy-start.4 = (bf16[4,512,1536]{2,1,0:T(8,128)(2,1)}, bf16[4,512,1536]{2,1,0:T(8,128)(2,1)S(1)}, u32[]{:S(2)}) copy-start(bf16[4,512,1536]{2,1,0:T(8,128)(2,1)S(1)} %get-tuple-element.52) | copy-start | bytes 18874372
  353.0 8.5 %copy-start.34 = (bf16[4,64,768]{2,1,0:T(8,128)(2,1)S(1)}, bf16[4,64,768]{2,1,0:T(8,128)(2,1)}, u32[]{:S(2)}) copy-start(bf16[4,64,768]{2,1,0:T(8,128)(2,1)} %copy-done.33) | copy-start | bytes 1179652
  353.0 10.0 %copy-start.25 = (bf16[768,768]{1,0:T(8,128)(2,1)S(1)}, bf16[768,768]{1,0:T(8,128)(2,1)}, u32[]{:S(2)}) copy-start(bf16[768,768]{1,0:T(8,128)(2,1)} %param.24) | copy-start | bytes 3538948
  353.0 12.8 %slice-start.4 = ((s8[4718592]{0:T(1024)(128)(4,1)}), s8[4194304]{0:T(1024)(128)(4,1)S(1)}, s32[]{:S(2)}) async-start(s8[4718592]{0:T(1024)(128)(4,1)} %bitcast.220), calls=%async_computation.7 | async-start | bytes 8388608
  354.3 43.7 %collective-permute-start.6 = (bf16[4,128,768]{2,1,0:T(8,128)(2,1)}, bf16[4,128,768]{2,1,0:T(8,128)(2,1)}, u32[]{:S(2)}, u32[]{:S(2)}) collective-permute-start(bf16[4,128,768]{2,1,0:T(8,128)(2,1)} %get-tuple-element.92), channel_id=1, source_target_pairs={{0,1},{1,2},{2,3},{3,4},{4,5},{5,6},{6,7},{8,9},{9,10},{10,11},{11... | collective-permute-start | bytes 2359304 | tf_op jit(solution)/shard_map/ppermute | solution.py:956
  360.2 37.9 %collective-permute-start.7 = (bf16[4,128,768]{2,1,0:T(8,128)(2,1)}, bf16[4,128,768]{2,1,0:T(8,128)(2,1)}, u32[]{:S(2)}, u32[]{:S(2)}) collective-permute-start(bf16[4,128,768]{2,1,0:T(8,128)(2,1)} %get-tuple-element.93), channel_id=1, source_target_pairs={{1,0},{2,1},{3,2},{4,3},{5,4},{6,5},{7,6},{9,8},{10,9},{11,10},{12... | collective-permute-start | bytes 2359304 | tf_op jit(solution)/shard_map/ppermute | solution.py:953
  374.9 8.9 %slice-start.2 = ((s8[6291456]{0:T(1024)(128)(4,1)}), s8[2097152]{0:T(1024)(128)(4,1)S(1)}, s32[]{:S(2)}) async-start(s8[6291456]{0:T(1024)(128)(4,1)} %bitcast.203), calls=%async_computation.5 | async-start | bytes 4194304
  378.2 5.6 %slice-start.3 = ((s8[6291456]{0:T(1024)(128)(4,1)}), s8[4194304]{0:T(1024)(128)(4,1)S(1)}, s32[]{:S(2)}) async-start(s8[6291456]{0:T(1024)(128)(4,1)} %bitcast.203), calls=%async_computation.6 | async-start | bytes 8388608
  378.2 5.6 %copy-start.13 = (bf16[4,512,768]{2,1,0:T(8,128)(2,1)S(1)}, bf16[4,512,768]{2,1,0:T(8,128)(2,1)}, u32[]{:S(2)}) copy-start(bf16[4,512,768]{2,1,0:T(8,128)(2,1)} %all-gather.2.cloned.1.call-done) | copy-start | bytes 9437188
  378.2 5.6 %copy-start.44 = (f32[4,512]{1,0:T(4,128)S(1)}, f32[4,512]{1,0:T(4,128)}, u32[]{:S(2)}) copy-start(f32[4,512]{1,0:T(4,128)} %get-tuple-element.99) | copy-start | bytes 24580
  383.9 6.6 %copy-start.19 = (bf16[1024,768]{1,0:T(8,128)(2,1)S(1)}, bf16[1024,768]{1,0:T(8,128)(2,1)}, u32[]{:S(2)}) copy-start(bf16[1024,768]{1,0:T(8,128)(2,1)} %copy-done.16) | copy-start | bytes 4718596
  391.0 7.0 %copy-start.37 = (f32[4,256]{1,0:T(4,128)S(1)}, f32[4,256]{1,0:T(4,128)}, u32[]{:S(2)}) copy-start(f32[4,256]{1,0:T(4,128)} %copy-done.36) | copy-start | bytes 12292
  391.0 7.0 %copy-start.43 = (s32[4,64]{1,0:T(4,128)S(1)}, s32[4,64]{1,0:T(4,128)}, u32[]{:S(2)}) copy-start(s32[4,64]{1,0:T(4,128)} %param.35) | copy-start | bytes 3076
  406.0 54.0 %copy-start.41 = (f32[4,256]{1,0:T(4,128)S(1)}, f32[4,256]{1,0:T(4,128)}, u32[]{:S(2)}) copy-start(f32[4,256]{1,0:T(4,128)} %get-tuple-element.103) | copy-start | bytes 12292
  (31 other events, 79.2 us)
Sparse Core Ops, SparseCore 0:
  10.9 82.5 all-gather.1
  224.1 118.2 reduce-scatter.1

commit v3 on v2

--- a/solution.py
+++ b/solution.py
@@ -82,10 +82,6 @@
     weighted = grad * gain
     inner = jnp.mean(weighted * values, axis=-1, keepdims=True)
     return scale * weighted - values * (scale * scale * scale) * inner
-
-
-def glu_rows(gate, up):
-    return jax.nn.gelu(gate) * up
 
 
 def head_windows():
@@ -371,238 +367,534 @@
     )(query, pairs, live, grad)
 
 
-def reduce_kernel(jobs, arrays, sizes, work, *refs):
-    n_x, n_y = sizes
-    n_dp = n_x * CORES
-    given, made = (3, 2) if work else (0, 0)
-    sources, outs = refs[:arrays], refs[arrays + given : 2 * arrays + given]
-    operands = refs[arrays : arrays + given] + refs[2 * arrays + given :][:made]
-    scratch = list(refs[2 * arrays + given + made :])
-    held = []
-    for job in jobs:
-        names = SCRATCH[job[1]]
-        held.append(dict(zip(names, scratch[: len(names)])))
-        del scratch[: len(names)]
+def glu_and_pull(gate, up, grad):
+    slope = 0.7978845608028654
+    square = gate * gate
+    curve = jnp.tanh(gate * (slope + (slope * 0.044715) * square))
+    half = 0.5 + 0.5 * curve
+    gelu = gate * half
+    bend = (0.5 * gate) * (1.0 - curve * curve) * (slope + (3 * slope * 0.044715) * square)
+    return gelu * up, grad * up * (half + bend), grad * gelu
+
+
+def feed_kernel(
+    n_y,
+    normed,
+    cot,
+    own_rows,
+    gates,
+    down,
+    gates_heavy,
+    down_heavy,
+    act_out,
+    pre_out,
+    feed_out,
+    grad_out,
+    back_out,
+    rows_out,
+    heavy_act_out,
+    heavy_pre_out,
+    wide,
+    tall,
+    rows,
+    part,
+    from_core,
+    to_y,
+    from_y,
+    weight_sem,
+    rows_rsem,
+    rows_ssem,
+    core_rsem,
+    core_ssem,
+    y_rsem,
+    y_ssem,
+):
+    dp, seq = lax.axis_index("dp"), lax.axis_index("seq")
+    c, y = dp % CORES, seq % n_y
+    me = c * n_y + y
+    to_core, to_beside = (dp + 1 - 2 * c, seq), (dp, seq + 1 - 2 * y)
+    share = tall.shape[0]
+    total = gates_heavy.shape[1] // 2
+    slots = rows.shape[2]
+    loads = [
+        pltpu.make_async_copy(
+            gates_heavy.at[:, pl.ds(pl.multiple_of(i * total + me * share, share), share)],
+            wide.at[i],
+            weight_sem.at[i],
+        )
+        for i in range(2)
+    ]
+    loads.append(
+        pltpu.make_async_copy(
+            down_heavy.at[pl.ds(pl.multiple_of(me * share, share), share)], tall, weight_sem.at[2]
+        )
+    )
+    for load in loads:
+        load.start()
+    barrier = pltpu.get_barrier_semaphore()
+    for peer in (to_core, to_beside):
+        pl.semaphore_signal(barrier, inc=1, device_id=peer, device_id_type=MESH)
+    pl.semaphore_wait(barrier, 2)
+
+    def copy(src, dst, ssem, rsem, peer):
+        return pltpu.make_async_remote_copy(
+            src_ref=src,
+            dst_ref=dst,
+            send_sem=ssem,
+            recv_sem=rsem,
+            device_id=peer,
+            device_id_type=MESH,
+        )
+
+    def rows_copy(slot, i, peer):
+        return copy(rows.at[slot], rows.at[slot], rows_ssem.at[i], rows_rsem.at[slot], peer)
+
+    rows[me] = own_rows[...]
+    rows_copy(me, 0, to_beside).start()
+    rows_copy(me, 1, to_core).start()
+    beside, diagonal, other = c * n_y + 1 - y, (1 - c) * n_y + 1 - y, (1 - c) * n_y + y
+    hidden = down.shape[0]
+    step = 256
+
+    @pl.loop(0, normed.shape[0] // step)
+    def _(t):
+        at = pl.ds(pl.multiple_of(t * step, step), step)
+        gate = mm(normed[at], gates[:, :hidden])
+        up = mm(normed[at], gates[:, hidden:])
+        act, grad_gate, grad_up = glu_and_pull(gate, up, mm_nt(cot[at], down[...]))
+        act = act.astype(bf16)
+        grad_gate = grad_gate.astype(bf16)
+        grad_up = grad_up.astype(bf16)
+        act_out[at] = act
+        pre_out[at, :hidden] = grad_gate
+        pre_out[at, hidden:] = grad_up
+        feed_out[at] = mm(act, down[...])
+        grad_out[at] = mm_nt(grad_gate, gates[:, :hidden]) + mm_nt(grad_up, gates[:, hidden:])
+
+    for load in loads:
+        load.wait()
+    rows_copy(beside, 2, to_core).wait_recv()
+    rows_copy(beside, 2, to_core).start()
+
+    @pl.loop(0, 4)
+    def _(i):
+        first, second, third = i == 0, i == 1, i == 2
+        slot = jnp.where(
+            first, me, jnp.where(second, diagonal, jnp.where(third, beside, other))
+        )
+
+        @pl.when(second)
+        def _():
+            rows_copy(diagonal, 0, to_core).wait_recv()
+
+        @pl.when(i == 3)
+        def _():
+            rows_copy(other, 0, to_core).wait_recv()
+
+        value, grad = rows[slot, 0], rows[slot, 1]
+        gate, up = mm(value, wide[0]), mm(value, wide[1])
+        act, grad_gate, grad_up = glu_and_pull(gate, up, mm_nt(grad, tall[...]))
+        act = act.astype(bf16)
+        grad_gate = grad_gate.astype(bf16)
+        grad_up = grad_up.astype(bf16)
+        heavy_act_out[slot] = act
+        heavy_pre_out[slot, :, :share] = grad_gate
+        heavy_pre_out[slot, :, share:] = grad_up
+        part[i, 0] = mm(act, tall[...]).astype(bf16)
+        part[i, 1] = (mm_nt(grad_gate, wide[0]) + mm_nt(grad_up, wide[1])).astype(bf16)
+
+        @pl.when(second)
+        def _():
+            copy(part.at[1], from_core.at[0], core_ssem.at[0], core_rsem.at[0], to_core).start()
+
+        @pl.when(third)
+        def _():
+            copy(part.at[1], from_core.at[0], core_ssem.at[0], core_rsem.at[0], to_core).wait_recv()
+            to_y[...] = part[2] + from_core[0]
+            copy(to_y, from_y, y_ssem, y_rsem, to_beside).start()
+
+        @pl.when(i == 3)
+        def _():
+            copy(part.at[3], from_core.at[1], core_ssem.at[1], core_rsem.at[1], to_core).start()
+
+    rows_out[...] = rows[...]
+    copy(part.at[3], from_core.at[1], core_ssem.at[1], core_rsem.at[1], to_core).wait()
+    copy(to_y, from_y, y_ssem, y_rsem, to_beside).wait()
+    sums = part[0].astype(f32) + from_core[1].astype(f32) + from_y[...].astype(f32)
+    back_out[...] = sums.astype(bf16)
+    copy(part.at[1], from_core.at[0], core_ssem.at[0], core_rsem.at[0], to_core).wait_send()
+    for i, slot in enumerate((me, me, beside)):
+        rows_copy(slot, i, to_core).wait_send()
+
+
+def feed_forward(normed, cot, own_rows, gates, down, gates_heavy, down_heavy, n_y):
+    count, hidden = normed.shape[0], down.shape[0]
+    slots = own_rows.shape[1]
+    share = down_heavy.shape[0] // 4
+    here, anywhere = pl.BlockSpec(memory_space=pltpu.VMEM), pl.BlockSpec(memory_space=pl.ANY)
+    pair = (2, slots, D)
+    return pl.pallas_call(
+        functools.partial(feed_kernel, n_y),
+        out_shape=[
+            jax.ShapeDtypeStruct((count, hidden), bf16),
+            jax.ShapeDtypeStruct((count, 2 * hidden), bf16),
+            jax.ShapeDtypeStruct((count, D), f32),
+            jax.ShapeDtypeStruct((count, D), f32),
+            jax.ShapeDtypeStruct(pair, bf16),
+            jax.ShapeDtypeStruct((4,) + pair, bf16),
+            jax.ShapeDtypeStruct((4, slots, share), bf16),
+            jax.ShapeDtypeStruct((4, slots, 2 * share), bf16),
+        ],
+        in_specs=[here] * 5 + [anywhere] * 2,
+        out_specs=[here] * 8,
+        scratch_shapes=[
+            pltpu.VMEM((2, D, share), bf16),
+            pltpu.VMEM((share, D), bf16),
+            pltpu.VMEM((4,) + pair, bf16),
+            pltpu.VMEM((4,) + pair, bf16),
+            pltpu.VMEM((2,) + pair, bf16),
+            pltpu.VMEM(pair, bf16),
+            pltpu.VMEM(pair, bf16),
+            pltpu.SemaphoreType.DMA((3,)),
+            pltpu.SemaphoreType.DMA((4,)),
+            pltpu.SemaphoreType.DMA((3,)),
+            pltpu.SemaphoreType.DMA((2,)),
+            pltpu.SemaphoreType.DMA((2,)),
+            pltpu.SemaphoreType.DMA,
+            pltpu.SemaphoreType.DMA,
+        ],
+        compiler_params=pltpu.CompilerParams(
+            collective_id=2, has_side_effects=True, vmem_limit_bytes=60 << 20
+        ),
+        cost_estimate=pl.CostEstimate(
+            flops=12 * count * D * hidden + 48 * slots * D * share,
+            bytes_accessed=30 << 20,
+            transcendentals=count * hidden + 4 * slots * share,
+        ),
+        name="feed_forward",
+    )(normed, cot, own_rows, gates, down, gates_heavy, down_heavy)
+
+
+def reduce_kernel(jobs, counts, n_y, *refs):
+    n_sources, n_outs, light = counts
+    refs = list(refs)
+
+    def take(count):
+        taken = refs[:count]
+        del refs[:count]
+        return taken
+
+    sources = take(n_sources)
+    given = take(4 if light else 0)
+    outs = take(n_outs)
+    made = take(3 if light else 0)
+    held = [dict(zip(SCRATCH[job[0]], take(len(SCRATCH[job[0]])))) for job in jobs]
+    kinds = [job[0] for job in jobs]
     dp, seq = lax.axis_index("dp"), lax.axis_index("seq")
     x, c = dp // CORES, dp % CORES
     z, y = seq // n_y, seq % n_y
-
-    def to_dp(by):
-        return (lax.rem(dp + by, n_dp), seq)
-
-    def to_core():
-        return (x * CORES + (1 - c), seq)
-
-    def to_x(by):
-        return (((x + by) % n_x) * CORES + c, seq)
-
-    def to_y(by):
-        return (dp, z * n_y + (y + by) % n_y)
-
-    def to_z(by):
-        return (dp, ((z + by) % DEPTH) * n_y + y)
-
-    peers = [to_dp(by) for by in range(1, n_dp)]
-    peers += [to_y(by) for by in range(1, n_y)]
-    peers += [to_z(by) for by in range(1, DEPTH)]
+    z_high, z_low = z // 2, z % 2
+    group = c * n_y + y
+
+    def device(x=x, c=c, z=z, y=y):
+        return (x * CORES + c, z * n_y + y)
+
+    to = {
+        "core": device(c=1 - c),
+        "x": device(x=1 - x),
+        "y": device(y=1 - y),
+        "low": device(z=z_high * 2 + 1 - z_low),
+        "high": device(z=(1 - z_high) * 2 + z_low),
+    }
+    owner = (group, x * DEPTH + z)
+    origin = device(x=seq // DEPTH, c=dp // n_y, z=seq % DEPTH, y=dp % n_y)
+    moved = jnp.logical_or(owner[0] != dp, owner[1] != seq)
+
     barrier = pltpu.get_barrier_semaphore()
-    for peer in peers:
+
+    def greet(peer):
         pl.semaphore_signal(barrier, inc=1, device_id=peer, device_id_type=MESH)
-    pl.semaphore_wait(barrier, len(peers))
+
+    for peer in to.values():
+        greet(peer)
+    expected = len(to)
+    if "gates" in kinds:
+        greet(device(c=1 - c, y=1 - y))
+        expected += 1
+    pairs = []
+    if "down" in kinds:
+        pairs += [(moved, owner), (moved, origin)]
+    if light:
+        pairs += [(seq > 0, (dp, seq - 1)), (seq < DEPTH * n_y - 1, (dp, seq + 1))]
+    for present, peer in pairs:
+
+        @pl.when(present)
+        def _():
+            greet(peer)
+
+    for present, _ in pairs:
+        expected = expected + jnp.where(present, 1, 0)
+    pl.semaphore_wait(barrier, expected)
 
     def copy(src, dst, a, stage, k, peer):
-        h = held[a]
         return pltpu.make_async_remote_copy(
             src_ref=src,
             dst_ref=dst,
-            send_sem=h["ssem"].at[stage],
-            recv_sem=h["rsem"].at[stage, k],
+            send_sem=held[a]["ssem"].at[stage],
+            recv_sem=held[a]["rsem"].at[stage, k],
             device_id=peer,
             device_id_type=MESH,
         )
 
-    def arrived(name, a, stage, k):
+    def send(src, name, k, a, place=None, slot=None):
+        dst = held[a][name].at[k] if slot is None else held[a][name].at[k, slot]
+        copy(src, dst, a, STAGES[name], k, place).start()
+
+    def arrived(name, a, k):
         buffer = held[a][name].at[k]
-        copy(buffer, buffer, a, stage, k, to_core()).wait_recv()
+        copy(buffer, buffer, a, STAGES[name], k, to["core"]).wait_recv()
 
     def columns(a, k):
-        _, _, start, width, _ = jobs[a]
+        start, width = jobs[a][2:4]
         return pl.ds(start + k * width, width)
 
-    def source(a):
-        return sources[jobs[a][0]]
-
     def local(a, k):
-        h, cols = held[a], columns(a, k)
-        whole = source(a)
-        part = whole.at[:, c, :, :, :, cols] if "core" in h else whole.at[..., cols]
-        return pltpu.make_async_copy(part, h["own"].at[k], h["lsem"].at[k])
-
-    def add_all(target, pairs):
-        for at, addend, place in pairs:
-            target[at] = target[at] + addend[place]
+        whole, cols = sources[jobs[a][1]], columns(a, k)
+        if kinds[a] in ("xy", "yx"):
+            part = whole.at[:, c, :, :, :, cols]
+        else:
+            part = whole.at[x, :, :, :, :, cols]
+        return pltpu.make_async_copy(part, held[a]["own"].at[k], held[a]["lsem"].at[k])
 
     def begin(a, k):
-        h = held[a]
+        whole, cols = sources[jobs[a][1]], columns(a, k)
         local(a, k).start()
-        if "core" in h:
-            src = source(a).at[:, 1 - c, :, :, :, columns(a, k)]
-            copy(src, h["core"].at[k], a, 0, k, to_core()).start()
+        if kinds[a] in ("xy", "yx"):
+            send(whole.at[:, 1 - c, :, :, :, cols], "core", k, a, to["core"])
         else:
-            for by in range(1, n_y):
-                src = source(a).at[:, :, (y + by) % n_y, :, columns(a, k)]
-                copy(src, h["yy"].at[k, by - 1], a, 2, k, to_y(by)).start()
+            send(whole.at[1 - x, :, :, :, :, cols], "xx", k, a, to["x"])
 
     def first(a, k):
-        h, kind = held[a], jobs[a][1]
+        h, kind = held[a], kinds[a]
+        own = h["own"]
         local(a, k).wait()
-        if "core" not in h:
+        if kind not in ("xy", "yx"):
             return
-        own = h["own"]
-        arrived("core", a, 0, k)
-
-        @pl.loop(0, n_x * DEPTH)
+        arrived("core", a, k)
+
+        @pl.loop(0, 2 * DEPTH)
         def _(i):
             for j in range(n_y):
                 at = (k, i // DEPTH, i % DEPTH, j)
                 own[at] = own[at] + h["core"][at]
 
         if kind == "xy":
-            for by in range(1, n_x):
-                src = own.at[k, (x + by) % n_x]
-                copy(src, h["xx"].at[k, by - 1], a, 1, k, to_x(by)).start()
+            send(own.at[k, 1 - x], "xx", k, a, to["x"])
         else:
-            for by in range(1, n_y):
-                src = own.at[k, :, :, (y + by) % n_y]
-                copy(src, h["yy"].at[k, by - 1], a, 2, k, to_y(by)).start()
+            send(own.at[k, :, :, 1 - y], "yy", k, a, to["y"])
 
     def second(a, k):
-        h, kind = held[a], jobs[a][1]
-        own = h.get("own")
+        h, kind = held[a], kinds[a]
+        own = h["own"]
         if kind == "xy":
-            arrived("xx", a, 1, k)
+            arrived("xx", a, k)
 
             @pl.loop(0, DEPTH)
             def _(i):
                 for j in range(n_y):
-                    for s in range(n_x - 1):
-                        at = (k, x, i, j)
-                        own[at] = own[at] + h["xx"][k, s, i, j]
-
-            for by in range(1, n_y):
-                src = own.at[k, x, :, (y + by) % n_y]
-                copy(src, h["yy"].at[k, by - 1], a, 2, k, to_y(by)).start()
+                    at = (k, x, i, j)
+                    own[at] = own[at] + h["xx"][k, i, j]
+
+            send(own.at[k, x, :, 1 - y], "yy", k, a, to["y"])
         elif kind == "yx":
-            arrived("yy", a, 2, k)
+            arrived("yy", a, k)
 
             @pl.loop(0, DEPTH)
             def _(i):
-                for j in range(n_x):
-                    for s in range(n_y - 1):
-                        at = (k, j, i, y)
-                        own[at] = own[at] + h["yy"][k, s, j, i]
-
-            for by in range(1, n_x):
-                src = own.at[k, (x + by) % n_x, :, y]
-                copy(src, h["xx"].at[k, by - 1], a, 1, k, to_x(by)).start()
+                for j in range(2):
+                    at = (k, j, i, y)
+                    own[at] = own[at] + h["yy"][k, j, i]
+
+            send(own.at[k, 1 - x, :, y], "xx", k, a, to["x"])
 
     def third(a, k):
-        h, kind = held[a], jobs[a][1]
-        own = h.get("own")
+        h, kind = held[a], kinds[a]
+        own = h["own"]
         if kind in ("xy", "yx"):
-            name, stage, others = ("yy", 2, n_y - 1) if kind == "xy" else ("xx", 1, n_x - 1)
-            arrived(name, a, stage, k)
+            name = "yy" if kind == "xy" else "xx"
+            arrived(name, a, k)
 
             @pl.loop(0, DEPTH)
             def _(i):
-                for s in range(others):
-                    at = (k, x, i, y)
-                    own[at] = own[at] + h[name][k, s, i]
-
-            for by in range(1, DEPTH):
-                src = own.at[k, x, (z + by) % DEPTH, y]
-                copy(src, h["zz"].at[k, by - 1], a, 3, k, to_z(by)).start()
+                at = (k, x, i, y)
+                own[at] = own[at] + h[name][k, i]
+
+            for high in range(2):
+                send(own.at[k, x, high * 2 + 1 - z_low, y], "za", k, a, to["low"], high)
         else:
-            arrived("yy", a, 2, k)
+            arrived("xx", a, k)
 
             @pl.loop(0, DEPTH)
             def _(i):
                 for g in range(own.shape[1]):
-                    for s in range(n_y - 1):
-                        at = (k, g, i, y)
-                        own[at] = own[at] + h["yy"][k, s, g, i]
-
-            for by in range(1, DEPTH):
-                src = own.at[k, :, (z + by) % DEPTH, y]
-                copy(src, h["zz"].at[k, by - 1], a, 3, k, to_z(by)).start()
+                    for j in range(own.shape[3]):
+                        at = (k, g, i, j)
+                        own[at] = own[at] + h["xx"][at]
+
+            for high in range(2):
+                send(own.at[k, :, high * 2 + 1 - z_low], "za", k, a, to["low"], high)
 
     def fourth(a, k):
+        h, kind = held[a], kinds[a]
+        own = h["own"]
+        arrived("za", a, k)
+        if kind in ("xy", "yx"):
+            for high in range(2):
+                at = (k, x, high * 2 + z_low, y)
+                own[at] = own[at] + h["za"][k, high]
+            send(own.at[k, x, (1 - z_high) * 2 + z_low, y], "zb", k, a, to["high"])
+        else:
+
+            @pl.loop(0, own.shape[1])
+            def _(g):
+                for j in range(own.shape[3]):
+                    for high in range(2):
+                        at = (k, g, high * 2 + z_low, j)
+                        own[at] = own[at] + h["za"][k, high, g, j]
+
+            send(own.at[k, :, (1 - z_high) * 2 + z_low], "zb", k, a, to["high"])
+
+    def fifth(a, k):
         h = held[a]
-        array, kind, start, width, chunks = jobs[a]
-        arrived("zz", a, 3, k)
-        if kind != "gates":
-            here = h["own"].at[k, 0, z, y] if kind == "seq" else h["own"].at[k, x, z, y]
-            total = here[...].astype(f32)
-            for s in range(DEPTH - 1):
-                block = h["zz"][k, s, 0] if kind == "seq" else h["zz"][k, s]
-                total = total + block.astype(f32)
-            outs[array][:, start + k * width : start + (k + 1) * width] = total
+        kind, _, _, width, _, out, start = jobs[a]
+        own = h["own"]
+        arrived("zb", a, k)
+        if kind in ("xy", "yx"):
+            total = own[k, x, z, y].astype(f32) + h["zb"][k].astype(f32)
+            outs[out][:, start + k * width : start + (k + 1) * width] = total
+        elif kind == "down":
+            h["sum"][k] = own[k, 0, z, 0] + h["zb"][k, 0, 0]
+
+            @pl.when(moved)
+            def _():
+                send(h["sum"].at[k], "dd", k, a, owner)
+
+            @pl.when(jnp.logical_not(moved))
+            def _():
+                h["dd"][k] = h["sum"][k]
         else:
 
-            @pl.loop(0, n_dp)
+            @pl.loop(0, CORES)
             def _(g):
-                total = h["own"][k, g, z, y].astype(f32)
-                for s in range(DEPTH - 1):
-                    total = total + h["zz"][k, s, g].astype(f32)
-                h["sum"][k, g] = total.astype(bf16)
-
-            h["dd"][k, dp] = h["sum"][k, dp]
-            for by in range(1, n_dp):
-                peer = lax.rem(dp + by, n_dp)
-                copy(h["sum"].at[k, peer], h["dd"].at[k, dp], a, 0, k, to_dp(by)).start()
+                for j in range(n_y):
+                    h["sum"][k, g * n_y + j] = own[k, g, z, j] + h["zb"][k, g, j]
+
+            h["dd"][k, group] = h["sum"][k, group]
+            for g, j in ((1 - c, y), (c, 1 - y), (1 - c, 1 - y)):
+                send(h["sum"].at[k, g * n_y + j], "dd", k, a, device(c=g, y=j), group)
 
     def last(a, k):
         h = held[a]
-        array, kind, start, width, chunks = jobs[a]
+        kind, _, _, width, chunks, out, start = jobs[a]
         if kind == "gates":
-            part = h["dd"].at[k, pl.ds(0, n_dp - 1)]
-            copy(part, part, a, 0, k, to_core()).wait_recv()
-            half = chunks // 2
-            for g in range(n_dp):
-                to = (((k // half) * n_dp + g) * half + k % half) * width
-                outs[array][:, to : to + width] = h["dd"][k, g].astype(f32)
+            part = h["dd"].at[k, pl.ds(0, 3)]
+            copy(part, part, a, STAGES["dd"], k, to["core"]).wait_recv()
+            for g in range(4):
+                at = start + (g * chunks + k) * width
+                outs[out][:, at : at + width] = h["dd"][k, g].astype(f32)
+        elif kind == "down":
+
+            @pl.when(moved)
+            def _():
+                arrived("dd", a, k)
+
+            outs[out][:, start + k * width : start + (k + 1) * width] = h["dd"][k].astype(f32)
 
     lists = {"all": [], "rest": []}
     for a, job in enumerate(jobs):
-        group = "all" if "core" in held[a] else "rest"
-        lists[group].append([(a, k) for k in range(job[4])])
+        lists["all" if job[0] in ("xy", "yx") else "rest"].append([(a, k) for k in range(job[4])])
+    stages = (begin, first, second, third, fourth, fifth, last)
+    longest = max(len(interleave(parts)) for parts in lists.values())
     events = []
-    for group, parts in lists.items():
+    for name, parts in lists.items():
         order = interleave(parts)
-        pace = max(len(interleave(p)) for p in lists.values()) / max(1, len(order))
-        for i, (a, k) in enumerate(order):
-            for stage, lag in zip((begin, first, second, third, fourth, last), LAGS[group]):
-                events.append((i * pace + lag, len(events), stage, (a, k)))
-    if work:
+        for i, what in enumerate(order):
+            for stage, lag in zip(stages, LAGS[name]):
+                events.append((i * longest / len(order) + lag, len(events), stage, what))
+    if light:
+        own_ref, edge_ref, grad_ref, weights = given
+        own_out, edge_out, edges_in = made
+        ready, landed, edge_ssem, edge_rsem = refs
+        pieces = own_ref.shape[0]
         reach = (seq > 0, seq < DEPTH * n_y - 1)
+        inner = (own_ref, edge_ref, grad_ref, own_out, edge_out)
+
+        def edge_copy(side, p):
+            src = ready.at[p, pl.ds(side * RADIUS, RADIUS)]
+            dst = landed.at[p, pl.ds((1 - side) * RADIUS, RADIUS)]
+            return pltpu.make_async_remote_copy(
+                src_ref=src,
+                dst_ref=dst,
+                send_sem=edge_ssem.at[side],
+                recv_sem=edge_rsem.at[1 - side, p],
+                device_id=(dp, seq - 1 + 2 * side),
+                device_id_type=MESH,
+            )
 
         def unit(p, g):
-            light_back_unit(reach, (g,), *[ref.at[pl.ds(p, 1)] for ref in operands])
-
-        for p in range(operands[0].shape[0]):
+            light_back_unit(reach, (g,), *[ref.at[pl.ds(p, 1)] for ref in inner])
+            if g == 1:
+                rows = mm_nt(edge_out[p], weights[:, D:])
+                ready[p] = rows.astype(bf16)
+                for side in range(2):
+
+                    @pl.when(reach[side])
+                    def _():
+                        edge_copy(side, p).start()
+
+        for p in range(pieces):
             for g in range(2):
-                events.append(((2 * p + g) * 1.5, len(events), unit, (p, g)))
+                events.append(((2 * p + g) * 1.2, len(events), unit, (p, g)))
     for _, _, stage, what in sorted(events, key=lambda e: e[:2]):
         stage(*what)
 
-    for a, job in enumerate(jobs):
+    if light:
+        for side in range(2):
+            rows = pl.ds(side * RADIUS, RADIUS)
+
+            @pl.when(reach[side])
+            def _():
+                for p in range(pieces):
+                    edge_copy(1 - side, p).wait_recv()
+                    edges_in[p, rows] = landed[p, rows]
+                whole = ready.at[:, rows]
+                pltpu.make_async_remote_copy(
+                    src_ref=whole,
+                    dst_ref=whole,
+                    send_sem=edge_ssem.at[side],
+                    recv_sem=edge_rsem.at[side, 0],
+                    device_id=(dp, seq - 1 + 2 * side),
+                    device_id_type=MESH,
+                ).wait_send()
+
+            @pl.when(jnp.logical_not(reach[side]))
+            def _():
+                for p in range(pieces):
+                    edges_in[p, rows] = jnp.zeros((RADIUS, D), bf16)
+
+    for a, kind in enumerate(kinds):
         h = held[a]
-        for name, stage in (("core", 0), ("xx", 1), ("yy", 2), ("zz", 3)):
+        for name in ("core", "xx", "yy", "za", "zb"):
             if name in h:
-                copy(h[name], h[name], a, stage, 0, to_core()).wait_send()
-        if job[1] == "gates":
-            part = h["dd"].at[:, pl.ds(0, n_dp - 1)]
-            copy(part, part, a, 0, 0, to_core()).wait_send()
+                copy(h[name], h[name], a, STAGES[name], 0, to["core"]).wait_send()
+        if kind == "gates":
+            part = h["dd"].at[:, pl.ds(0, 3)]
+            copy(part, part, a, STAGES["dd"], 0, to["core"]).wait_send()
+        elif kind == "down":
+
+            @pl.when(moved)
+            def _():
+                copy(h["dd"], h["dd"], a, STAGES["dd"], 0, to["core"]).wait_send()
 
 
 def interleave(parts):
@@ -610,13 +902,64 @@
     return [v for _, _, v in sorted(keyed)]
 
 
-LAGS = {"all": (-4, 0, 2, 4, 6.5, 9), "rest": (-2, -1, -1, 1, 3.5, 6)}
+LAGS = {"all": (-4, 0, 2, 4, 6, 8, 8), "rest": (-2, -1, -1, 1.5, 3.5, 5.5, 8)}
+STAGES = {"core": 0, "xx": 1, "yy": 2, "za": 3, "zb": 4, "dd": 5}
 SCRATCH = {
-    "xy": ("own", "core", "xx", "yy", "zz", "lsem", "rsem", "ssem"),
-    "yx": ("own", "core", "xx", "yy", "zz", "lsem", "rsem", "ssem"),
-    "seq": ("own", "yy", "zz", "lsem", "rsem", "ssem"),
-    "gates": ("own", "yy", "zz", "sum", "dd", "lsem", "rsem", "ssem"),
+    "xy": ("own", "core", "xx", "yy", "za", "zb", "lsem", "rsem", "ssem"),
+    "yx": ("own", "core", "xx", "yy", "za", "zb", "lsem", "rsem", "ssem"),
+    "gates": ("own", "xx", "za", "zb", "sum", "dd", "lsem", "rsem", "ssem"),
+    "down": ("own", "xx", "za", "zb", "sum", "dd", "lsem", "rsem", "ssem"),
 }
+
+
+def reduce_all(values, jobs, widths, n_y, collective_id, light=()):
+    operands, scratch = [], []
+    for value, inner in values:
+        height, columns = value.shape
+        lead = (2, CORES, DEPTH, n_y) if inner else (2, 1, DEPTH, 1)
+        operands.append(value.reshape(lead + (height // math.prod(lead), columns)))
+    heights = {job[5]: operands[job[1]].shape[4] for job in jobs}
+    out_shape = [jax.ShapeDtypeStruct((heights[o], w), f32) for o, w in enumerate(widths)]
+    for kind, source, _, width, k, _, _ in jobs:
+        _, inner, _, outer, height, _ = operands[source].shape
+        if kind == "xy":
+            shapes = [(2, DEPTH, n_y)] * 2 + [(DEPTH, n_y), (DEPTH,), (2,), ()]
+        elif kind == "yx":
+            shapes = [(2, DEPTH, n_y)] * 2 + [(DEPTH,), (2, DEPTH), (2,), ()]
+        else:
+            both = (inner, outer)
+            shapes = [(inner, DEPTH, outer)] * 2 + [(2,) + both, both]
+            shapes += [(4,), (4,)] if kind == "gates" else [(), ()]
+        scratch += [pltpu.VMEM((k,) + shape + (height, width), bf16) for shape in shapes]
+        scratch += [
+            pltpu.SemaphoreType.DMA((k,)),
+            pltpu.SemaphoreType.DMA((6, k)),
+            pltpu.SemaphoreType.DMA((6,)),
+        ]
+    if light:
+        pieces, edge_rows = light[1].shape[:2]
+        out_shape += [jax.ShapeDtypeStruct(v.shape, bf16) for v in light[:2]]
+        out_shape.append(jax.ShapeDtypeStruct((pieces, edge_rows, D), bf16))
+        scratch += [pltpu.VMEM((pieces, edge_rows, D), bf16)] * 2
+        scratch += [pltpu.SemaphoreType.DMA((2,)), pltpu.SemaphoreType.DMA((2, pieces))]
+    total = sum(v.size for v, _ in values)
+    here = pl.BlockSpec(memory_space=pltpu.VMEM)
+    return pl.pallas_call(
+        functools.partial(
+            reduce_kernel, tuple(jobs), (len(values), len(widths), bool(light)), n_y
+        ),
+        out_shape=out_shape,
+        in_specs=[pl.BlockSpec(memory_space=pl.ANY)] * len(values) + [here] * len(light),
+        out_specs=[here] * len(out_shape),
+        scratch_shapes=scratch,
+        compiler_params=pltpu.CompilerParams(
+            collective_id=collective_id, has_side_effects=True, vmem_limit_bytes=60 << 20
+        ),
+        cost_estimate=pl.CostEstimate(
+            flops=2 * total, bytes_accessed=32 * total, transcendentals=0
+        ),
+        name="reduce_gradients",
+    )(*operands, *light)
 
 
 def copy_kernel(*refs):
@@ -634,54 +977,6 @@
         out_specs=[pl.BlockSpec(memory_space=pltpu.VMEM)] * count,
         name="copy_outputs",
     )(*values)
-
-
-def reduce_all(values, jobs, n_x, n_y, collective_id, work=()):
-    n_dp = n_x * CORES
-    kinds = {array: kind for array, kind, _, _, _ in jobs}
-    operands, out_shape, scratch = [], [], []
-    for array, value in enumerate(values):
-        height, columns = value.shape
-        groups = {"seq": (1,), "gates": (n_dp,)}.get(kinds[array], (n_x, CORES))
-        chunk = height // (n_y * DEPTH * math.prod(groups))
-        operands.append(value.reshape(groups + (DEPTH, n_y, chunk, columns)))
-        columns *= n_dp if kinds[array] == "gates" else 1
-        out_shape.append(jax.ShapeDtypeStruct((chunk, columns), f32))
-    for array, kind, _, width, k in jobs:
-        tile = (out_shape[array].shape[0], width)
-        lead = {"seq": (1,), "gates": (n_dp,)}.get(kind, (n_x,))
-        shapes = [(k,) + lead + (DEPTH, n_y)]
-        if kind == "xy":
-            shapes += shapes + [(k, n_x - 1, DEPTH, n_y), (k, n_y - 1, DEPTH), (k, DEPTH - 1)]
-        elif kind == "yx":
-            shapes += shapes + [(k, n_x - 1, DEPTH), (k, n_y - 1, n_x, DEPTH), (k, DEPTH - 1)]
-        else:
-            shapes += [(k, n_y - 1) + lead + (DEPTH,), (k, DEPTH - 1) + lead]
-        if kind == "gates":
-            shapes += [(k, n_dp)] * 2
-        scratch += [pltpu.VMEM(shape + tile, bf16) for shape in shapes]
-        scratch += [
-            pltpu.SemaphoreType.DMA((k,)),
-            pltpu.SemaphoreType.DMA((4, k)),
-            pltpu.SemaphoreType.DMA((4,)),
-        ]
-    total = sum(v.size for v in values)
-    out_shape += [jax.ShapeDtypeStruct(v.shape, bf16) for v in work[:2]]
-    here = pl.BlockSpec(memory_space=pltpu.VMEM)
-    return pl.pallas_call(
-        functools.partial(reduce_kernel, tuple(jobs), len(values), (n_x, n_y), bool(work)),
-        out_shape=out_shape,
-        in_specs=[pl.BlockSpec(memory_space=pl.ANY)] * len(values) + [here] * len(work),
-        out_specs=[here] * len(out_shape),
-        scratch_shapes=scratch,
-        compiler_params=pltpu.CompilerParams(
-            collective_id=collective_id, has_side_effects=True, vmem_limit_bytes=60 << 20
-        ),
-        cost_estimate=pl.CostEstimate(
-            flops=2 * total, bytes_accessed=32 * total, transcendentals=0
-        ),
-        name="reduce_gradients",
-    )(*operands, *work)
 
 
 def per_device(
@@ -716,8 +1011,8 @@
     ring_z = Ring("seq", n_y, DEPTH)
     capacity = max(2, 3 * rows // (16 * n_seq))
     slots = n_seq * capacity
-    light_factor = LHD ** (-0.5)
-    heavy_factor = HHD ** (-0.5)
+    each = D // (n_dp * n_seq)
+    kernels = each % 8 == 0 and n_x == n_y == 2
 
     def reduce_grad(value, first, second):
         height, width = value.shape
@@ -745,11 +1040,6 @@
             axis=1,
         )
 
-    def reduce_seq(value):
-        parts = value.reshape(1, DEPTH, n_y, value.shape[0] // n_seq, value.shape[1])
-        parts = ring_z.scatter_sum(parts, 1).astype(bf16)
-        return ring_y.scatter_sum(parts, 1)[0]
-
     def reduce_vectors(value):
         count, width = value.shape
         chunk = width // (n_dp * n_seq)
@@ -826,56 +1116,52 @@
     feed_in = mm(pick, normed_second).astype(bf16)
     grad_in = mm(pick, grad_token).astype(bf16)
 
-    hidden = light_gates.shape[1] // 2
-    light_gate = mm(normed_second, light_gates[:, :hidden])
-    light_up = mm(normed_second, light_gates[:, hidden:])
-    light_act, light_pull = jax.vjp(glu_rows, light_gate, light_up)
-    light_act = light_act.astype(bf16)
-    light_feed = mm(light_act, light_down)
-    grad_light_gate, grad_light_up = light_pull(mm_nt(cot, light_down))
-    grad_light_pre = jnp.concatenate([grad_light_gate.astype(bf16), grad_light_up.astype(bf16)], 1)
-
-    dp_rank = lax.axis_index("dp")
-    share = heavy_gates.shape[1] // (2 * n_dp)
-    gates_here = [
-        lax.dynamic_slice_in_dim(heavy_gates, (part * n_dp + dp_rank) * share, share, 1)
-        for part in range(2)
-    ]
-    down_here = lax.dynamic_slice_in_dim(heavy_down, dp_rank * share, share, 0)
-    feed_all = core.gather(ring_x.gather(jnp.stack([feed_in, grad_in]), 1), 1)
-    feed_all, light_act, grad_light_pre = lax.optimization_barrier(
-        (feed_all, light_act, grad_light_pre)
-    )
-    feed_rows, grad_rows = feed_all[0], feed_all[1]
-    heavy_gate = mm(feed_rows, gates_here[0])
-    heavy_up = mm(feed_rows, gates_here[1])
-    heavy_act, heavy_pull = jax.vjp(glu_rows, heavy_gate, heavy_up)
-    heavy_act = heavy_act.astype(bf16)
-    heavy_part = mm(heavy_act, down_here).astype(bf16)
-    grad_heavy_gate, grad_heavy_up = heavy_pull(mm_nt(grad_rows, down_here))
-    grad_heavy_pre = [grad_heavy_gate.astype(bf16), grad_heavy_up.astype(bf16)]
-    grad_part = (
-        mm_nt(grad_heavy_pre[0], gates_here[0]) + mm_nt(grad_heavy_pre[1], gates_here[1])
-    ).astype(bf16)
-    back = core.return_sum(jnp.stack([heavy_part, grad_part]), 1).astype(bf16)
-    back, light_act_late, grad_light_late = lax.optimization_barrier(
-        (back, light_act, grad_light_pre)
-    )
-    back = ring_x.return_sum(back, 1).astype(bf16)
-    heavy_result, grad_feed_in = back[0], back[1]
+    wide = heavy_gates.shape[1] // 2
+    share = wide // 4
+    if kernels:
+        light_act, grad_light_pre, light_feed, grad_light, back, feed_all, heavy_act, heavy_pre = (
+            feed_forward(
+                normed_second,
+                cot,
+                jnp.stack([feed_in, grad_in]),
+                light_gates,
+                light_down,
+                heavy_gates,
+                heavy_down,
+                n_y,
+            )
+        )
+        feed_rows = feed_all[:, 0].reshape(4 * slots, D)
+        grad_rows = feed_all[:, 1].reshape(4 * slots, D)
+        heavy_act = heavy_act.reshape(4 * slots, share)
+        heavy_pre = heavy_pre.reshape(4 * slots, 2 * share)
+        heavy_result, grad_feed_in = back[0], back[1]
+    else:
+        feed_rows, grad_rows = feed_in, grad_in
+        hidden = light_down.shape[0]
+        pre = mm(normed_second, light_gates)
+        light_act, *grads = glu_and_pull(pre[:, :hidden], pre[:, hidden:], mm_nt(cot, light_down))
+        light_act = light_act.astype(bf16)
+        grad_light_pre = jnp.concatenate(grads, axis=1).astype(bf16)
+        light_feed = mm(light_act, light_down)
+        grad_light = mm_nt(grad_light_pre, light_gates)
+        pre = mm(feed_in, heavy_gates)
+        heavy_act, *grads = glu_and_pull(pre[:, :wide], pre[:, wide:], mm_nt(grad_in, heavy_down))
+        heavy_act = heavy_act.astype(bf16)
+        heavy_pre = jnp.concatenate(grads, axis=1).astype(bf16)
+        heavy_result = mm(heavy_act, heavy_down).astype(bf16)
+        grad_feed_in = mm_nt(heavy_pre, heavy_gates).astype(bf16)
     heavy_down_grad = mm_tn(heavy_act, grad_rows).astype(bf16)
-    heavy_gates_grad = jnp.concatenate(
-        [mm_tn(feed_rows, grad_heavy_pre[0]), mm_tn(feed_rows, grad_heavy_pre[1])], axis=1
-    ).astype(bf16)
-    light_down_grad = mm_tn(light_act_late, cot).astype(bf16)
-    light_gates_grad = mm_tn(normed_second, grad_light_late).astype(bf16)
+    heavy_gates_grad = mm_tn(feed_rows, heavy_pre).astype(bf16)
+    light_down_grad = mm_tn(light_act, cot).astype(bf16)
+    light_gates_grad = mm_tn(normed_second, grad_light_pre).astype(bf16)
 
     token_result = mm_tn(pick, heavy_result)
     output = (middle + light_feed + gating * token_result).astype(bf16).reshape(layer_input.shape)
     grad_gating = jnp.sum(cot.astype(f32) * token_result, axis=-1, keepdims=True)
     grad_logit = grad_gating * gating * (1.0 - gating)
     grad_second = (
-        mm_nt(grad_light_pre, light_gates)
+        grad_light
         + mm_tn(pick, grad_feed_in)
         + grad_logit * router.astype(f32)
     )
@@ -916,61 +1202,58 @@
         grad_key_rows.reshape(pieces, key_slots, D), "seq", scatter_dimension=1, tiled=True
     )
     grad_light_att = grad_light_att.reshape(pieces, tokens, D)
-    each = D // (n_dp * n_seq)
-    early = [
-        light_gates_grad,
-        light_down_grad,
-        light_output_grad,
-        heavy_output_grad,
-        heavy_gates_grad,
-        heavy_down_grad,
-    ]
-    if each % 8 == 0:
+    if kernels:
+        early = [
+            (light_gates_grad, True),
+            (light_down_grad, True),
+            (light_output_grad, True),
+            (heavy_output_grad, True),
+            (heavy_gates_grad, True),
+            (heavy_down_grad, False),
+        ]
+        half = light_gates_grad.shape[1] // 2
         jobs = [
-            (0, "xy", 0, 512, light_gates_grad.shape[1] // 512),
-            (1, "xy", 0, 384, D // 384),
-            (2, "xy", 0, 384, D // 384),
-            (3, "xy", 0, 384, D // 384),
-            (4, "gates", 0, 256, heavy_gates_grad.shape[1] // 256),
-            (5, "seq", 0, 128, D // 128),
+            ("xy", 0, 0, 512, half // 512, 0, 0),
+            ("yx", 0, half, 512, half // 512, 0, half),
+            ("yx", 1, 0, 384, D // 384, 1, 0),
+            ("xy", 2, 0, 384, D // 384, 2, 0),
+            ("yx", 3, 0, 384, D // 384, 3, 0),
+            ("gates", 4, 0, 256, share // 256, 4, 0),
+            ("gates", 4, share, 256, share // 256, 4, wide),
+            ("down", 5, 0, 128, D // 128, 5, 0),
         ]
-        *early, grad_own, grad_edge = reduce_all(
-            early, jobs, n_x, n_y, 0, (own_proj, edge_proj, grad_light_att)
+        widths = (2 * half, D, D, D, 2 * wide, D)
+        *early, grad_own, grad_edge, grad_around = reduce_all(
+            early, jobs, widths, n_y, 0, (own_proj, edge_proj, grad_light_att, light_inputs)
         )
     else:
         grad_own, grad_edge = light_attention_back(reach, own_proj, edge_proj, grad_light_att)
-        parts = heavy_gates_grad.reshape(n_dp, DEPTH, n_y, each, -1)
-        parts = ring_z.scatter_sum(parts, 1).astype(bf16)
-        parts = ring_y.scatter_sum(parts, 1).astype(bf16)
-        parts = lax.all_to_all(parts, "dp", split_axis=0, concat_axis=0, tiled=True)
-        parts = parts.reshape(n_dp, each, 2, -1).transpose(1, 2, 0, 3)
-        early = [reduce_split(v) for v in early[:4]]
-        early += [parts.reshape(each, -1).astype(f32), reduce_seq(heavy_down_grad)]
+        early = [light_gates_grad, light_down_grad, light_output_grad, heavy_output_grad]
+        early += [heavy_gates_grad, heavy_down_grad]
+        early = [reduce_split(v) for v in early]
+        grad_edge_rows = mm_nt(grad_edge.reshape(-1, 2 * D), light_inputs[:, D:]).astype(bf16)
+        grad_edge_rows = grad_edge_rows.reshape(pieces, 2 * RADIUS, D)
+        from_right = lax.ppermute(
+            grad_edge_rows[:, :RADIUS], "seq", [(i + 1, i) for i in range(ends)]
+        )
+        from_left = lax.ppermute(
+            grad_edge_rows[:, RADIUS:], "seq", [(i, i + 1) for i in range(ends)]
+        )
+        grad_around = jnp.concatenate([from_left, from_right], axis=1)
     grad_own = grad_own.reshape(rows, 3 * D)
     grad_edge = grad_edge.reshape(pieces * 2 * RADIUS, 2 * D)
-    grad_edge_rows = mm_nt(grad_edge, light_inputs[:, D:]).astype(bf16)
-    grad_edge_rows = grad_edge_rows.reshape(pieces, 2 * RADIUS, D)
-    from_right = lax.ppermute(
-        grad_edge_rows[:, :RADIUS], "seq", [(i + 1, i) for i in range(ends)]
-    )
-    from_left = lax.ppermute(
-        grad_edge_rows[:, RADIUS:], "seq", [(i, i + 1) for i in range(ends)]
-    )
-    light_inputs_grad = jnp.concatenate(
-        [
-            mm_tn(normed_flat, grad_own[:, :D]),
-            mm_tn(normed_flat, grad_own[:, D:]) + mm_tn(edge_flat, grad_edge),
-        ],
-        axis=1,
-    ).astype(bf16)
+    light_query_grad = mm_tn(normed_flat, grad_own[:, :D]).astype(bf16)
+    light_pair_grad = mm_tn(normed_flat, grad_own[:, D:]) + mm_tn(edge_flat, grad_edge)
+    light_pair_grad = light_pair_grad.astype(bf16)
 
     grad_hq_rows = mm_nt(grad_hq_low, heavy_queries).astype(bf16).reshape(pieces, QCAP, D)
     grad_first = mm_nt(grad_own, light_inputs).reshape(pieces, tokens, D)
+    grad_slots = jnp.concatenate([grad_hq_rows, grad_key_own.astype(bf16)], axis=1)
+    both_pick = jnp.concatenate([query_pick, key_pick], axis=1)
     grad_first = (
         grad_first
-        + jnp.einsum("pqt,pqd->ptd", query_pick, grad_hq_rows, preferred_element_type=f32)
-        + jnp.einsum("pkt,pkd->ptd", key_pick, grad_key_own.astype(bf16), preferred_element_type=f32)
-        + jnp.concatenate([from_left, from_right], axis=1).astype(f32)
+        + jnp.einsum("pkt,pkd->ptd", both_pick, grad_slots, preferred_element_type=f32)
+        + grad_around.astype(f32)
     )
     first_gain_grad = jnp.sum(grad_first * unit_first, axis=(0, 1))
     input_grad = grad_middle.reshape(pieces, tokens, D) + norm_pull(
@@ -978,20 +1261,32 @@
     )
     vectors = jnp.stack([first_gain_grad, second_gain_grad, router_grad])
     devices = n_dp * n_seq
-    late = [light_inputs_grad, heavy_queries_grad, heavy_keyvalue_grad]
-    if each % 8 == 0:
+    if kernels:
         lines = vectors.reshape(3, devices, each).transpose(1, 0, 2)
         lines = jnp.pad(lines, ((0, 0), (0, 5), (0, 256 - each))).reshape(devices * 8, 256)
-        jobs = []
-        for array, value in enumerate(late):
-            half = value.shape[1] // 2
-            jobs += [(array, "xy", 0, 384, half // 384), (array, "yx", half, 384, half // 384)]
-        jobs.append((len(late), "xy", 0, 256, 1))
-        sums = reduce_all(late + [lines.astype(bf16)], jobs, n_x, n_y, 1)
+        late = [light_query_grad, light_pair_grad, heavy_queries_grad, heavy_keyvalue_grad]
+        late = [(v, True) for v in [*late, lines.astype(bf16)]]
+        jobs = (
+            ("xy", 0, 0, 384, 1, 0, 0),
+            ("yx", 0, 384, 384, 1, 0, 384),
+            ("xy", 1, 0, 384, 2, 0, D),
+            ("yx", 1, D, 384, 2, 0, 2 * D),
+            ("xy", 2, 0, 384, 1, 1, 0),
+            ("yx", 2, 384, 384, 1, 1, 384),
+            ("xy", 3, 0, 384, 2, 2, 0),
+            ("yx", 3, D, 384, 2, 2, D),
+            ("xy", 4, 0, 256, 1, 3, 0),
+        )
+        sums = reduce_all(late, jobs, (3 * D, D, 2 * D, 256), n_y, 1)
         *sums, lines = copy_all([*early, *sums])
         early, late = sums[: len(early)], sums[len(early) :]
         vectors = lines[:3, :each]
     else:
+        late = [
+            jnp.concatenate([light_query_grad, light_pair_grad], axis=1),
+            heavy_queries_grad,
+            heavy_keyvalue_grad,
+        ]
         late = [reduce_split(v) for v in late]
         vectors = reduce_vectors(vectors)
     light_gates_grad, light_down_grad, light_output_grad, heavy_output_grad = early[:4]

time: 475 us -> 447 us (0.941)
  Pallas kernels: 205 us -> 258 us
  matrix products: 137 us -> 92.8 us
  starting transfers between devices: 17.2 us -> 6.28 us
  waiting for transfers between devices: 43.5 us -> 33.2 us
  local copies, waits for them, and re-layouts: 21 us -> 12.8 us
  other arithmetic: 33 us -> 25.4 us
    pallas_call x2 -> x3, Pallas kernels: 174 us -> 227 us  [the longest x2 179 us: reduce_all(): pl.pallas_call(functools.partial(reduce_kernel, tuple(jobs), (len(values)...]
    dot_general x39 -> x26, matrix products: 123 us -> 82.7 us  [dot(): lax.dot_general(left, right, (over, ((), ())), preferred_element_type=f32)]
    ppermute x6 -> x0, starting transfers between devices: 10.7 us -> none  [the longest x1 5.86 us: per_device(): lax.ppermute(grad_edge_rows[:, RADIUS:], 'seq', [(i, i + 1) for i in rang...]
    concatenate x5 -> x0, other arithmetic: 8.83 us -> none  [the longest x1 2.39 us: per_device(): jnp.concatenate([grad_light_gate.astype(bf16), grad_light_up.astype(bf16)...]
    ppermute x6 -> x0, waiting for transfers between devices: 8.34 us -> none  [the longest x4 8.34 us: shift(): return lax.ppermute(value, self.axis, pairs)]
    dot_general x3 -> x0, local copies, waits for them, and re-layouts: 6.44 us -> none  [dot(): lax.dot_general(left, right, (over, ((), ())), preferred_element_type=f32)]
  transfers between devices with their start and end apart: 10 -> 4, of which waited for: 4 -> 2; matrix products, arithmetic and copies ran while one was open for 21% -> 16% of each run, Pallas kernels for 30% -> 33%
where the time goes in v3:
time: 447 us; the launch traced here: 444 us
  Pallas kernels  258 us (58%)
  matrix products  92.8 us (21%)
  waiting for transfers between devices  33.2 us (7%)
  other arithmetic  25.4 us (6%)
  between operations  15.1 us (3%)
  local copies, waits for them, and re-layouts  12.8 us (3%)
  starting transfers between devices  6.28 us (1%)
    pallas_call x2, Pallas kernels, reduce_all(): pl.pallas_call(functools.partial(reduce_kernel, tuple(jobs), (len(values)...  179 us
    dot_general x26, matrix products, dot(): lax.dot_general(left, right, (over, ((), ())), preferred_element_type=f32)  82.7 us
    pallas_call x1, Pallas kernels, feed_forward(): pl.pallas_call(functools.partial(feed_kernel, n_y), out_shape=[jax.ShapeD...  47.9 us
    ppermute x1, waiting for transfers between devices, per_device(): lax.ppermute(layer_input[:, tokens - RADIUS:], 'seq', [(i, i + 1) for i i...  22.8 us
    pallas_call x1, Pallas kernels, light_attention(): pl.pallas_call(light_kernel, out_shape=jax.ShapeDtypeStruct((pieces, toke...  15.9 us
    all_gather x1, waiting for transfers between devices, per_device(): key_all = lax.all_gather(key_raw, 'seq', axis=1, tiled=True)  10.4 us
  transfers between devices with their start and end apart: 4, of which 2 were waited for; matrix products, arithmetic and copies ran while one was open for 16% of the time, Pallas kernels for 33%

profile of v3, /device:TPU:0, one launch (start us, length us, event | category | flops | bytes accessed | tf_op | source)
XLA Modules:
  0.0 443.9 jit_solution(4375206178607174739)
XLA Ops:
  7.3 2.7 convolution_convert_fusion.12
  10.1 2.6 fusion.69
  12.7 4.9 %collective-permute-start = (bf16[4,128,768]{2,1,0:T(8,128)(2,1)}, bf16[4,128,768]{2,1,0:T(8,128)(2,1)S(1)}, u32[]{:S(2)}, u32[]{:S(2)}) collective-permute-start(bf16[4,128,768]{2,1,0:T(8,128)(2,1)} %get-tuple-element.95), channel_id=1, source_target_pairs={{0,1},{1,2},{2,3},{3,4},{4,5},{5,6},{6,7},{8,9},{9,10},{10,11},{11... | collective-permute-start | bytes 2359304 | tf_op jit(solution)/shard_map/ppermute | solution.py:1053
  17.7 1.3 collective-permute-start.1
  21.1 1.9 multiply_reduce_fusion.7
  25.8 2.0 multiply_convert_fusion.4
  28.7 4.2 convolution_convert_fusion.1
  33.0 22.8 %collective-permute-done = bf16[4,128,768]{2,1,0:T(8,128)(2,1)S(1)} collective-permute-done((bf16[4,128,768]{2,1,0:T(8,128)(2,1)}, bf16[4,128,768]{2,1,0:T(8,128)(2,1)S(1)}, u32[]{:S(2)}, u32[]{:S(2)}) %collective-permute-start) | collective-permute-done | bytes 786464 | tf_op jit(solution)/shard_map/ppermute | solution.py:1053
  55.8 1.8 multiply_reduce_fusion.6
  58.2 1.4 maximum_convert_fusion
  59.9 2.8 convolution_convert_fusion.2
  62.8 15.9 %light_attention.1 = bf16[4,256,768]{2,1,0:T(8,128)(2,1)S(1)} custom-call(s32[2]{0:T(128)S(1)} %add_convert_fusion.1.ends_ref, bf16[4,256,2304]{2,1,0:T(8,128)(2,1)S(1)} %bitcast.147, bf16[4,256,1536]{2,1,0:T(8,128)(2,1)S(1)} %bitcast.149), custom_call_target="tpu_custom_call" | custom-call | flops 3221225472 | bytes 9437184 | tf_op jit(solution)/shard_map/light_attention/pallas_call | solution.py:152
  78.7 1.1 copy-done.5
  79.8 3.1 fusion.70
  82.9 10.4 %all-gather.2.cloned.1.call-done = bf16[4,512,768]{2,1,0:T(8,128)(2,1)} async-done(((bf16[4,64,768]{2,1,0:T(8,128)(2,1)}), bf16[4,512,768]{2,1,0:T(8,128)(2,1)}) %all-gather.2.cloned.1.call-update) | async-done | bytes 3145744 | tf_op jit(solution)/shard_map/all_gather | solution.py:1065
  93.3 2.7 multiply_reduce_fusion
  96.9 5.2 %convolution_convert_fusion = bf16[2048,1536]{1,0:T(8,128)(2,1)S(1)} fusion(bf16[2048,768]{1,0:T(8,128)(2,1)S(1)} %fusion.1, bf16[768,1536]{1,0:T(8,128)(2,1)S(1)} %copy-done), kind=kOutput, calls=%fused_computation | convolution fusion | flops 4834983936 | bytes 11796480 | tf_op jit(solution)/shard_map/dot_general | solution.py:26
  102.2 4.1 heavy_attention.1
  107.2 1.6 multiply_reduce_fusion.5
  110.5 1.0 copy-done.13
  112.2 0.9 pad_maximum_fusion.own_rows
  113.0 47.9 %feed_forward.1 = (bf16[1024,1024]{1,0:T(8,128)(2,1)}, bf16[1024,2048]{1,0:T(8,128)(2,1)}, f32[1024,768]{1,0:T(8,128)}, f32[1024,768]{1,0:T(8,128)}, bf16[2,192,...) custom-call(bf16[1024,768]{1,0:T(8,128)(2,1)} %copy-done.16, ...), custom_call_target="tpu_custom_call" | custom-call | flops 16911433728 | bytes 31457280 | tf_op jit(solution)/shard_map/feed_forward/pallas_call | solution.py:536
  160.9 5.2 %convolution_convert_fusion.8 = bf16[1024,768]{1,0:T(8,128)(2,1)} fusion(bf16[1024,1024]{1,0:T(8,128)(2,1)} %get-tuple-element.53, bf16[1024,768]{1,0:T(8,128)(2,1)} %bitcast.165), kind=kOutput, calls=%fused_computation.55 | convolution fusion | flops 1611399168 | bytes 5242880 | tf_op jit(solution)/shard_map/dot_general | solution.py:26
  166.1 1.5 fusion.68
  168.5 0.9 fusion.8
  169.5 1.1 copy-done.8
  170.6 1.5 multiply_reduce_fusion.1
  172.5 3.0 fusion.67
  175.5 2.6 convolution_convert_fusion.6
  178.6 1.5 bitcast_convert_fusion.2
  180.6 8.7 %heavy_attention_back.1 = (bf16[4,64,768]{2,1,0:T(8,128)(2,1)S(1)}, bf16[4,512,1536]{2,1,0:T(8,128)(2,1)S(1)}) custom-call(bf16[4,64,768]{2,1,0:T(8,128)(2,1)S(1)} %bitcast.152, bf16[4,512,1536]{2,1,0:T(8,128)(2,1)S(1)} %bitcast.146, f32[4,1,512]{2,1,0:T(1,128)S(1)} %compare_convert_fusion.live_ref, bf16[4,64,768]{2,1,0:T(8,128)(2,1)S(1)} %bitcast.154), custom_call_target="tpu_custom_call" | custom-call | flops 4026531840 | bytes 14155776 | tf_op jit(solution)/shard_map/heavy_attention_back/pallas_call | solution.py:343
  189.3 6.6 %convolution_convert_fusion.5 = bf16[2048,768]{1,0:T(8,128)(2,1)} fusion(bf16[2048,1536]{1,0:T(8,128)(2,1)S(1)} %bitcast.155, bf16[768,1536]{1,0:T(8,128)(2,1)S(1)} %copy-done), kind=kOutput, calls=%fused_computation.20 | convolution fusion | flops 4833411072 | bytes 11796480 | tf_op jit(solution)/shard_map/dot_general | solution.py:26
  196.0 4.5 %convolution_convert_fusion.7 = bf16[1024,768]{1,0:T(8,128)(2,1)} fusion(bf16[768,1024]{1,0:T(8,128)(2,1)} %bitcast.201, bf16[768,768]{1,0:T(8,128)(2,1)} %bitcast.190), kind=kOutput, calls=%fused_computation.54 | convolution fusion | flops 1208745984 | bytes 4325376 | tf_op jit(solution)/shard_map/dot_general | solution.py:26
  201.1 4.8 %convolution_convert_fusion.10 = bf16[768,768]{1,0:T(8,128)(2,1)} fusion(bf16[1024,768]{1,0:T(8,128)(2,1)} %bitcast.159, bf16[1024,768]{1,0:T(8,128)(2,1)} %copy-done.15), kind=kOutput, calls=%fused_computation.65 | convolution fusion | flops 1208549376 | bytes 4325376 | tf_op jit(solution)/shard_map/dot_general | solution.py:26
  205.9 4.0 convolution_convert_fusion.3
  209.9 4.9 %convolution_convert_fusion.4 = bf16[768,2048]{1,0:T(8,128)(2,1)} fusion(bf16[1024,768]{1,0:T(8,128)(2,1)S(1)} %copy-done.18, bf16[1024,2048]{1,0:T(8,128)(2,1)S(1)} %copy-done.56), kind=kOutput, calls=%fused_computation.19 | convolution fusion | flops 3222798336 | bytes 8912896 | tf_op jit(solution)/shard_map/dot_general | solution.py:26
  214.8 128.5 %reduce_gradients.2 = (f32[24,2048]{1,0:T(8,128)}, f32[32,768]{1,0:T(8,128)}, f32[24,768]{1,0:T(8,128)}, f32[24,768]{1,0:T(8,128)}, f32[24,8192]{1,0:T(8,128)}, ...) custom-call(bf16[2,2,4,2,24,2048]{5,4,3,2,1,0:T(8,128)(2,1)} %bitcas, ...), custom_call_target="tpu_custom_call" | custom-call | flops 11796480 | bytes 188743680 | tf_op jit(solution)/shard_map/reduce_gradients/pallas_call | solution.py:947
  343.3 1.5 bitcast_convert_fusion.1
  345.5 4.2 fusion.25
  349.7 2.7 fusion.9
  352.4 5.9 %fusion.2 = bf16[768,1536]{1,0:T(8,128)(2,1)} fusion(f32[768,1536]{1,0:T(8,128)S(1)} %fusion.9, bf16[4,256,1536]{2,1,0:T(8,128)(2,1)S(1)} %copy-done.51, f32[4,256]{1,0:T(4,128)S(1)} %copy-done.45, f32[768]{0:T(1024)S(1)} %convert_element_type.169, bf16[4,128,768]{2,1,0:T(8,128)(2,1)} %collective-permute-done.1, bf16[4,128,768]{2,1,0:T(8,128)(2,1)S(1)} %copy-done.27), kind=kOutput, calls=%fused_computation.12 | convolution fusion | flops 2423783424 | bytes 11803648 | tf_op jit(solution)/shard_map/dot_general | solution.py:26
  358.3 5.6 %fusion.3 = f32[4,256,768]{2,1,0:T(8,128)} fusion(bf16[4,256,2304]{2,1,0:T(8,128)(2,1)S(1)} %bitcast.176, bf16[768,2304]{1,0:T(8,128)(2,1)S(1)} %copy-done.24), kind=kOutput, calls=%fused_computation.16 | convolution fusion | flops 3623878656 | bytes 11403264 | tf_op jit(solution)/shard_map/dot_general | solution.py:26
  363.9 6.6 %bitcast_convert_fusion = bf16[768,1536]{1,0:T(8,128)(2,1)} fusion(bf16[4,512,1536]{2,1,0:T(8,128)(2,1)S(1)} %bitcast.157, bf16[4,512,768]{2,1,0:T(8,128)(2,1)S(1)} %copy-done.12, f32[768]{0:T(1024)S(1)} %convert_element_type.169, f32[4,512]{1,0:T(4,128)S(1)} %get-tuple-element.100), kind=kOutput, calls=%fused_computation.10 | convolution fusion | flops 4839309312 | bytes 11807744 | tf_op jit(solution)/shard_map/dot_general | solution.py:26
  370.5 6.1 %multiply_reduce_fusion.2 = (bf16[768]{0:T(1024)(128)(2,1)S(1)}, f32[4,256]{1,0:T(4,128)S(1)}, f32[4,256,768]{2,1,0:T(8,128)}) fusion(bf16[4,256,768]{2,1,0:T(8,128)(2,1)} %param.19, f32[4,256]{1,0:T(4,128)S(1)} %get-tuple-element.105, f32[768]{0:T(1024)S(1)} %convert_element_type.169, bf16[4,256,768]{2,1,0:T(8,128)(2,1)} %get-tuple-element.62, ...), kind=kOutput, calls=%fused_computation.34 | convolution fusion | flops 210893056 | bytes 10367488 | tf_op jit(solution)/shard_map/pkt,pkd->ptd/dot_general | solution.py:1255
  377.4 50.5 %reduce_gradients.3 = (f32[24,2304]{1,0:T(8,128)}, f32[24,768]{1,0:T(8,128)}, f32[24,1536]{1,0:T(8,128)}, f32[8,256]{1,0:T(8,128)}) custom-call(bf16[2,2,4,2,24,768]{5,4,3,2,1,0:T(8,128)(2,1)} %bitcast.188, bf16[2,2,4,2,24,1536]{5,4,3,2,1,0:T(8,128)(2,1)} %bitcast.172, bf16[2,2,4,2,24,768]{5,4,3,2,1,0:T(8,128)(2,1)} %bitcast.187, ...), custom_call_target="tpu_custom_call" | custom-call | flops 7208960 | bytes 115343360 | tf_op jit(solution)/shard_map/reduce_gradients/pallas_call | solution.py:947
  427.9 2.8 copy_outputs.1
  430.7 1.3 slice_bitcast_fusion
  432.0 4.9 %subtract_add_fusion = f32[4,256,768]{2,1,0:T(8,128)} fusion(f32[4,256,768]{2,1,0:T(8,128)} %bitcast.163, bf16[4,256,768]{2,1,0:T(8,128)(2,1)} %param.19, f32[4,256,768]{2,1,0:T(8,128)} %get-tuple-element.113, f32[4,256]{1,0:T(4,128)S(1)} %broadcast_multiply_fusion.1, f32[4,256]{1,0:T(4,128)S(1)} %copy-done.42, f32[768]{0:T(1024)S(1)} %convert_element_type.169, ...), kind=kLoop, calls=%fused_computation.38 | loop fusion | flops 5505024 | bytes 11025408 | tf_op jit(solution)/shard_map/add | solution.py:1259
  (173 shorter events, 15.1 us)
Async XLA Ops:
  7.2 89.7 %copy-start = (bf16[768,1536]{1,0:T(8,128)(2,1)S(1)}, bf16[768,1536]{1,0:T(8,128)(2,1)}, u32[]{:S(2)}) copy-start(bf16[768,1536]{1,0:T(8,128)(2,1)} %param.25) | copy-start | bytes 7077892
  7.2 17.1 %copy-start.43 = (s32[4,64]{1,0:T(4,128)S(1)}, s32[4,64]{1,0:T(4,128)}, u32[]{:S(2)}) copy-start(s32[4,64]{1,0:T(4,128)} %param.35) | copy-start | bytes 3076
  7.2 11.8 %copy-start.47 = (bf16[768]{0:T(1024)(128)(2,1)S(1)}, bf16[768]{0:T(1024)(128)(2,1)}, u32[]{:S(2)}) copy-start(bf16[768]{0:T(1024)(128)(2,1)} %param.21) | copy-start | bytes 4612
  7.2 11.8 %copy-start.48 = (bf16[768]{0:T(1024)(128)(2,1)S(1)}, bf16[768]{0:T(1024)(128)(2,1)}, u32[]{:S(2)}) copy-start(bf16[768]{0:T(1024)(128)(2,1)} %param.27) | copy-start | bytes 4612
  7.2 12.4 %copy-start.49 = (bf16[768]{0:T(1024)(128)(2,1)S(1)}, bf16[768]{0:T(1024)(128)(2,1)}, u32[]{:S(2)}) copy-start(bf16[768]{0:T(1024)(128)(2,1)} %param.28) | copy-start | bytes 4612
  7.2 12.9 %copy-start.46 = (s32[4,256]{1,0:T(4,128)S(1)}, s32[4,256]{1,0:T(4,128)}, u32[]{:S(2)}) copy-start(s32[4,256]{1,0:T(4,128)} %param.37) | copy-start | bytes 12292
  7.2 13.6 %copy-start.50 = (s32[4,8]{1,0:T(4,128)S(1)}, s32[4,8]{1,0:T(4,128)}, u32[]{:S(2)}) copy-start(s32[4,8]{1,0:T(4,128)} %param.36) | copy-start | bytes 388
  7.3 15.8 %copy-start.54 = (s32[4,1]{0,1:T(1,128)S(1)}, s32[4,1]{0,1:T(1,128)}, u32[]{:S(2)}) copy-start(s32[4,1]{0,1:T(1,128)} %param.34) | copy-start | bytes 52
  7.3 86.0 %all-gather.2.cloned.1.call-start = ((), (), s32[]{:S(2)}) async-start(), calls=%async_computation.1 | async-start | bytes 3538944 | tf_op jit(solution)/shard_map/all_gather | solution.py:1065
  10.0 15.0 %copy-start.40 = (s32[4,64]{1,0:T(4,128)S(1)}, s32[4,64]{1,0:T(4,128)}, u32[]{:S(2)}) copy-start(s32[4,64]{1,0:T(4,128)} %param.33) | copy-start | bytes 3076
  10.1 360.4 %reduce-scatter.2.cloned.1.call-start = ((), (), s32[]{:S(2)}) async-start(), calls=%async_computation.2 | async-start | bytes 3538944 | tf_op jit(solution)/shard_map/reduce_scatter | solution.py:1201
  12.7 43.0 %collective-permute-start = (bf16[4,128,768]{2,1,0:T(8,128)(2,1)}, bf16[4,128,768]{2,1,0:T(8,128)(2,1)S(1)}, u32[]{:S(2)}, u32[]{:S(2)}) collective-permute-start(bf16[4,128,768]{2,1,0:T(8,128)(2,1)} %get-tuple-element.95), channel_id=1, source_target_pairs={{0,1},{1,2},{2,3},{3,4},{4,5},{5,6},{6,7},{8,9},{9,10},{10,11},{11... | collective-permute-start | bytes 2359304 | tf_op jit(solution)/shard_map/ppermute | solution.py:1053
  17.7 38.1 %collective-permute-start.1 = (bf16[4,128,768]{2,1,0:T(8,128)(2,1)}, bf16[4,128,768]{2,1,0:T(8,128)(2,1)}, u32[]{:S(2)}, u32[]{:S(2)}) collective-permute-start(bf16[4,128,768]{2,1,0:T(8,128)(2,1)} %get-tuple-element.96), channel_id=1, source_target_pairs={{1,0},{2,1},{3,2},{4,3},{5,4},{6,5},{7,6},{9,8},{10,9},{11,10},{12... | collective-permute-start | bytes 2359304 | tf_op jit(solution)/shard_map/ppermute | solution.py:1056
  21.1 7.1 %copy-start.21 = (bf16[768,768]{1,0:T(8,128)(2,1)S(1)}, bf16[768,768]{1,0:T(8,128)(2,1)}, u32[]{:S(2)}) copy-start(bf16[768,768]{1,0:T(8,128)(2,1)} %param.24) | copy-start | bytes 3538948
  27.7 5.2 %copy-start.9 = (bf16[4,256,768]{2,1,0:T(8,128)(2,1)}, bf16[4,256,768]{2,1,0:T(8,128)(2,1)S(1)}, u32[]{:S(2)}) copy-start(bf16[4,256,768]{2,1,0:T(8,128)(2,1)S(1)} %multiply_convert_fusion.4) | copy-start | bytes 4718596
  28.2 4.8 %copy-start.31 = (bf16[4,64,768]{2,1,0:T(8,128)(2,1)}, bf16[4,64,768]{2,1,0:T(8,128)(2,1)S(1)}, u32[]{:S(2)}) copy-start(bf16[4,64,768]{2,1,0:T(8,128)(2,1)S(1)} %convolution_convert_fusion.13) | copy-start | bytes 1179652
  33.0 29.8 %copy-start.2 = (bf16[1024,2304]{1,0:T(8,128)(2,1)}, bf16[1024,2304]{1,0:T(8,128)(2,1)S(1)}, u32[]{:S(2)}) copy-start(bf16[1024,2304]{1,0:T(8,128)(2,1)S(1)} %convolution_convert_fusion.1) | copy-start | bytes 14155780
  55.8 3.8 copy-start.26
  62.8 15.9 %copy-start.3 = (bf16[1024,1536]{1,0:T(8,128)(2,1)}, bf16[1024,1536]{1,0:T(8,128)(2,1)S(1)}, u32[]{:S(2)}) copy-start(bf16[1024,1536]{1,0:T(8,128)(2,1)S(1)} %convolution_convert_fusion.2) | copy-start | bytes 9437188
  62.8 17.0 %copy-start.52 = (bf16[768,768]{1,0:T(8,128)(2,1)S(1)}, bf16[768,768]{1,0:T(8,128)(2,1)}, u32[]{:S(2)}) copy-start(bf16[768,768]{1,0:T(8,128)(2,1)} %param.23) | copy-start | bytes 3538948
  102.2 4.2 copy-start.1
  102.2 4.2 copy-start.41
  102.2 4.2 copy-start.44
  102.2 4.7 %copy-start.6 = (bf16[4,256,768]{2,1,0:T(8,128)(2,1)S(1)}, bf16[4,256,768]{2,1,0:T(8,128)(2,1)}, u32[]{:S(2)}) copy-start(bf16[4,256,768]{2,1,0:T(8,128)(2,1)} %param.19) | copy-start | bytes 4718596
  102.2 4.7 %copy-start.19 = (bf16[768,768]{1,0:T(8,128)(2,1)S(1)}, bf16[768,768]{1,0:T(8,128)(2,1)}, u32[]{:S(2)}) copy-start(bf16[768,768]{1,0:T(8,128)(2,1)} %param.26) | copy-start | bytes 3538948
  102.2 5.0 %copy-start.29 = (f32[1024,768]{1,0:T(8,128)S(1)}, f32[1024,768]{1,0:T(8,128)}, u32[]{:S(2)}) copy-start(f32[1024,768]{1,0:T(8,128)} %fusion.70) | copy-start | bytes 9437188
  160.9 5.2 %copy-start.30 = (bf16[4,2,192,768]{3,2,1,0:T(8,128)(2,1)S(1)}, bf16[4,2,192,768]{3,2,1,0:T(8,128)(2,1)}, u32[]{:S(2)}) copy-start(bf16[4,2,192,768]{3,2,1,0:T(8,128)(2,1)} %get-tuple-element.54) | copy-start | bytes 7077892
  166.1 3.4 copy-start.28
  167.7 2.9 copy-start.8
  170.6 10.0 %slice-start = ((s8[6291456]{0:T(1024)(128)(4,1)}), s8[4194304]{0:T(1024)(128)(4,1)S(1)}, s32[]{:S(2)}) async-start(s8[6291456]{0:T(1024)(128)(4,1)} %bitcast.144), calls=%async_computation.3 | async-start | bytes 8388608
  172.5 3.0 copy-start.53
  172.5 8.1 %slice-start.1 = ((s8[6291456]{0:T(1024)(128)(4,1)}), s8[2097152]{0:T(1024)(128)(4,1)S(1)}, s32[]{:S(2)}) async-start(s8[6291456]{0:T(1024)(128)(4,1)} %bitcast.144), calls=%async_computation.4 | async-start | bytes 4194304
  189.3 6.7 %copy-start.4 = (bf16[4,512,1536]{2,1,0:T(8,128)(2,1)}, bf16[4,512,1536]{2,1,0:T(8,128)(2,1)S(1)}, u32[]{:S(2)}) copy-start(bf16[4,512,1536]{2,1,0:T(8,128)(2,1)S(1)} %get-tuple-element.57) | copy-start | bytes 18874372
  196.0 4.5 %copy-start.17 = (bf16[1024,768]{1,0:T(8,128)(2,1)S(1)}, bf16[1024,768]{1,0:T(8,128)(2,1)}, u32[]{:S(2)}) copy-start(bf16[1024,768]{1,0:T(8,128)(2,1)} %copy-done.16) | copy-start | bytes 4718596
  201.1 4.8 %copy-start.33 = (bf16[4,1,192,768]{3,2,1,0:T(8,128)(2,1)S(1)}, bf16[4,1,192,768]{3,2,1,0:T(8,128)(2,1)}, u32[]{:S(2)}) copy-start(bf16[4,1,192,768]{3,2,1,0:T(8,128)(2,1)} %get-tuple-element.94) | copy-start | bytes 3538948
  201.1 4.8 %copy-start.55 = (bf16[4,192,2048]{2,1,0:T(8,128)(2,1)S(1)}, bf16[4,192,2048]{2,1,0:T(8,128)(2,1)}, u32[]{:S(2)}) copy-start(bf16[4,192,2048]{2,1,0:T(8,128)(2,1)} %get-tuple-element.55) | copy-start | bytes 9437188
  205.9 4.1 copy-start.18
  205.9 4.1 copy-start.56
  214.8 128.5 %copy-start.32 = (bf16[4,64,768]{2,1,0:T(8,128)(2,1)S(1)}, bf16[4,64,768]{2,1,0:T(8,128)(2,1)}, u32[]{:S(2)}) copy-start(bf16[4,64,768]{2,1,0:T(8,128)(2,1)} %copy-done.31) | copy-start | bytes 1179652
  344.9 4.8 %slice-start.4 = ((s8[4718592]{0:T(1024)(128)(4,1)}), s8[4194304]{0:T(1024)(128)(4,1)S(1)}, s32[]{:S(2)}) async-start(s8[4718592]{0:T(1024)(128)(4,1)} %bitcast.175), calls=%async_computation.7 | async-start | bytes 8388608
  345.5 4.2 slice-start.5
  352.4 5.9 %copy-start.24 = (bf16[768,2304]{1,0:T(8,128)(2,1)S(1)}, bf16[768,2304]{1,0:T(8,128)(2,1)}, u32[]{:S(2)}) copy-start(bf16[768,2304]{1,0:T(8,128)(2,1)} %refs_9_.1) | copy-start | bytes 10616836
  352.4 11.4 %slice-start.2 = ((s8[6291456]{0:T(1024)(128)(4,1)}), s8[4194304]{0:T(1024)(128)(4,1)S(1)}, s32[]{:S(2)}) async-start(s8[6291456]{0:T(1024)(128)(4,1)} %bitcast.156), calls=%async_computation.5 | async-start | bytes 8388608
  358.3 5.6 %slice-start.3 = ((s8[6291456]{0:T(1024)(128)(4,1)}), s8[2097152]{0:T(1024)(128)(4,1)S(1)}, s32[]{:S(2)}) async-start(s8[6291456]{0:T(1024)(128)(4,1)} %bitcast.156), calls=%async_computation.6 | async-start | bytes 4194304
  358.3 5.6 %copy-start.12 = (bf16[4,512,768]{2,1,0:T(8,128)(2,1)S(1)}, bf16[4,512,768]{2,1,0:T(8,128)(2,1)}, u32[]{:S(2)}) copy-start(bf16[4,512,768]{2,1,0:T(8,128)(2,1)} %all-gather.2.cloned.1.call-done) | copy-start | bytes 9437188
  363.9 6.6 %copy-start.35 = (pred[4,64,256]{1,2,0:T(32,128)(4,1)S(1)}, pred[4,64,256]{1,2,0:T(32,128)(4,1)}, u32[]{:S(2)}) copy-start(pred[4,64,256]{1,2,0:T(32,128)(4,1)} %iota_compare_fusion.5) | copy-start | bytes 196612
  363.9 6.6 %copy-start.36 = (pred[4,64,256]{1,2,0:T(32,128)(4,1)S(1)}, pred[4,64,256]{1,2,0:T(32,128)(4,1)}, u32[]{:S(2)}) copy-start(pred[4,64,256]{1,2,0:T(32,128)(4,1)} %iota_compare_fusion.6) | copy-start | bytes 196612
  377.4 54.7 %copy-start.42 = (f32[4,256]{1,0:T(4,128)S(1)}, f32[4,256]{1,0:T(4,128)}, u32[]{:S(2)}) copy-start(f32[4,256]{1,0:T(4,128)} %get-tuple-element.104) | copy-start | bytes 12292
  (19 other events, 40.8 us)
Sparse Core Ops, SparseCore 0:
  10.9 82.3 all-gather.1
  196.1 96.1 reduce-scatter.1

commit v4 on v3

--- a/solution.py
+++ b/solution.py
@@ -379,19 +379,29 @@
 
 def feed_kernel(
     n_y,
+    normed_in,
+    cot_in,
+    own_rows,
+    gates_in,
+    down_in,
+    gates_heavy,
+    down_heavy,
+    act_to,
+    pre_to,
+    feed_to,
+    grad_to,
+    back_out,
+    rows_to,
+    heavy_act_to,
+    heavy_pre_to,
     normed,
     cot,
-    own_rows,
     gates,
     down,
-    gates_heavy,
-    down_heavy,
     act_out,
     pre_out,
     feed_out,
     grad_out,
-    back_out,
-    rows_out,
     heavy_act_out,
     heavy_pre_out,
     wide,
@@ -401,6 +411,8 @@
     from_core,
     to_y,
     from_y,
+    in_sem,
+    out_sem,
     weight_sem,
     rows_rsem,
     rows_ssem,
@@ -415,7 +427,20 @@
     to_core, to_beside = (dp + 1 - 2 * c, seq), (dp, seq + 1 - 2 * y)
     share = tall.shape[0]
     total = gates_heavy.shape[1] // 2
-    slots = rows.shape[2]
+    inputs = [
+        pltpu.make_async_copy(src, dst, in_sem.at[i])
+        for i, (src, dst) in enumerate(
+            (
+                (own_rows, rows.at[me]),
+                (gates_in, gates),
+                (down_in, down),
+                (normed_in, normed),
+                (cot_in, cot),
+            )
+        )
+    ]
+    for load in inputs:
+        load.start()
     loads = [
         pltpu.make_async_copy(
             gates_heavy.at[:, pl.ds(pl.multiple_of(i * total + me * share, share), share)],
@@ -449,12 +474,23 @@
     def rows_copy(slot, i, peer):
         return copy(rows.at[slot], rows.at[slot], rows_ssem.at[i], rows_rsem.at[slot], peer)
 
-    rows[me] = own_rows[...]
+    inputs[0].wait()
     rows_copy(me, 0, to_beside).start()
     rows_copy(me, 1, to_core).start()
     beside, diagonal, other = c * n_y + 1 - y, (1 - c) * n_y + 1 - y, (1 - c) * n_y + y
     hidden = down.shape[0]
     step = 256
+    for load in inputs[1:]:
+        load.wait()
+    outputs = (
+        (act_out, act_to),
+        (pre_out, pre_to),
+        (feed_out, feed_to),
+        (grad_out, grad_to),
+        (heavy_act_out, heavy_act_to),
+        (heavy_pre_out, heavy_pre_to),
+        (rows, rows_to),
+    )
 
     @pl.loop(0, normed.shape[0] // step)
     def _(t):
@@ -470,6 +506,8 @@
         pre_out[at, hidden:] = grad_up
         feed_out[at] = mm(act, down[...])
         grad_out[at] = mm_nt(grad_gate, gates[:, :hidden]) + mm_nt(grad_up, gates[:, hidden:])
+        for i, (src, dst) in enumerate(outputs[:4]):
+            pltpu.make_async_copy(src.at[at], dst.at[at], out_sem.at[i]).start()
 
     for load in loads:
         load.wait()
@@ -500,6 +538,8 @@
         heavy_act_out[slot] = act
         heavy_pre_out[slot, :, :share] = grad_gate
         heavy_pre_out[slot, :, share:] = grad_up
+        for n, (src, dst) in enumerate(outputs[4:6]):
+            pltpu.make_async_copy(src.at[slot], dst.at[slot], out_sem.at[4 + n]).start()
         part[i, 0] = mm(act, tall[...]).astype(bf16)
         part[i, 1] = (mm_nt(grad_gate, wide[0]) + mm_nt(grad_up, wide[1])).astype(bf16)
 
@@ -517,7 +557,7 @@
         def _():
             copy(part.at[3], from_core.at[1], core_ssem.at[1], core_rsem.at[1], to_core).start()
 
-    rows_out[...] = rows[...]
+    pltpu.make_async_copy(rows, rows_to, out_sem.at[6]).start()
     copy(part.at[3], from_core.at[1], core_ssem.at[1], core_rsem.at[1], to_core).wait()
     copy(to_y, from_y, y_ssem, y_rsem, to_beside).wait()
     sums = part[0].astype(f32) + from_core[1].astype(f32) + from_y[...].astype(f32)
@@ -525,6 +565,8 @@
     copy(part.at[1], from_core.at[0], core_ssem.at[0], core_rsem.at[0], to_core).wait_send()
     for i, slot in enumerate((me, me, beside)):
         rows_copy(slot, i, to_core).wait_send()
+    for i, (src, dst) in enumerate(outputs):
+        pltpu.make_async_copy(src, dst, out_sem.at[i]).wait()
 
 
 def feed_forward(normed, cot, own_rows, gates, down, gates_heavy, down_heavy, n_y):
@@ -545,9 +587,19 @@
             jax.ShapeDtypeStruct((4, slots, share), bf16),
             jax.ShapeDtypeStruct((4, slots, 2 * share), bf16),
         ],
-        in_specs=[here] * 5 + [anywhere] * 2,
-        out_specs=[here] * 8,
+        in_specs=[anywhere] * 7,
+        out_specs=[anywhere] * 4 + [here] + [anywhere] * 3,
         scratch_shapes=[
+            pltpu.VMEM((count, D), bf16),
+            pltpu.VMEM((count, D), bf16),
+            pltpu.VMEM((D, 2 * hidden), bf16),
+            pltpu.VMEM((hidden, D), bf16),
+            pltpu.VMEM((count, hidden), bf16),
+            pltpu.VMEM((count, 2 * hidden), bf16),
+            pltpu.VMEM((count, D), f32),
+            pltpu.VMEM((count, D), f32),
+            pltpu.VMEM((4, slots, share), bf16),
+            pltpu.VMEM((4, slots, 2 * share), bf16),
             pltpu.VMEM((2, D, share), bf16),
             pltpu.VMEM((share, D), bf16),
             pltpu.VMEM((4,) + pair, bf16),
@@ -555,6 +607,8 @@
             pltpu.VMEM((2,) + pair, bf16),
             pltpu.VMEM(pair, bf16),
             pltpu.VMEM(pair, bf16),
+            pltpu.SemaphoreType.DMA((5,)),
+            pltpu.SemaphoreType.DMA((7,)),
             pltpu.SemaphoreType.DMA((3,)),
             pltpu.SemaphoreType.DMA((4,)),
             pltpu.SemaphoreType.DMA((3,)),
@@ -576,7 +630,7 @@
 
 
 def reduce_kernel(jobs, counts, n_y, *refs):
-    n_sources, n_outs, light = counts
+    n_sources, n_outs, light, factors = counts
     refs = list(refs)
 
     def take(count):
@@ -585,10 +639,13 @@
         return taken
 
     sources = take(n_sources)
-    given = take(4 if light else 0)
+    given = take(4 if light else factors)
     outs = take(n_outs)
     made = take(3 if light else 0)
-    held = [dict(zip(SCRATCH[job[0]], take(len(SCRATCH[job[0]])))) for job in jobs]
+    held = []
+    for job in jobs:
+        names = SCRATCH[job[0]] + (("full",) if len(job) > 7 else ())
+        held.append(dict(zip(names, take(len(names)))))
     kinds = [job[0] for job in jobs]
     dp, seq = lax.axis_index("dp"), lax.axis_index("seq")
     x, c = dp // CORES, dp % CORES
@@ -658,6 +715,40 @@
         start, width = jobs[a][2:4]
         return pl.ds(start + k * width, width)
 
+    if factors:
+        *kept, factor_sem = refs
+        wanted, fetched = [], set()
+        for a, job in enumerate(jobs):
+            for left, right, start in job[7:]:
+                for k in range(job[4]):
+                    wanted.append((k, a, left, right, pl.ds(start + k * job[3], job[3])))
+        fetches = {}
+        for k, a, left, right, cols in sorted(wanted, key=lambda w: w[:2]):
+            for key, part in (((left,), slice(None)), ((right, cols.start), cols)):
+                if key not in fetches:
+                    src, dst = given[key[0]].at[:, part], kept[key[0]].at[:, part]
+                    fetches[key] = pltpu.make_async_copy(src, dst, factor_sem.at[len(fetches)])
+                    fetches[key].start()
+
+    def produce(a, k):
+        width, height = jobs[a][3], held[a]["full"].shape[-2]
+        total = 0.0
+        for left, right, start in jobs[a][7:]:
+            for key in ((left,), (right, start + k * width)):
+                if key not in fetched:
+                    fetched.add(key)
+                    fetches[key].wait()
+            cols = slice(start + k * width, start + (k + 1) * width)
+            total = total + mm_tn(kept[left][...], kept[right][:, cols])
+        at = 0
+        for i in range(2):
+            for j in range(CORES):
+                for m in range(DEPTH):
+                    for n in range(n_y):
+                        rows = total[at * height : (at + 1) * height]
+                        held[a]["full"][k, i, j, m, n] = rows.astype(bf16)
+                        at += 1
+
     def local(a, k):
         whole, cols = sources[jobs[a][1]], columns(a, k)
         if kinds[a] in ("xy", "yx"):
@@ -667,6 +758,10 @@
         return pltpu.make_async_copy(part, held[a]["own"].at[k], held[a]["lsem"].at[k])
 
     def begin(a, k):
+        if len(jobs[a]) > 7:
+            produce(a, k)
+            send(held[a]["full"].at[k, :, 1 - c], "core", k, a, to["core"])
+            return
         whole, cols = sources[jobs[a][1]], columns(a, k)
         local(a, k).start()
         if kinds[a] in ("xy", "yx"):
@@ -677,7 +772,9 @@
     def first(a, k):
         h, kind = held[a], kinds[a]
         own = h["own"]
-        local(a, k).wait()
+        made_here = "full" in h
+        if not made_here:
+            local(a, k).wait()
         if kind not in ("xy", "yx"):
             return
         arrived("core", a, k)
@@ -686,7 +783,8 @@
         def _(i):
             for j in range(n_y):
                 at = (k, i // DEPTH, i % DEPTH, j)
-                own[at] = own[at] + h["core"][at]
+                mine = h["full"][at[:2] + (c,) + at[2:]] if made_here else own[at]
+                own[at] = mine + h["core"][at]
 
         if kind == "xy":
             send(own.at[k, 1 - x], "xx", k, a, to["x"])
@@ -766,7 +864,7 @@
 
     def fifth(a, k):
         h = held[a]
-        kind, _, _, width, _, out, start = jobs[a]
+        kind, _, _, width, _, out, start = jobs[a][:7]
         own = h["own"]
         arrived("zb", a, k)
         if kind in ("xy", "yx"):
@@ -795,7 +893,7 @@
 
     def last(a, k):
         h = held[a]
-        kind, _, _, width, chunks, out, start = jobs[a]
+        kind, _, _, width, chunks, out, start = jobs[a][:7]
         if kind == "gates":
             part = h["dd"].at[k, pl.ds(0, 3)]
             copy(part, part, a, STAGES["dd"], k, to["core"]).wait_recv()
@@ -822,12 +920,26 @@
             for stage, lag in zip(stages, LAGS[name]):
                 events.append((i * longest / len(order) + lag, len(events), stage, what))
     if light:
-        own_ref, edge_ref, grad_ref, weights = given
-        own_out, edge_out, edges_in = made
-        ready, landed, edge_ssem, edge_rsem = refs
-        pieces = own_ref.shape[0]
+        edges_in = made[2]
+        *inner, weights, ready, landed, load_sem, weight_sem, out_sem, edge_ssem, edge_rsem = refs
+        edge_out = inner[4]
+        pieces = edge_out.shape[0]
         reach = (seq > 0, seq < DEPTH * n_y - 1)
-        inner = (own_ref, edge_ref, grad_ref, own_out, edge_out)
+
+        def load(i, p):
+            return pltpu.make_async_copy(given[i].at[p], inner[i].at[p], load_sem.at[i, p])
+
+        def store(i, p):
+            src, dst = inner[3 + i], made[i]
+            if p is not None:
+                src, dst = src.at[p], dst.at[p]
+            return pltpu.make_async_copy(src, dst, out_sem.at[i])
+
+        for p in range(pieces):
+            for i in range(3):
+                load(i, p).start()
+        load_weights = pltpu.make_async_copy(given[3], weights, weight_sem)
+        load_weights.start()
 
         def edge_copy(side, p):
             src = ready.at[p, pl.ds(side * RADIUS, RADIUS)]
@@ -842,8 +954,15 @@
             )
 
         def unit(p, g):
+            if g == 0:
+                for i in range(3):
+                    load(i, p).wait()
             light_back_unit(reach, (g,), *[ref.at[pl.ds(p, 1)] for ref in inner])
             if g == 1:
+                for i in range(2):
+                    store(i, p).start()
+                if p == 0:
+                    load_weights.wait()
                 rows = mm_nt(edge_out[p], weights[:, D:])
                 ready[p] = rows.astype(bf16)
                 for side in range(2):
@@ -859,6 +978,8 @@
         stage(*what)
 
     if light:
+        for i in range(2):
+            store(i, None).wait()
         for side in range(2):
             rows = pl.ds(side * RADIUS, RADIUS)
 
@@ -912,16 +1033,17 @@
 }
 
 
-def reduce_all(values, jobs, widths, n_y, collective_id, light=()):
+def reduce_all(values, jobs, widths, n_y, collective_id, light=(), factors=()):
     operands, scratch = [], []
     for value, inner in values:
         height, columns = value.shape
         lead = (2, CORES, DEPTH, n_y) if inner else (2, 1, DEPTH, 1)
         operands.append(value.reshape(lead + (height // math.prod(lead), columns)))
-    heights = {job[5]: operands[job[1]].shape[4] for job in jobs}
+    heights = {job[5]: D // (8 * DEPTH) if len(job) > 7 else operands[job[1]].shape[4] for job in jobs}
     out_shape = [jax.ShapeDtypeStruct((heights[o], w), f32) for o, w in enumerate(widths)]
-    for kind, source, _, width, k, _, _ in jobs:
-        _, inner, _, outer, height, _ = operands[source].shape
+    for kind, source, _, width, k, out, *rest in jobs:
+        _, inner, _, outer = operands[source].shape[:4]
+        height = heights[out]
         if kind == "xy":
             shapes = [(2, DEPTH, n_y)] * 2 + [(DEPTH, n_y), (DEPTH,), (2,), ()]
         elif kind == "yx":
@@ -936,21 +1058,33 @@
             pltpu.SemaphoreType.DMA((6, k)),
             pltpu.SemaphoreType.DMA((6,)),
         ]
+        if len(rest) > 1:
+            scratch.append(pltpu.VMEM((k, 2, CORES, DEPTH, n_y, height, width), bf16))
     if light:
         pieces, edge_rows = light[1].shape[:2]
         out_shape += [jax.ShapeDtypeStruct(v.shape, bf16) for v in light[:2]]
         out_shape.append(jax.ShapeDtypeStruct((pieces, edge_rows, D), bf16))
+        own, edge, grad, weights = light
+        scratch += [pltpu.VMEM(v.shape, bf16) for v in (own, edge, grad, own, edge, weights)]
         scratch += [pltpu.VMEM((pieces, edge_rows, D), bf16)] * 2
-        scratch += [pltpu.SemaphoreType.DMA((2,)), pltpu.SemaphoreType.DMA((2, pieces))]
-    total = sum(v.size for v, _ in values)
-    here = pl.BlockSpec(memory_space=pltpu.VMEM)
+        scratch += [pltpu.SemaphoreType.DMA((3, pieces)), pltpu.SemaphoreType.DMA]
+        scratch += [pltpu.SemaphoreType.DMA((2,))] * 2 + [pltpu.SemaphoreType.DMA((2, pieces))]
+    if factors:
+        scratch += [pltpu.VMEM(v.shape, bf16) for v in factors]
+        scratch.append(pltpu.SemaphoreType.DMA((32,)))
+    total = 16 * n_y * sum(math.prod(shape.shape) for shape in out_shape[: len(widths)])
+    here, anywhere = pl.BlockSpec(memory_space=pltpu.VMEM), pl.BlockSpec(memory_space=pl.ANY)
+    out_specs = [here] * len(widths) + ([anywhere] * 2 + [here] if light else [])
     return pl.pallas_call(
         functools.partial(
-            reduce_kernel, tuple(jobs), (len(values), len(widths), bool(light)), n_y
+            reduce_kernel,
+            tuple(jobs),
+            (len(values), len(widths), bool(light), len(factors)),
+            n_y,
         ),
         out_shape=out_shape,
-        in_specs=[pl.BlockSpec(memory_space=pl.ANY)] * len(values) + [here] * len(light),
-        out_specs=[here] * len(out_shape),
+        in_specs=[anywhere] * len([*values, *light, *factors]),
+        out_specs=out_specs,
         scratch_shapes=scratch,
         compiler_params=pltpu.CompilerParams(
             collective_id=collective_id, has_side_effects=True, vmem_limit_bytes=60 << 20
@@ -959,7 +1093,7 @@
             flops=2 * total, bytes_accessed=32 * total, transcendentals=0
         ),
         name="reduce_gradients",
-    )(*operands, *light)
+    )(*operands, *light, *factors)
 
 
 def copy_kernel(*refs):
@@ -1210,6 +1344,8 @@
             (heavy_output_grad, True),
             (heavy_gates_grad, True),
             (heavy_down_grad, False),
+            (heavy_queries_grad, True),
+            (heavy_keyvalue_grad, True),
         ]
         half = light_gates_grad.shape[1] // 2
         jobs = [
@@ -1221,8 +1357,10 @@
             ("gates", 4, 0, 256, share // 256, 4, 0),
             ("gates", 4, share, 256, share // 256, 4, wide),
             ("down", 5, 0, 128, D // 128, 5, 0),
+            ("xy", 6, 0, 384, 2, 6, 0),
+            ("xy", 7, 0, 512, 3, 7, 0),
         ]
-        widths = (2 * half, D, D, D, 2 * wide, D)
+        widths = (2 * half, D, D, D, 2 * wide, D, D, 2 * D)
         *early, grad_own, grad_edge, grad_around = reduce_all(
             early, jobs, widths, n_y, 0, (own_proj, edge_proj, grad_light_att, light_inputs)
         )
@@ -1242,10 +1380,6 @@
         grad_around = jnp.concatenate([from_left, from_right], axis=1)
     grad_own = grad_own.reshape(rows, 3 * D)
     grad_edge = grad_edge.reshape(pieces * 2 * RADIUS, 2 * D)
-    light_query_grad = mm_tn(normed_flat, grad_own[:, :D]).astype(bf16)
-    light_pair_grad = mm_tn(normed_flat, grad_own[:, D:]) + mm_tn(edge_flat, grad_edge)
-    light_pair_grad = light_pair_grad.astype(bf16)
-
     grad_hq_rows = mm_nt(grad_hq_low, heavy_queries).astype(bf16).reshape(pieces, QCAP, D)
     grad_first = mm_nt(grad_own, light_inputs).reshape(pieces, tokens, D)
     grad_slots = jnp.concatenate([grad_hq_rows, grad_key_own.astype(bf16)], axis=1)
@@ -1264,30 +1398,29 @@
     if kernels:
         lines = vectors.reshape(3, devices, each).transpose(1, 0, 2)
         lines = jnp.pad(lines, ((0, 0), (0, 5), (0, 256 - each))).reshape(devices * 8, 256)
-        late = [light_query_grad, light_pair_grad, heavy_queries_grad, heavy_keyvalue_grad]
-        late = [(v, True) for v in [*late, lines.astype(bf16)]]
         jobs = (
-            ("xy", 0, 0, 384, 1, 0, 0),
-            ("yx", 0, 384, 384, 1, 0, 384),
-            ("xy", 1, 0, 384, 2, 0, D),
-            ("yx", 1, D, 384, 2, 0, 2 * D),
-            ("xy", 2, 0, 384, 1, 1, 0),
-            ("yx", 2, 384, 384, 1, 1, 384),
-            ("xy", 3, 0, 384, 2, 2, 0),
-            ("yx", 3, D, 384, 2, 2, D),
-            ("xy", 4, 0, 256, 1, 3, 0),
+            ("xy", 0, 0, 384, 1, 0, 0, (0, 2, 0)),
+            ("yx", 0, 384, 384, 1, 0, 384, (0, 2, 384)),
+            ("xy", 0, D, 384, 2, 0, D, (0, 2, D), (1, 3, 0)),
+            ("yx", 0, 2 * D, 384, 2, 0, 2 * D, (0, 2, 2 * D), (1, 3, D)),
+            ("xy", 0, 0, 256, 1, 1, 0),
         )
-        sums = reduce_all(late, jobs, (3 * D, D, 2 * D, 256), n_y, 1)
-        *sums, lines = copy_all([*early, *sums])
-        early, late = sums[: len(early)], sums[len(early) :]
+        factors = (normed_flat, edge_flat, grad_own, grad_edge)
+        late = [(lines.astype(bf16), True)]
+        light_inputs_grad, lines = reduce_all(
+            late, jobs, (3 * D, 256), n_y, 1, (), factors
+        )
+        *early, light_inputs_grad, lines = copy_all([*early, light_inputs_grad, lines])
+        late = [light_inputs_grad, *early[6:]]
         vectors = lines[:3, :each]
     else:
+        light_pair_grad = mm_tn(normed_flat, grad_own[:, D:]) + mm_tn(edge_flat, grad_edge)
         late = [
-            jnp.concatenate([light_query_grad, light_pair_grad], axis=1),
+            jnp.concatenate([mm_tn(normed_flat, grad_own[:, :D]), light_pair_grad], axis=1),
             heavy_queries_grad,
             heavy_keyvalue_grad,
         ]
-        late = [reduce_split(v) for v in late]
+        late = [reduce_split(v.astype(bf16)) for v in late]
         vectors = reduce_vectors(vectors)
     light_gates_grad, light_down_grad, light_output_grad, heavy_output_grad = early[:4]
     return (

time: 447 us -> 417 us (0.933)
  Pallas kernels: 258 us -> 237 us
  matrix products: 92.8 us -> 82.6 us
    pallas_call x2, Pallas kernels: 179 us -> 167 us  [reduce_all(): pl.pallas_call(functools.partial(reduce_kernel, tuple(jobs), (len(values)...]
    dot_general x26 -> x23, matrix products: 82.7 us -> 72.9 us  [dot(): lax.dot_general(left, right, (over, ((), ())), preferred_element_type=f32)]
    pallas_call x1, Pallas kernels: 47.9 us -> 38.4 us  [feed_forward(): pl.pallas_call(functools.partial(feed_kernel, n_y), out_shape=[jax.ShapeD...]
  transfers between devices with their start and end apart: 4 -> 4, of which waited for: 2 -> 2; matrix products, arithmetic and copies ran while one was open for 16% -> 16% of each run, Pallas kernels for 33% -> 34%
where the time goes in v4:
time: 417 us; the launch traced here: 414 us
  Pallas kernels  237 us (57%)
  matrix products  82.6 us (20%)
  waiting for transfers between devices  34.4 us (8%)
  other arithmetic  25.7 us (6%)
  between operations  15.3 us (4%)
  local copies, waits for them, and re-layouts  12.1 us (3%)
  starting transfers between devices  6.41 us (2%)
    pallas_call x2, Pallas kernels, reduce_all(): pl.pallas_call(functools.partial(reduce_kernel, tuple(jobs), (len(values)...  167 us
    dot_general x23, matrix products, dot(): lax.dot_general(left, right, (over, ((), ())), preferred_element_type=f32)  72.9 us
    pallas_call x1, Pallas kernels, feed_forward(): pl.pallas_call(functools.partial(feed_kernel, n_y), out_shape=[jax.ShapeD...  38.4 us
    ppermute x1, waiting for transfers between devices, per_device(): lax.ppermute(layer_input[:, tokens - RADIUS:], 'seq', [(i, i + 1) for i i...  23.2 us
    pallas_call x1, Pallas kernels, light_attention(): pl.pallas_call(light_kernel, out_shape=jax.ShapeDtypeStruct((pieces, toke...  15.9 us
    all_gather x1, waiting for transfers between devices, per_device(): key_all = lax.all_gather(key_raw, 'seq', axis=1, tiled=True)  11.2 us
    pallas_call x1, Pallas kernels, heavy_attention_back(): pl.pallas_call(heavy_back_kernel, out_shape=[jax.ShapeDtypeStruct((pieces...  8.66 us
  transfers between devices with their start and end apart: 4, of which 2 were waited for; matrix products, arithmetic and copies ran while one was open for 16% of the time, Pallas kernels for 34%

profile of v4, /device:TPU:0, one launch (start us, length us, event | category | flops | bytes accessed | tf_op | source)
XLA Modules:
  0.0 413.8 jit_solution(6775427033112949432)
XLA Ops:
  7.3 2.7 convolution_convert_fusion.12
  10.1 2.6 fusion.57
  12.7 5.0 %collective-permute-start = (bf16[4,128,768]{2,1,0:T(8,128)(2,1)}, bf16[4,128,768]{2,1,0:T(8,128)(2,1)S(1)}, u32[]{:S(2)}, u32[]{:S(2)}) collective-permute-start(bf16[4,128,768]{2,1,0:T(8,128)(2,1)} %get-tuple-element.95), channel_id=1, source_target_pairs={{0,1},{1,2},{2,3},{3,4},{4,5},{5,6},{6,7},{8,9},{9,10},{10,11},{11... | collective-permute-start | bytes 2359304 | tf_op jit(solution)/shard_map/ppermute | solution.py:1187
  17.8 1.3 collective-permute-start.1
  21.2 1.9 multiply_reduce_fusion.7
  24.4 0.7 iota_compare_fusion.5
  25.2 2.0 multiply_convert_fusion.3
  28.1 4.6 %convolution_convert_fusion.1 = bf16[1024,2304]{1,0:T(8,128)(2,1)S(1)} fusion(bf16[1024,768]{1,0:T(8,128)(2,1)S(1)} %bitcast.152, bf16[768,2304]{1,0:T(8,128)(2,1)S(1)} %copy-done.28), kind=kOutput, calls=%fused_computation.6 | convolution fusion | flops 3626237952 | bytes 9830400 | tf_op jit(solution)/shard_map/dot_general | solution.py:26
  32.7 23.2 %collective-permute-done = bf16[4,128,768]{2,1,0:T(8,128)(2,1)S(1)} collective-permute-done((bf16[4,128,768]{2,1,0:T(8,128)(2,1)}, bf16[4,128,768]{2,1,0:T(8,128)(2,1)S(1)}, u32[]{:S(2)}, u32[]{:S(2)}) %collective-permute-start) | collective-permute-done | bytes 786464 | tf_op jit(solution)/shard_map/ppermute | solution.py:1187
  55.9 1.5 multiply_reduce_fusion.6
  57.4 1.4 maximum_convert_fusion
  59.2 2.8 convolution_convert_fusion.2
  62.1 15.9 %light_attention.1 = bf16[4,256,768]{2,1,0:T(8,128)(2,1)S(1)} custom-call(s32[2]{0:T(128)S(1)} %add_convert_fusion.1.ends_ref, bf16[4,256,2304]{2,1,0:T(8,128)(2,1)S(1)} %bitcast.139, bf16[4,256,1536]{2,1,0:T(8,128)(2,1)S(1)} %bitcast.141), custom_call_target="tpu_custom_call" | custom-call | flops 3221225472 | bytes 9437184 | tf_op jit(solution)/shard_map/light_attention/pallas_call | solution.py:152
  78.0 1.2 copy-done.6
  79.2 3.1 fusion.58
  82.2 11.2 %all-gather.2.cloned.1.call-done = bf16[4,512,768]{2,1,0:T(8,128)(2,1)} async-done(((bf16[4,64,768]{2,1,0:T(8,128)(2,1)}), bf16[4,512,768]{2,1,0:T(8,128)(2,1)}) %all-gather.2.cloned.1.call-update) | async-done | bytes 3145744 | tf_op jit(solution)/shard_map/all_gather | solution.py:1199
  93.4 2.7 multiply_reduce_fusion
  96.8 0.8 fusion.1
  97.6 5.2 %convolution_convert_fusion = bf16[2048,1536]{1,0:T(8,128)(2,1)S(1)} fusion(bf16[2048,768]{1,0:T(8,128)(2,1)S(1)} %fusion.1, bf16[768,1536]{1,0:T(8,128)(2,1)S(1)} %copy-done), kind=kOutput, calls=%fused_computation | convolution fusion | flops 4834983936 | bytes 11796480 | tf_op jit(solution)/shard_map/dot_general | solution.py:26
  102.9 4.1 heavy_attention.1
  107.8 1.6 multiply_reduce_fusion.5
  109.5 0.7 fusion.4
  111.1 1.0 copy-done.15
  112.8 0.9 pad_maximum_fusion.own_rows
  113.7 38.4 %feed_forward.1 = (bf16[1024,1024]{1,0:T(8,128)(2,1)}, bf16[1024,2048]{1,0:T(8,128)(2,1)}, f32[1024,768]{1,0:T(8,128)}, f32[1024,768]{1,0:T(8,128)}, bf16[2,192,...) custom-call(bf16[1024,768]{1,0:T(8,128)(2,1)} %copy-done.20, ...), custom_call_target="tpu_custom_call" | custom-call | flops 16911433728 | bytes 31457280 | tf_op jit(solution)/shard_map/feed_forward/pallas_call | solution.py:578
  152.1 2.5 fusion.7
  154.8 4.1 multiply_reduce_fusion.1
  158.9 3.4 fusion.55
  162.3 2.6 convolution_convert_fusion.6
  165.9 8.7 %heavy_attention_back.1 = (bf16[4,64,768]{2,1,0:T(8,128)(2,1)S(1)}, bf16[4,512,1536]{2,1,0:T(8,128)(2,1)S(1)}) custom-call(bf16[4,64,768]{2,1,0:T(8,128)(2,1)S(1)} %bitcast.144, bf16[4,512,1536]{2,1,0:T(8,128)(2,1)S(1)} %bitcast.138, f32[4,1,512]{2,1,0:T(1,128)S(1)} %compare_convert_fusion.live_ref, bf16[4,64,768]{2,1,0:T(8,128)(2,1)S(1)} %bitcast.146), custom_call_target="tpu_custom_call" | custom-call | flops 4026531840 | bytes 14155776 | tf_op jit(solution)/shard_map/heavy_attention_back/pallas_call | solution.py:343
  174.6 6.5 %convolution_convert_fusion.5 = bf16[2048,768]{1,0:T(8,128)(2,1)} fusion(bf16[2048,1536]{1,0:T(8,128)(2,1)S(1)} %bitcast.147, bf16[768,1536]{1,0:T(8,128)(2,1)S(1)} %copy-done), kind=kOutput, calls=%fused_computation.18 | convolution fusion | flops 4833411072 | bytes 11796480 | tf_op jit(solution)/shard_map/dot_general | solution.py:26
  181.8 0.7 iota_compare_fusion.6
  184.3 2.7 bitcast_convert_fusion.2
  187.0 1.6 bitcast_convert_fusion.1
  188.7 1.3 copy-done.62
  190.0 2.6 convolution_convert_fusion.7
  192.6 2.5 convolution_convert_fusion.10
  195.1 3.1 convolution_convert_fusion.8
  198.2 4.3 %convolution_convert_fusion.3 = bf16[768,2048]{1,0:T(8,128)(2,1)} fusion(bf16[768,768]{1,0:T(8,128)(2,1)S(1)} %bitcast.176, bf16[768,2048]{1,0:T(8,128)(2,1)S(1)} %bitcast.187), kind=kOutput, calls=%fused_computation.16 | convolution fusion | flops 2417491968 | bytes 7471104 | tf_op jit(solution)/shard_map/dot_general | solution.py:26
  202.5 4.9 %convolution_convert_fusion.4 = bf16[768,2048]{1,0:T(8,128)(2,1)} fusion(bf16[1024,768]{1,0:T(8,128)(2,1)S(1)} %copy-done.22, bf16[1024,2048]{1,0:T(8,128)(2,1)S(1)} %copy-done.63), kind=kOutput, calls=%fused_computation.17 | convolution fusion | flops 3222798336 | bytes 8912896 | tf_op jit(solution)/shard_map/dot_general | solution.py:26
  207.4 6.5 %bitcast_convert_fusion = bf16[768,1536]{1,0:T(8,128)(2,1)} fusion(bf16[4,512,1536]{2,1,0:T(8,128)(2,1)S(1)} %bitcast.149, bf16[4,512,768]{2,1,0:T(8,128)(2,1)S(1)} %copy-done.14, f32[768]{0:T(1024)S(1)} %convert_element_type.161, f32[4,512]{1,0:T(4,128)S(1)} %copy-done.51), kind=kOutput, calls=%fused_computation.10 | convolution fusion | flops 4839309312 | bytes 11807744 | tf_op jit(solution)/shard_map/dot_general | solution.py:26
  213.9 124.5 %reduce_gradients.2 = (f32[24,2048]{1,0:T(8,128)}, f32[32,768]{1,0:T(8,128)}, f32[24,768]{1,0:T(8,128)}, f32[24,768]{1,0:T(8,128)}, f32[24,8192]{1,0:T(8,128)}, ...) custom-call(bf16[2,2,4,2,24,2048]{5,4,3,2,1,0:T(8,128)(2,1)} %bitcas, ...), custom_call_target="tpu_custom_call" | custom-call | flops 29491200 | bytes 471859200 | tf_op jit(solution)/shard_map/reduce_gradients/pallas_call | solution.py:1078
  339.0 9.1 %fusion.2 = f32[4,256,768]{2,1,0:T(8,128)} fusion(bf16[4,256,2304]{2,1,0:T(8,128)(2,1)} %get-tuple-element.60, bf16[768,2304]{1,0:T(8,128)(2,1)} %refs_11_.1), kind=kOutput, calls=%fused_computation.14 | convolution fusion | flops 3623878656 | bytes 11403264 | tf_op jit(solution)/shard_map/dot_general | solution.py:26
  348.1 5.6 %multiply_reduce_fusion.2 = (bf16[768]{0:T(1024)(128)(2,1)S(1)}, f32[4,256]{1,0:T(4,128)S(1)}, f32[4,256,768]{2,1,0:T(8,128)}) fusion(bf16[4,256,768]{2,1,0:T(8,128)(2,1)S(1)} %copy-done.9, f32[4,256]{1,0:T(4,128)S(1)} %get-tuple-element.103, f32[768]{0:T(1024)S(1)} %convert_element_type.161, bf16[4,256,768]{2,1,0:T(8,128)(2,1)} %get-tuple-element.62, ...), kind=kOutput, calls=%fused_computation.30 | convolution fusion | flops 210893056 | bytes 10367488 | tf_op jit(solution)/shard_map/pkt,pkd->ptd/dot_general | solution.py:1389
  354.5 43.0 %reduce_gradients.3 = (f32[24,2304]{1,0:T(8,128)}, f32[8,256]{1,0:T(8,128)}) custom-call(bf16[2,2,4,2,8,256]{5,4,3,2,1,0:T(8,128)(2,1)} %bitcast.178, bf16[1024,768]{1,0:T(8,128)(2,1)} %bitcast.153, bf16[1024,768]{1,0:T(8,128)(2,1)} %copy-done.23, bf16[1024,2304]{1,0:T(8,128)(2,1)} %bitcast.160, bf16[1024,1536]{1,0:T(8,128)(2,1)} %bitcast.164), custom_call_target="tpu_custom_call" | custom-call | flops 3670016 | bytes 58720256 | tf_op jit(solution)/shard_map/reduce_gradients/pallas_call | solution.py:1078
  397.6 2.8 copy_outputs.1
  400.4 1.3 slice_bitcast_fusion
  401.7 5.0 %subtract_add_fusion = f32[4,256,768]{2,1,0:T(8,128)} fusion(f32[4,256,768]{2,1,0:T(8,128)} %bitcast.154, bf16[4,256,768]{2,1,0:T(8,128)(2,1)} %param.19, f32[4,256,768]{2,1,0:T(8,128)} %get-tuple-element.111, f32[4,256]{1,0:T(4,128)S(1)} %broadcast_multiply_fusion.1, f32[4,256]{1,0:T(4,128)S(1)} %copy-done.48, f32[768]{0:T(1024)S(1)} %convert_element_type.161, ...), kind=kLoop, calls=%fused_computation.31 | loop fusion | flops 5505024 | bytes 11025408 | tf_op jit(solution)/shard_map/add | solution.py:1393
  (181 shorter events, 12.9 us)
Async XLA Ops:
  7.2 90.4 %copy-start = (bf16[768,1536]{1,0:T(8,128)(2,1)S(1)}, bf16[768,1536]{1,0:T(8,128)(2,1)}, u32[]{:S(2)}) copy-start(bf16[768,1536]{1,0:T(8,128)(2,1)} %param.25) | copy-start | bytes 7077892
  7.2 17.2 %copy-start.49 = (s32[4,64]{1,0:T(4,128)S(1)}, s32[4,64]{1,0:T(4,128)}, u32[]{:S(2)}) copy-start(s32[4,64]{1,0:T(4,128)} %param.35) | copy-start | bytes 3076
  7.2 11.9 %copy-start.54 = (bf16[768]{0:T(1024)(128)(2,1)S(1)}, bf16[768]{0:T(1024)(128)(2,1)}, u32[]{:S(2)}) copy-start(bf16[768]{0:T(1024)(128)(2,1)} %param.21) | copy-start | bytes 4612
  7.2 11.9 %copy-start.55 = (bf16[768]{0:T(1024)(128)(2,1)S(1)}, bf16[768]{0:T(1024)(128)(2,1)}, u32[]{:S(2)}) copy-start(bf16[768]{0:T(1024)(128)(2,1)} %param.27) | copy-start | bytes 4612
  7.2 12.5 %copy-start.56 = (bf16[768]{0:T(1024)(128)(2,1)S(1)}, bf16[768]{0:T(1024)(128)(2,1)}, u32[]{:S(2)}) copy-start(bf16[768]{0:T(1024)(128)(2,1)} %param.28) | copy-start | bytes 4612
  7.2 13.1 %copy-start.53 = (s32[4,256]{1,0:T(4,128)S(1)}, s32[4,256]{1,0:T(4,128)}, u32[]{:S(2)}) copy-start(s32[4,256]{1,0:T(4,128)} %param.37) | copy-start | bytes 12292
  7.2 13.8 %copy-start.57 = (s32[4,8]{1,0:T(4,128)S(1)}, s32[4,8]{1,0:T(4,128)}, u32[]{:S(2)}) copy-start(s32[4,8]{1,0:T(4,128)} %param.36) | copy-start | bytes 388
  7.3 15.9 %copy-start.60 = (s32[4,1]{0,1:T(1,128)S(1)}, s32[4,1]{0,1:T(1,128)}, u32[]{:S(2)}) copy-start(s32[4,1]{0,1:T(1,128)} %param.34) | copy-start | bytes 52
  7.3 86.1 %all-gather.2.cloned.1.call-start = ((), (), s32[]{:S(2)}) async-start(), calls=%async_computation.1 | async-start | bytes 3538944 | tf_op jit(solution)/shard_map/all_gather | solution.py:1199
  10.1 338.0 %reduce-scatter.2.cloned.1.call-start = ((), (), s32[]{:S(2)}) async-start(), calls=%async_computation.2 | async-start | bytes 3538944 | tf_op jit(solution)/shard_map/reduce_scatter | solution.py:1335
  12.7 14.4 %copy-start.45 = (s32[4,64]{1,0:T(4,128)S(1)}, s32[4,64]{1,0:T(4,128)}, u32[]{:S(2)}) copy-start(s32[4,64]{1,0:T(4,128)} %param.33) | copy-start | bytes 3076
  12.7 43.2 %collective-permute-start = (bf16[4,128,768]{2,1,0:T(8,128)(2,1)}, bf16[4,128,768]{2,1,0:T(8,128)(2,1)S(1)}, u32[]{:S(2)}, u32[]{:S(2)}) collective-permute-start(bf16[4,128,768]{2,1,0:T(8,128)(2,1)} %get-tuple-element.95), channel_id=1, source_target_pairs={{0,1},{1,2},{2,3},{3,4},{4,5},{5,6},{6,7},{8,9},{9,10},{10,11},{11... | collective-permute-start | bytes 2359304 | tf_op jit(solution)/shard_map/ppermute | solution.py:1187
  17.8 38.1 %collective-permute-start.1 = (bf16[4,128,768]{2,1,0:T(8,128)(2,1)}, bf16[4,128,768]{2,1,0:T(8,128)(2,1)}, u32[]{:S(2)}, u32[]{:S(2)}) collective-permute-start(bf16[4,128,768]{2,1,0:T(8,128)(2,1)} %get-tuple-element.96), channel_id=1, source_target_pairs={{1,0},{2,1},{3,2},{4,3},{5,4},{6,5},{7,6},{9,8},{10,9},{11,10},{12... | collective-permute-start | bytes 2359304 | tf_op jit(solution)/shard_map/ppermute | solution.py:1190
  21.2 6.4 %copy-start.26 = (bf16[768,768]{1,0:T(8,128)(2,1)S(1)}, bf16[768,768]{1,0:T(8,128)(2,1)}, u32[]{:S(2)}) copy-start(bf16[768,768]{1,0:T(8,128)(2,1)} %param.24) | copy-start | bytes 3538948
  27.1 5.5 %copy-start.12 = (bf16[4,256,768]{2,1,0:T(8,128)(2,1)}, bf16[4,256,768]{2,1,0:T(8,128)(2,1)S(1)}, u32[]{:S(2)}) copy-start(bf16[4,256,768]{2,1,0:T(8,128)(2,1)S(1)} %multiply_convert_fusion.3) | copy-start | bytes 4718596
  27.6 5.1 %copy-start.32 = (bf16[4,64,768]{2,1,0:T(8,128)(2,1)}, bf16[4,64,768]{2,1,0:T(8,128)(2,1)S(1)}, u32[]{:S(2)}) copy-start(bf16[4,64,768]{2,1,0:T(8,128)(2,1)S(1)} %convolution_convert_fusion.13) | copy-start | bytes 1179652
  32.7 29.3 %copy-start.3 = (bf16[1024,2304]{1,0:T(8,128)(2,1)}, bf16[1024,2304]{1,0:T(8,128)(2,1)S(1)}, u32[]{:S(2)}) copy-start(bf16[1024,2304]{1,0:T(8,128)(2,1)S(1)} %convolution_convert_fusion.1) | copy-start | bytes 14155780
  62.1 15.9 %copy-start.4 = (bf16[1024,1536]{1,0:T(8,128)(2,1)}, bf16[1024,1536]{1,0:T(8,128)(2,1)S(1)}, u32[]{:S(2)}) copy-start(bf16[1024,1536]{1,0:T(8,128)(2,1)S(1)} %convolution_convert_fusion.2) | copy-start | bytes 9437188
  62.1 17.1 %copy-start.58 = (bf16[768,768]{1,0:T(8,128)(2,1)S(1)}, bf16[768,768]{1,0:T(8,128)(2,1)}, u32[]{:S(2)}) copy-start(bf16[768,768]{1,0:T(8,128)(2,1)} %param.23) | copy-start | bytes 3538948
  102.8 4.1 copy-start.2
  102.8 4.1 copy-start.46
  102.8 4.1 copy-start.52
  102.8 4.7 %copy-start.8 = (bf16[4,256,768]{2,1,0:T(8,128)(2,1)S(1)}, bf16[4,256,768]{2,1,0:T(8,128)(2,1)}, u32[]{:S(2)}) copy-start(bf16[4,256,768]{2,1,0:T(8,128)(2,1)} %param.19) | copy-start | bytes 4718596
  102.8 4.7 %copy-start.24 = (bf16[768,768]{1,0:T(8,128)(2,1)S(1)}, bf16[768,768]{1,0:T(8,128)(2,1)}, u32[]{:S(2)}) copy-start(bf16[768,768]{1,0:T(8,128)(2,1)} %param.26) | copy-start | bytes 3538948
  102.9 5.0 %copy-start.30 = (f32[1024,768]{1,0:T(8,128)S(1)}, f32[1024,768]{1,0:T(8,128)}, u32[]{:S(2)}) copy-start(f32[1024,768]{1,0:T(8,128)} %fusion.58) | copy-start | bytes 9437188
  154.7 4.1 copy-start.39
  154.7 4.1 copy-start.16
  154.7 4.1 copy-start.29
  154.8 11.1 %slice-start = ((s8[6291456]{0:T(1024)(128)(4,1)}), s8[4194304]{0:T(1024)(128)(4,1)S(1)}, s32[]{:S(2)}) async-start(s8[6291456]{0:T(1024)(128)(4,1)} %bitcast.136), calls=%async_computation.3 | async-start | bytes 8388608
  158.9 7.0 %slice-start.1 = ((s8[6291456]{0:T(1024)(128)(4,1)}), s8[2097152]{0:T(1024)(128)(4,1)S(1)}, s32[]{:S(2)}) async-start(s8[6291456]{0:T(1024)(128)(4,1)} %bitcast.136), calls=%async_computation.4 | async-start | bytes 4194304
  165.3 9.2 %copy-start.34 = (bf16[4,64,768]{2,1,0:T(8,128)(2,1)}, bf16[4,64,768]{2,1,0:T(8,128)(2,1)S(1)}, u32[]{:S(2)}) copy-start(bf16[4,64,768]{2,1,0:T(8,128)(2,1)S(1)} %convolution_convert_fusion.11) | copy-start | bytes 1179652
  174.5 6.5 %copy-start.5 = (bf16[4,512,1536]{2,1,0:T(8,128)(2,1)}, bf16[4,512,1536]{2,1,0:T(8,128)(2,1)S(1)}, u32[]{:S(2)}) copy-start(bf16[4,512,1536]{2,1,0:T(8,128)(2,1)S(1)} %get-tuple-element.58) | copy-start | bytes 18874372
  181.8 5.2 %copy-start.33 = (bf16[4,64,768]{2,1,0:T(8,128)(2,1)S(1)}, bf16[4,64,768]{2,1,0:T(8,128)(2,1)}, u32[]{:S(2)}) copy-start(bf16[4,64,768]{2,1,0:T(8,128)(2,1)} %copy-done.32) | copy-start | bytes 1179652
  184.3 4.3 %copy-start.31 = (bf16[4,2,192,768]{3,2,1,0:T(8,128)(2,1)S(1)}, bf16[4,2,192,768]{3,2,1,0:T(8,128)(2,1)}, u32[]{:S(2)}) copy-start(bf16[4,2,192,768]{3,2,1,0:T(8,128)(2,1)} %get-tuple-element.54) | copy-start | bytes 7077892
  195.1 12.3 %slice-start.2 = ((s8[6291456]{0:T(1024)(128)(4,1)}), s8[4194304]{0:T(1024)(128)(4,1)S(1)}, s32[]{:S(2)}) async-start(s8[6291456]{0:T(1024)(128)(4,1)} %bitcast.148), calls=%async_computation.5 | async-start | bytes 8388608
  198.2 4.3 %copy-start.22 = (bf16[1024,768]{1,0:T(8,128)(2,1)S(1)}, bf16[1024,768]{1,0:T(8,128)(2,1)}, u32[]{:S(2)}) copy-start(bf16[1024,768]{1,0:T(8,128)(2,1)} %copy-done.20) | copy-start | bytes 4718596
  198.2 4.3 %copy-start.63 = (bf16[1024,2048]{1,0:T(8,128)(2,1)S(1)}, bf16[1024,2048]{1,0:T(8,128)(2,1)}, u32[]{:S(2)}) copy-start(bf16[1024,2048]{1,0:T(8,128)(2,1)} %get-tuple-element.52) | copy-start | bytes 12582916
  198.2 9.2 %slice-start.3 = ((s8[6291456]{0:T(1024)(128)(4,1)}), s8[2097152]{0:T(1024)(128)(4,1)S(1)}, s32[]{:S(2)}) async-start(s8[6291456]{0:T(1024)(128)(4,1)} %bitcast.148), calls=%async_computation.6 | async-start | bytes 4194304
  202.5 4.9 %copy-start.14 = (bf16[4,512,768]{2,1,0:T(8,128)(2,1)S(1)}, bf16[4,512,768]{2,1,0:T(8,128)(2,1)}, u32[]{:S(2)}) copy-start(bf16[4,512,768]{2,1,0:T(8,128)(2,1)} %all-gather.2.cloned.1.call-done) | copy-start | bytes 9437188
  202.5 4.9 %copy-start.51 = (f32[4,512]{1,0:T(4,128)S(1)}, f32[4,512]{1,0:T(4,128)}, u32[]{:S(2)}) copy-start(f32[4,512]{1,0:T(4,128)} %get-tuple-element.100) | copy-start | bytes 24580
  213.9 124.5 %copy-start.27 = (bf16[768,768]{1,0:T(8,128)(2,1)S(1)}, bf16[768,768]{1,0:T(8,128)(2,1)}, u32[]{:S(2)}) copy-start(bf16[768,768]{1,0:T(8,128)(2,1)} %param.24) | copy-start | bytes 3538948
  338.9 9.1 %copy-start.9 = (bf16[4,256,768]{2,1,0:T(8,128)(2,1)S(1)}, bf16[4,256,768]{2,1,0:T(8,128)(2,1)}, u32[]{:S(2)}) copy-start(bf16[4,256,768]{2,1,0:T(8,128)(2,1)} %param.19) | copy-start | bytes 4718596
  338.9 9.1 %copy-start.36 = (pred[4,64,256]{1,2,0:T(32,128)(4,1)S(1)}, pred[4,64,256]{1,2,0:T(32,128)(4,1)}, u32[]{:S(2)}) copy-start(pred[4,64,256]{1,2,0:T(32,128)(4,1)} %iota_compare_fusion.5) | copy-start | bytes 196612
  338.9 9.1 %copy-start.37 = (pred[4,64,256]{1,2,0:T(32,128)(4,1)S(1)}, pred[4,64,256]{1,2,0:T(32,128)(4,1)}, u32[]{:S(2)}) copy-start(pred[4,64,256]{1,2,0:T(32,128)(4,1)} %iota_compare_fusion.6) | copy-start | bytes 196612
  348.1 5.7 %copy-start.43 = (bf16[1,32,24]{2,1,0:T(8,128)(2,1)S(1)}, bf16[1,32,24]{2,1,0:T(8,128)(2,1)}, u32[]{:S(2)}) copy-start(bf16[1,32,24]{2,1,0:T(8,128)(2,1)} %stack.37) | copy-start | bytes 4612
  348.1 5.7 %copy-start.44 = (bf16[1,32,24]{2,1,0:T(8,128)(2,1)S(1)}, bf16[1,32,24]{2,1,0:T(8,128)(2,1)}, u32[]{:S(2)}) copy-start(bf16[1,32,24]{2,1,0:T(8,128)(2,1)} %stack.38) | copy-start | bytes 4612
  354.5 47.2 %copy-start.48 = (f32[4,256]{1,0:T(4,128)S(1)}, f32[4,256]{1,0:T(4,128)}, u32[]{:S(2)}) copy-start(f32[4,256]{1,0:T(4,128)} %get-tuple-element.102) | copy-start | bytes 12292
  401.7 5.0 %copy-start.1 = (bf16[768,1536]{1,0:T(8,128)(2,1)S(1)}, bf16[768,1536]{1,0:T(8,128)(2,1)}, u32[]{:S(2)}) copy-start(bf16[768,1536]{1,0:T(8,128)(2,1)} %param.25) | copy-start | bytes 7077892
  (25 other events, 56.6 us)
Sparse Core Ops, SparseCore 0:
  10.9 82.4 all-gather.1
  181.2 84.6 reduce-scatter.1

commit v5 on v4

--- a/solution.py
+++ b/solution.py
@@ -916,8 +916,11 @@
     events = []
     for name, parts in lists.items():
         order = interleave(parts)
+        order.sort(key=lambda what: len(jobs[what[0]]) > 7)
         for i, what in enumerate(order):
             for stage, lag in zip(stages, LAGS[name]):
+                if factors and stage is begin and len(jobs[what[0]]) == 7:
+                    lag = -20
                 events.append((i * longest / len(order) + lag, len(events), stage, what))
     if light:
         edges_in = made[2]
@@ -1339,11 +1342,8 @@
     if kernels:
         early = [
             (light_gates_grad, True),
-            (light_down_grad, True),
             (light_output_grad, True),
-            (heavy_output_grad, True),
             (heavy_gates_grad, True),
-            (heavy_down_grad, False),
             (heavy_queries_grad, True),
             (heavy_keyvalue_grad, True),
         ]
@@ -1351,24 +1351,18 @@
         jobs = [
             ("xy", 0, 0, 512, half // 512, 0, 0),
             ("yx", 0, half, 512, half // 512, 0, half),
-            ("yx", 1, 0, 384, D // 384, 1, 0),
-            ("xy", 2, 0, 384, D // 384, 2, 0),
-            ("yx", 3, 0, 384, D // 384, 3, 0),
-            ("gates", 4, 0, 256, share // 256, 4, 0),
-            ("gates", 4, share, 256, share // 256, 4, wide),
-            ("down", 5, 0, 128, D // 128, 5, 0),
-            ("xy", 6, 0, 384, 2, 6, 0),
-            ("xy", 7, 0, 512, 3, 7, 0),
+            ("xy", 1, 0, 384, D // 384, 1, 0),
+            ("gates", 2, 0, 256, share // 256, 2, 0),
+            ("gates", 2, share, 256, share // 256, 2, wide),
+            ("xy", 3, 0, 384, 2, 3, 0),
+            ("xy", 4, 0, 512, 3, 4, 0),
         ]
-        widths = (2 * half, D, D, D, 2 * wide, D, D, 2 * D)
+        widths = (2 * half, D, 2 * wide, D, 2 * D)
         *early, grad_own, grad_edge, grad_around = reduce_all(
             early, jobs, widths, n_y, 0, (own_proj, edge_proj, grad_light_att, light_inputs)
         )
     else:
         grad_own, grad_edge = light_attention_back(reach, own_proj, edge_proj, grad_light_att)
-        early = [light_gates_grad, light_down_grad, light_output_grad, heavy_output_grad]
-        early += [heavy_gates_grad, heavy_down_grad]
-        early = [reduce_split(v) for v in early]
         grad_edge_rows = mm_nt(grad_edge.reshape(-1, 2 * D), light_inputs[:, D:]).astype(bf16)
         grad_edge_rows = grad_edge_rows.reshape(pieces, 2 * RADIUS, D)
         from_right = lax.ppermute(
@@ -1404,40 +1398,53 @@
             ("xy", 0, D, 384, 2, 0, D, (0, 2, D), (1, 3, 0)),
             ("yx", 0, 2 * D, 384, 2, 0, 2 * D, (0, 2, 2 * D), (1, 3, D)),
             ("xy", 0, 0, 256, 1, 1, 0),
+            ("yx", 1, 0, 384, 2, 2, 0),
+            ("yx", 2, 0, 384, 2, 3, 0),
+            ("down", 3, 0, 128, D // 128, 4, 0),
         )
         factors = (normed_flat, edge_flat, grad_own, grad_edge)
-        late = [(lines.astype(bf16), True)]
-        light_inputs_grad, lines = reduce_all(
-            late, jobs, (3 * D, 256), n_y, 1, (), factors
-        )
-        *early, light_inputs_grad, lines = copy_all([*early, light_inputs_grad, lines])
-        late = [light_inputs_grad, *early[6:]]
+        late = [
+            (lines.astype(bf16), True),
+            (light_down_grad, True),
+            (heavy_output_grad, True),
+            (heavy_down_grad, False),
+        ]
+        late = reduce_all(late, jobs, (3 * D, 256, D, D, D), n_y, 1, (), factors)
+        sums = copy_all([*early, *late])
+        light_gates_grad, light_output_grad, heavy_gates_grad, heavy_queries_grad = sums[:4]
+        heavy_keyvalue_grad, light_inputs_grad, lines = sums[4:7]
+        light_down_grad, heavy_output_grad, heavy_down_grad = sums[7:]
         vectors = lines[:3, :each]
     else:
         light_pair_grad = mm_tn(normed_flat, grad_own[:, D:]) + mm_tn(edge_flat, grad_edge)
-        late = [
-            jnp.concatenate([mm_tn(normed_flat, grad_own[:, :D]), light_pair_grad], axis=1),
-            heavy_queries_grad,
-            heavy_keyvalue_grad,
-        ]
-        late = [reduce_split(v.astype(bf16)) for v in late]
+        light_inputs_grad = jnp.concatenate(
+            [mm_tn(normed_flat, grad_own[:, :D]), light_pair_grad], axis=1
+        ).astype(bf16)
+        light_inputs_grad = reduce_split(light_inputs_grad)
+        light_output_grad = reduce_split(light_output_grad)
+        heavy_queries_grad = reduce_split(heavy_queries_grad)
+        heavy_keyvalue_grad = reduce_split(heavy_keyvalue_grad)
+        heavy_output_grad = reduce_split(heavy_output_grad)
+        light_gates_grad = reduce_split(light_gates_grad)
+        light_down_grad = reduce_split(light_down_grad)
+        heavy_gates_grad = reduce_split(heavy_gates_grad)
+        heavy_down_grad = reduce_split(heavy_down_grad)
         vectors = reduce_vectors(vectors)
-    light_gates_grad, light_down_grad, light_output_grad, heavy_output_grad = early[:4]
     return (
         output,
         input_grad,
         vectors[0],
-        late[0],
+        light_inputs_grad,
         light_output_grad,
-        late[1],
-        late[2],
+        heavy_queries_grad,
+        heavy_keyvalue_grad,
         heavy_output_grad,
         vectors[1],
         vectors[2],
         light_gates_grad,
         light_down_grad,
-        early[4],
-        early[5],
+        heavy_gates_grad,
+        heavy_down_grad,
     )
 
 

time: 417 us -> 410 us (0.983)
  matrix products: 82.6 us -> 77.7 us
    dot_general x23, matrix products: 72.9 us -> 68 us  [dot(): lax.dot_general(left, right, (over, ((), ())), preferred_element_type=f32)]
  transfers between devices with their start and end apart: 4 -> 4, of which waited for: 2 -> 2; matrix products, arithmetic and copies ran while one was open for 16% -> 14% of each run, Pallas kernels for 34% -> 30%
where the time goes in v5:
time: 410 us; the launch traced here: 407 us
  Pallas kernels  235 us (57%)
  matrix products  77.7 us (19%)
  waiting for transfers between devices  35.7 us (9%)
  other arithmetic  23.9 us (6%)
  between operations  15.2 us (4%)
  local copies, waits for them, and re-layouts  12.1 us (3%)
  starting transfers between devices  7.24 us (2%)
    pallas_call x2, Pallas kernels, reduce_all(): pl.pallas_call(functools.partial(reduce_kernel, tuple(jobs), (len(values)...  165 us
    dot_general x23, matrix products, dot(): lax.dot_general(left, right, (over, ((), ())), preferred_element_type=f32)  68 us
    pallas_call x1, Pallas kernels, feed_forward(): pl.pallas_call(functools.partial(feed_kernel, n_y), out_shape=[jax.ShapeD...  38.4 us
    ppermute x1, waiting for transfers between devices, per_device(): lax.ppermute(layer_input[:, tokens - RADIUS:], 'seq', [(i, i + 1) for i i...  24.9 us
    pallas_call x1, Pallas kernels, light_attention(): pl.pallas_call(light_kernel, out_shape=jax.ShapeDtypeStruct((pieces, toke...  15.9 us
    all_gather x1, waiting for transfers between devices, per_device(): key_all = lax.all_gather(key_raw, 'seq', axis=1, tiled=True)  10.8 us
    pallas_call x1, Pallas kernels, heavy_attention_back(): pl.pallas_call(heavy_back_kernel, out_shape=[jax.ShapeDtypeStruct((pieces...  8.66 us
  transfers between devices with their start and end apart: 4, of which 2 were waited for; matrix products, arithmetic and copies ran while one was open for 14% of the time, Pallas kernels for 30%

profile of v5, /device:TPU:0, one launch (start us, length us, event | category | flops | bytes accessed | tf_op | source)
XLA Modules:
  0.0 406.6 jit_solution(11935181487615077588)
XLA Ops:
  7.3 2.7 convolution_convert_fusion.12
  10.1 2.6 fusion.57
  12.7 5.9 %collective-permute-start = (bf16[4,128,768]{2,1,0:T(8,128)(2,1)}, bf16[4,128,768]{2,1,0:T(8,128)(2,1)}, u32[]{:S(2)}, u32[]{:S(2)}) collective-permute-start(bf16[4,128,768]{2,1,0:T(8,128)(2,1)} %get-tuple-element.95), channel_id=1, source_target_pairs={{0,1},{1,2},{2,3},{3,4},{4,5},{5,6},{6,7},{8,9},{9,10},{10,11},{11... | collective-permute-start | bytes 2359304 | tf_op jit(solution)/shard_map/ppermute | solution.py:1190
  18.6 1.3 collective-permute-start.1
  20.3 2.0 multiply_reduce_fusion.7
  23.0 0.7 iota_compare_fusion.5
  23.7 2.0 multiply_convert_fusion.3
  26.7 4.3 %convolution_convert_fusion.1 = bf16[1024,2304]{1,0:T(8,128)(2,1)S(1)} fusion(bf16[1024,768]{1,0:T(8,128)(2,1)S(1)} %bitcast.152, bf16[768,2304]{1,0:T(8,128)(2,1)S(1)} %copy-done.28), kind=kOutput, calls=%fused_computation.6 | convolution fusion | flops 3626237952 | bytes 9830400 | tf_op jit(solution)/shard_map/dot_general | solution.py:26
  31.0 24.9 %collective-permute-done = bf16[4,128,768]{2,1,0:T(8,128)(2,1)} collective-permute-done((bf16[4,128,768]{2,1,0:T(8,128)(2,1)}, bf16[4,128,768]{2,1,0:T(8,128)(2,1)}, u32[]{:S(2)}, u32[]{:S(2)}) %collective-permute-start) | collective-permute-done | bytes 786464 | tf_op jit(solution)/shard_map/ppermute | solution.py:1190
  55.9 1.8 multiply_reduce_fusion.6
  57.7 1.6 maximum_convert_fusion
  59.7 2.8 convolution_convert_fusion.2
  62.6 15.9 %light_attention.1 = bf16[4,256,768]{2,1,0:T(8,128)(2,1)S(1)} custom-call(s32[2]{0:T(128)S(1)} %add_convert_fusion.1.ends_ref, bf16[4,256,2304]{2,1,0:T(8,128)(2,1)S(1)} %bitcast.139, bf16[4,256,1536]{2,1,0:T(8,128)(2,1)S(1)} %bitcast.141), custom_call_target="tpu_custom_call" | custom-call | flops 3221225472 | bytes 9437184 | tf_op jit(solution)/shard_map/light_attention/pallas_call | solution.py:152
  78.4 1.1 copy-done.6
  79.6 3.1 fusion.58
  82.6 10.8 %all-gather.2.cloned.1.call-done = bf16[4,512,768]{2,1,0:T(8,128)(2,1)} async-done(((bf16[4,64,768]{2,1,0:T(8,128)(2,1)}), bf16[4,512,768]{2,1,0:T(8,128)(2,1)}) %all-gather.2.cloned.1.call-update) | async-done | bytes 3145744 | tf_op jit(solution)/shard_map/all_gather | solution.py:1202
  93.4 2.7 multiply_reduce_fusion
  96.8 0.8 fusion.1
  97.6 5.2 %convolution_convert_fusion = bf16[2048,1536]{1,0:T(8,128)(2,1)S(1)} fusion(bf16[2048,768]{1,0:T(8,128)(2,1)S(1)} %fusion.1, bf16[768,1536]{1,0:T(8,128)(2,1)S(1)} %copy-done), kind=kOutput, calls=%fused_computation | convolution fusion | flops 4834983936 | bytes 11796480 | tf_op jit(solution)/shard_map/dot_general | solution.py:26
  102.9 4.1 %heavy_attention.1 = bf16[4,64,768]{2,1,0:T(8,128)(2,1)S(1)} custom-call(bf16[4,64,768]{2,1,0:T(8,128)(2,1)S(1)} %bitcast.143, bf16[4,512,1536]{2,1,0:T(8,128)(2,1)S(1)} %bitcast.135, f32[4,1,512]{2,1,0:T(1,128)S(1)} %compare_convert_fusion.live_ref), custom_call_target="tpu_custom_call" | custom-call | flops 1610612736 | bytes 7077888 | tf_op jit(solution)/shard_map/heavy_attention/pallas_call | solution.py:299
  107.8 1.6 multiply_reduce_fusion.5
  109.5 0.7 fusion.4
  111.1 0.9 copy-done.15
  112.8 0.9 pad_maximum_fusion.own_rows
  113.6 38.4 %feed_forward.1 = (bf16[1024,1024]{1,0:T(8,128)(2,1)}, bf16[1024,2048]{1,0:T(8,128)(2,1)}, f32[1024,768]{1,0:T(8,128)}, f32[1024,768]{1,0:T(8,128)}, bf16[2,192,...) custom-call(bf16[1024,768]{1,0:T(8,128)(2,1)} %copy-done.21, ...), custom_call_target="tpu_custom_call" | custom-call | flops 16911433728 | bytes 31457280 | tf_op jit(solution)/shard_map/feed_forward/pallas_call | solution.py:578
  152.1 2.5 fusion.7
  154.7 4.1 multiply_reduce_fusion.1
  158.8 3.5 fusion.55
  162.3 2.6 convolution_convert_fusion.8
  165.9 8.7 %heavy_attention_back.1 = (bf16[4,64,768]{2,1,0:T(8,128)(2,1)S(1)}, bf16[4,512,1536]{2,1,0:T(8,128)(2,1)S(1)}) custom-call(bf16[4,64,768]{2,1,0:T(8,128)(2,1)S(1)} %bitcast.144, bf16[4,512,1536]{2,1,0:T(8,128)(2,1)S(1)} %bitcast.138, f32[4,1,512]{2,1,0:T(1,128)S(1)} %compare_convert_fusion.live_ref, bf16[4,64,768]{2,1,0:T(8,128)(2,1)S(1)} %bitcast.146), custom_call_target="tpu_custom_call" | custom-call | flops 4026531840 | bytes 14155776 | tf_op jit(solution)/shard_map/heavy_attention_back/pallas_call | solution.py:343
  174.6 6.5 %convolution_convert_fusion.5 = bf16[2048,768]{1,0:T(8,128)(2,1)} fusion(bf16[2048,1536]{1,0:T(8,128)(2,1)S(1)} %bitcast.147, bf16[768,1536]{1,0:T(8,128)(2,1)S(1)} %copy-done), kind=kOutput, calls=%fused_computation.18 | convolution fusion | flops 4833411072 | bytes 11796480 | tf_op jit(solution)/shard_map/dot_general | solution.py:26
  183.1 1.6 bitcast_convert_fusion.2
  185.1 1.2 fusion.56
  186.3 0.8 copy-done.20
  187.1 2.5 convolution_convert_fusion.10
  189.6 4.0 convolution_convert_fusion.3
  193.6 4.9 %convolution_convert_fusion.4 = bf16[768,2048]{1,0:T(8,128)(2,1)} fusion(bf16[1024,768]{1,0:T(8,128)(2,1)S(1)} %copy-done.23, bf16[1024,2048]{1,0:T(8,128)(2,1)S(1)} %copy-done.58), kind=kOutput, calls=%fused_computation.17 | convolution fusion | flops 3222798336 | bytes 8912896 | tf_op jit(solution)/shard_map/dot_general | solution.py:26
  198.5 6.7 %bitcast_convert_fusion = bf16[768,1536]{1,0:T(8,128)(2,1)} fusion(bf16[4,512,1536]{2,1,0:T(8,128)(2,1)S(1)} %bitcast.149, bf16[4,512,768]{2,1,0:T(8,128)(2,1)S(1)} %copy-done.14, f32[768]{0:T(1024)S(1)} %convert_element_type.161, f32[4,512]{1,0:T(4,128)S(1)} %copy-done.47), kind=kOutput, calls=%fused_computation.10 | convolution fusion | flops 4839309312 | bytes 11807744 | tf_op jit(solution)/shard_map/dot_general | solution.py:26
  205.2 104.2 %reduce_gradients.2 = (f32[24,2048]{1,0:T(8,128)}, f32[24,768]{1,0:T(8,128)}, f32[24,8192]{1,0:T(8,128)}, f32[24,768]{1,0:T(8,128)}, f32[24,1536]{1,0:T(8,128)},...) custom-call(bf16[2,2,4,2,24,2048]{5,4,3,2,1,0:T(8,128)(2,1)} %bitcast.166, ...), custom_call_target="tpu_custom_call" | custom-call | flops 20447232 | bytes 327155712 | tf_op jit(solution)/shard_map/reduce_gradients/pallas_call | solution.py:1081
  309.4 1.6 bitcast_convert_fusion.1
  312.0 2.6 convolution_convert_fusion.6
  314.6 3.1 convolution_convert_fusion.7
  317.7 5.6 %fusion.2 = f32[4,256,768]{2,1,0:T(8,128)} fusion(bf16[4,256,2304]{2,1,0:T(8,128)(2,1)S(1)} %bitcast.162, bf16[768,2304]{1,0:T(8,128)(2,1)S(1)} %copy-done.29), kind=kOutput, calls=%fused_computation.14 | convolution fusion | flops 3623878656 | bytes 11403264 | tf_op jit(solution)/shard_map/dot_general | solution.py:26
  323.3 5.6 %multiply_reduce_fusion.2 = (bf16[768]{0:T(1024)(128)(2,1)S(1)}, f32[4,256]{1,0:T(4,128)S(1)}, f32[4,256,768]{2,1,0:T(8,128)}) fusion(bf16[4,256,768]{2,1,0:T(8,128)(2,1)S(1)} %copy-done.9, f32[4,256]{1,0:T(4,128)S(1)} %get-tuple-element.103, f32[768]{0:T(1024)S(1)} %convert_element_type.161, bf16[4,256,768]{2,1,0:T(8,128)(2,1)} %get-tuple-element.60, ...), kind=kOutput, calls=%fused_computation.30 | convolution fusion | flops 210893056 | bytes 10367488 | tf_op jit(solution)/shard_map/pkt,pkd->ptd/dot_general | solution.py:1383
  329.7 60.5 %reduce_gradients.3 = (f32[24,2304]{1,0:T(8,128)}, f32[8,256]{1,0:T(8,128)}, f32[32,768]{1,0:T(8,128)}, f32[24,768]{1,0:T(8,128)}, f32[128,768]{1,0:T(8,128)}) custom-call(bf16[2,2,4,2,8,256]{5,4,3,2,1,0:T(8,128)(2,1)} %bitcast.180, bf16[2,2,4,2,32,768]{5,4,3,2,1,0:T(8,128)(2,1)} %bitcast.172, bf16[2,2,4,2,24,768]{5,4,3,2,1,0:T(8,128)(2,1)} %bitcast.179, ...), custom_call_target="tpu_custom_call" | custom-call | flops 12713984 | bytes 203423744 | tf_op jit(solution)/shard_map/reduce_gradients/pallas_call | solution.py:1081
  390.3 3.0 copy_outputs.1
  393.2 1.3 slice_bitcast_fusion
  394.5 5.0 %subtract_add_fusion = f32[4,256,768]{2,1,0:T(8,128)} fusion(f32[4,256,768]{2,1,0:T(8,128)} %bitcast.154, bf16[4,256,768]{2,1,0:T(8,128)(2,1)} %param.19, f32[4,256,768]{2,1,0:T(8,128)} %get-tuple-element.111, f32[4,256]{1,0:T(4,128)S(1)} %broadcast_multiply_fusion.1, f32[4,256]{1,0:T(4,128)S(1)} %copy-done.44, f32[768]{0:T(1024)S(1)} %convert_element_type.161, ...), kind=kLoop, calls=%fused_computation.31 | loop fusion | flops 5505024 | bytes 11025408 | tf_op jit(solution)/shard_map/add | solution.py:1387
  (176 shorter events, 10.6 us)
Async XLA Ops:
  7.2 90.4 %copy-start = (bf16[768,1536]{1,0:T(8,128)(2,1)S(1)}, bf16[768,1536]{1,0:T(8,128)(2,1)}, u32[]{:S(2)}) copy-start(bf16[768,1536]{1,0:T(8,128)(2,1)} %param.25) | copy-start | bytes 7077892
  7.2 15.8 %copy-start.45 = (s32[4,64]{1,0:T(4,128)S(1)}, s32[4,64]{1,0:T(4,128)}, u32[]{:S(2)}) copy-start(s32[4,64]{1,0:T(4,128)} %param.35) | copy-start | bytes 3076
  7.2 12.7 %copy-start.49 = (bf16[768]{0:T(1024)(128)(2,1)S(1)}, bf16[768]{0:T(1024)(128)(2,1)}, u32[]{:S(2)}) copy-start(bf16[768]{0:T(1024)(128)(2,1)} %param.21) | copy-start | bytes 4612
  7.2 12.7 %copy-start.50 = (bf16[768]{0:T(1024)(128)(2,1)S(1)}, bf16[768]{0:T(1024)(128)(2,1)}, u32[]{:S(2)}) copy-start(bf16[768]{0:T(1024)(128)(2,1)} %param.27) | copy-start | bytes 4612
  7.2 12.7 %copy-start.51 = (bf16[768]{0:T(1024)(128)(2,1)S(1)}, bf16[768]{0:T(1024)(128)(2,1)}, u32[]{:S(2)}) copy-start(bf16[768]{0:T(1024)(128)(2,1)} %param.28) | copy-start | bytes 4612
  7.2 12.7 %copy-start.48 = (s32[4,256]{1,0:T(4,128)S(1)}, s32[4,256]{1,0:T(4,128)}, u32[]{:S(2)}) copy-start(s32[4,256]{1,0:T(4,128)} %param.37) | copy-start | bytes 12292
  7.2 12.8 %copy-start.52 = (s32[4,8]{1,0:T(4,128)S(1)}, s32[4,8]{1,0:T(4,128)}, u32[]{:S(2)}) copy-start(s32[4,8]{1,0:T(4,128)} %param.36) | copy-start | bytes 388
  7.3 15.0 %copy-start.55 = (s32[4,1]{0,1:T(1,128)S(1)}, s32[4,1]{0,1:T(1,128)}, u32[]{:S(2)}) copy-start(s32[4,1]{0,1:T(1,128)} %param.34) | copy-start | bytes 52
  7.3 86.2 %all-gather.2.cloned.1.call-start = ((), (), s32[]{:S(2)}) async-start(), calls=%async_computation.1 | async-start | bytes 3538944 | tf_op jit(solution)/shard_map/all_gather | solution.py:1202
  10.1 313.2 %reduce-scatter.2.cloned.1.call-start = ((), (), s32[]{:S(2)}) async-start(), calls=%async_computation.2 | async-start | bytes 3538944 | tf_op jit(solution)/shard_map/reduce_scatter | solution.py:1338
  12.7 13.0 %copy-start.42 = (s32[4,64]{1,0:T(4,128)S(1)}, s32[4,64]{1,0:T(4,128)}, u32[]{:S(2)}) copy-start(s32[4,64]{1,0:T(4,128)} %param.33) | copy-start | bytes 3076
  12.7 43.2 %collective-permute-start = (bf16[4,128,768]{2,1,0:T(8,128)(2,1)}, bf16[4,128,768]{2,1,0:T(8,128)(2,1)}, u32[]{:S(2)}, u32[]{:S(2)}) collective-permute-start(bf16[4,128,768]{2,1,0:T(8,128)(2,1)} %get-tuple-element.95), channel_id=1, source_target_pairs={{0,1},{1,2},{2,3},{3,4},{4,5},{5,6},{6,7},{8,9},{9,10},{10,11},{11... | collective-permute-start | bytes 2359304 | tf_op jit(solution)/shard_map/ppermute | solution.py:1190
  18.6 37.3 %collective-permute-start.1 = (bf16[4,128,768]{2,1,0:T(8,128)(2,1)}, bf16[4,128,768]{2,1,0:T(8,128)(2,1)}, u32[]{:S(2)}, u32[]{:S(2)}) collective-permute-start(bf16[4,128,768]{2,1,0:T(8,128)(2,1)} %get-tuple-element.96), channel_id=1, source_target_pairs={{1,0},{2,1},{3,2},{4,3},{5,4},{6,5},{7,6},{9,8},{10,9},{11,10},{12... | collective-permute-start | bytes 2359304 | tf_op jit(solution)/shard_map/ppermute | solution.py:1193
  20.3 5.9 %copy-start.26 = (bf16[768,768]{1,0:T(8,128)(2,1)S(1)}, bf16[768,768]{1,0:T(8,128)(2,1)}, u32[]{:S(2)}) copy-start(bf16[768,768]{1,0:T(8,128)(2,1)} %param.24) | copy-start | bytes 3538948
  23.7 2.9 copy-start.28
  25.7 5.2 %copy-start.12 = (bf16[4,256,768]{2,1,0:T(8,128)(2,1)}, bf16[4,256,768]{2,1,0:T(8,128)(2,1)S(1)}, u32[]{:S(2)}) copy-start(bf16[4,256,768]{2,1,0:T(8,128)(2,1)S(1)} %multiply_convert_fusion.3) | copy-start | bytes 4718596
  26.2 4.8 %copy-start.33 = (bf16[4,64,768]{2,1,0:T(8,128)(2,1)}, bf16[4,64,768]{2,1,0:T(8,128)(2,1)S(1)}, u32[]{:S(2)}) copy-start(bf16[4,64,768]{2,1,0:T(8,128)(2,1)S(1)} %convolution_convert_fusion.13) | copy-start | bytes 1179652
  31.0 31.6 %copy-start.3 = (bf16[1024,2304]{1,0:T(8,128)(2,1)}, bf16[1024,2304]{1,0:T(8,128)(2,1)S(1)}, u32[]{:S(2)}) copy-start(bf16[1024,2304]{1,0:T(8,128)(2,1)S(1)} %convolution_convert_fusion.1) | copy-start | bytes 14155780
  62.5 15.9 %copy-start.4 = (bf16[1024,1536]{1,0:T(8,128)(2,1)}, bf16[1024,1536]{1,0:T(8,128)(2,1)S(1)}, u32[]{:S(2)}) copy-start(bf16[1024,1536]{1,0:T(8,128)(2,1)S(1)} %convolution_convert_fusion.2) | copy-start | bytes 9437188
  62.5 17.0 %copy-start.53 = (bf16[768,768]{1,0:T(8,128)(2,1)S(1)}, bf16[768,768]{1,0:T(8,128)(2,1)}, u32[]{:S(2)}) copy-start(bf16[768,768]{1,0:T(8,128)(2,1)} %param.23) | copy-start | bytes 3538948
  93.4 3.4 copy-start.13
  102.8 4.2 %copy-start.2 = (bf16[2048,1536]{1,0:T(8,128)(2,1)}, bf16[2048,1536]{1,0:T(8,128)(2,1)S(1)}, u32[]{:S(2)}) copy-start(bf16[2048,1536]{1,0:T(8,128)(2,1)S(1)} %convolution_convert_fusion) | copy-start | bytes 18874372
  102.8 4.7 %copy-start.8 = (bf16[4,256,768]{2,1,0:T(8,128)(2,1)S(1)}, bf16[4,256,768]{2,1,0:T(8,128)(2,1)}, u32[]{:S(2)}) copy-start(bf16[4,256,768]{2,1,0:T(8,128)(2,1)} %param.19) | copy-start | bytes 4718596
  102.8 4.7 %copy-start.24 = (bf16[768,768]{1,0:T(8,128)(2,1)S(1)}, bf16[768,768]{1,0:T(8,128)(2,1)}, u32[]{:S(2)}) copy-start(bf16[768,768]{1,0:T(8,128)(2,1)} %param.26) | copy-start | bytes 3538948
  102.8 5.0 %copy-start.31 = (f32[1024,768]{1,0:T(8,128)S(1)}, f32[1024,768]{1,0:T(8,128)}, u32[]{:S(2)}) copy-start(f32[1024,768]{1,0:T(8,128)} %fusion.58) | copy-start | bytes 9437188
  154.6 4.1 %copy-start.40 = (f32[1024]{0:T(1024)}, f32[1024]{0:T(1024)S(1)}, u32[]{:S(2)}) copy-start(f32[1024]{0:T(1024)S(1)} %subtract_multiply_fusion) | copy-start | bytes 12292
  154.7 4.1 %copy-start.16 = (bf16[4,256,768]{2,1,0:T(8,128)(2,1)S(1)}, bf16[4,256,768]{2,1,0:T(8,128)(2,1)}, u32[]{:S(2)}) copy-start(bf16[4,256,768]{2,1,0:T(8,128)(2,1)} %param.20) | copy-start | bytes 4718596
  154.7 4.1 %copy-start.30 = (f32[1024,768]{1,0:T(8,128)S(1)}, f32[1024,768]{1,0:T(8,128)}, u32[]{:S(2)}) copy-start(f32[1024,768]{1,0:T(8,128)} %get-tuple-element.49) | copy-start | bytes 9437188
  154.7 11.2 %slice-start = ((s8[6291456]{0:T(1024)(128)(4,1)}), s8[4194304]{0:T(1024)(128)(4,1)S(1)}, s32[]{:S(2)}) async-start(s8[6291456]{0:T(1024)(128)(4,1)} %bitcast.136), calls=%async_computation.3 | async-start | bytes 8388608
  158.8 3.5 copy-start.54
  158.8 7.1 %slice-start.1 = ((s8[6291456]{0:T(1024)(128)(4,1)}), s8[2097152]{0:T(1024)(128)(4,1)S(1)}, s32[]{:S(2)}) async-start(s8[6291456]{0:T(1024)(128)(4,1)} %bitcast.136), calls=%async_computation.4 | async-start | bytes 4194304
  162.3 3.1 copy-start.25
  165.4 9.2 %copy-start.35 = (bf16[4,64,768]{2,1,0:T(8,128)(2,1)}, bf16[4,64,768]{2,1,0:T(8,128)(2,1)S(1)}, u32[]{:S(2)}) copy-start(bf16[4,64,768]{2,1,0:T(8,128)(2,1)S(1)} %convolution_convert_fusion.11) | copy-start | bytes 1179652
  174.6 6.5 %copy-start.5 = (bf16[4,512,1536]{2,1,0:T(8,128)(2,1)}, bf16[4,512,1536]{2,1,0:T(8,128)(2,1)S(1)}, u32[]{:S(2)}) copy-start(bf16[4,512,1536]{2,1,0:T(8,128)(2,1)S(1)} %get-tuple-element.56) | copy-start | bytes 18874372
  187.1 11.4 %slice-start.2 = ((s8[6291456]{0:T(1024)(128)(4,1)}), s8[4194304]{0:T(1024)(128)(4,1)S(1)}, s32[]{:S(2)}) async-start(s8[6291456]{0:T(1024)(128)(4,1)} %bitcast.148), calls=%async_computation.5 | async-start | bytes 8388608
  189.6 4.1 copy-start.23
  189.6 4.1 copy-start.58
  189.6 8.9 %slice-start.3 = ((s8[6291456]{0:T(1024)(128)(4,1)}), s8[2097152]{0:T(1024)(128)(4,1)S(1)}, s32[]{:S(2)}) async-start(s8[6291456]{0:T(1024)(128)(4,1)} %bitcast.148), calls=%async_computation.6 | async-start | bytes 4194304
  193.6 4.9 %copy-start.14 = (bf16[4,512,768]{2,1,0:T(8,128)(2,1)S(1)}, bf16[4,512,768]{2,1,0:T(8,128)(2,1)}, u32[]{:S(2)}) copy-start(bf16[4,512,768]{2,1,0:T(8,128)(2,1)} %all-gather.2.cloned.1.call-done) | copy-start | bytes 9437188
  193.6 4.9 %copy-start.47 = (f32[4,512]{1,0:T(4,128)S(1)}, f32[4,512]{1,0:T(4,128)}, u32[]{:S(2)}) copy-start(f32[4,512]{1,0:T(4,128)} %get-tuple-element.100) | copy-start | bytes 24580
  205.2 104.2 %copy-start.36 = (bf16[4,64,768]{2,1,0:T(8,128)(2,1)S(1)}, bf16[4,64,768]{2,1,0:T(8,128)(2,1)}, u32[]{:S(2)}) copy-start(bf16[4,64,768]{2,1,0:T(8,128)(2,1)} %copy-done.35) | copy-start | bytes 1179652
  312.0 5.7 %slice-start.4 = ((s8[4718592]{0:T(1024)(128)(4,1)}), s8[4194304]{0:T(1024)(128)(4,1)S(1)}, s32[]{:S(2)}) async-start(s8[4718592]{0:T(1024)(128)(4,1)} %bitcast.161), calls=%async_computation.7 | async-start | bytes 8388608
  314.6 3.1 slice-start.5
  314.6 3.1 copy-start.29
  317.7 5.6 %copy-start.9 = (bf16[4,256,768]{2,1,0:T(8,128)(2,1)S(1)}, bf16[4,256,768]{2,1,0:T(8,128)(2,1)}, u32[]{:S(2)}) copy-start(bf16[4,256,768]{2,1,0:T(8,128)(2,1)} %param.19) | copy-start | bytes 4718596
  317.7 5.6 %copy-start.39 = (pred[4,64,256]{1,2,0:T(32,128)(4,1)S(1)}, pred[4,64,256]{1,2,0:T(32,128)(4,1)}, u32[]{:S(2)}) copy-start(pred[4,64,256]{1,2,0:T(32,128)(4,1)} %iota_compare_fusion.5) | copy-start | bytes 196612
  329.7 64.8 %copy-start.44 = (f32[4,256]{1,0:T(4,128)S(1)}, f32[4,256]{1,0:T(4,128)}, u32[]{:S(2)}) copy-start(f32[4,256]{1,0:T(4,128)} %get-tuple-element.102) | copy-start | bytes 12292
  394.5 5.0 %copy-start.1 = (bf16[768,1536]{1,0:T(8,128)(2,1)S(1)}, bf16[768,1536]{1,0:T(8,128)(2,1)}, u32[]{:S(2)}) copy-start(bf16[768,1536]{1,0:T(8,128)(2,1)} %param.25) | copy-start | bytes 7077892
  (22 other events, 45.1 us)
Sparse Core Ops, SparseCore 0:
  10.9 82.5 all-gather.1
  181.3 88.2 reduce-scatter.1

commit v6 on v5

--- a/solution.py
+++ b/solution.py
@@ -1349,8 +1349,7 @@
         ]
         half = light_gates_grad.shape[1] // 2
         jobs = [
-            ("xy", 0, 0, 512, half // 512, 0, 0),
-            ("yx", 0, half, 512, half // 512, 0, half),
+            ("xy", 0, 0, 512, 2 * half // 512, 0, 0),
             ("xy", 1, 0, 384, D // 384, 1, 0),
             ("gates", 2, 0, 256, share // 256, 2, 0),
             ("gates", 2, share, 256, share // 256, 2, wide),

time: 410 us -> 406 us (level)
  transfers between devices with their start and end apart: 4 -> 4, of which waited for: 2 -> 2; matrix products, arithmetic and copies ran while one was open for 14% -> 14% of each run, Pallas kernels for 30% -> 29%
where the time goes in v6:
time: 406 us; the launch traced here: 403 us
  Pallas kernels  231 us (57%)
  matrix products  77.7 us (19%)
  waiting for transfers between devices  35.7 us (9%)
  other arithmetic  23.9 us (6%)
  between operations  15.2 us (4%)
  local copies, waits for them, and re-layouts  12.1 us (3%)
  starting transfers between devices  7.24 us (2%)
    pallas_call x2, Pallas kernels, reduce_all(): pl.pallas_call(functools.partial(reduce_kernel, tuple(jobs), (len(values)...  161 us
    dot_general x23, matrix products, dot(): lax.dot_general(left, right, (over, ((), ())), preferred_element_type=f32)  68 us
    pallas_call x1, Pallas kernels, feed_forward(): pl.pallas_call(functools.partial(feed_kernel, n_y), out_shape=[jax.ShapeD...  38.4 us
    ppermute x1, waiting for transfers between devices, per_device(): lax.ppermute(layer_input[:, tokens - RADIUS:], 'seq', [(i, i + 1) for i i...  24.9 us
    pallas_call x1, Pallas kernels, light_attention(): pl.pallas_call(light_kernel, out_shape=jax.ShapeDtypeStruct((pieces, toke...  15.9 us
    all_gather x1, waiting for transfers between devices, per_device(): key_all = lax.all_gather(key_raw, 'seq', axis=1, tiled=True)  10.8 us
    pallas_call x1, Pallas kernels, heavy_attention_back(): pl.pallas_call(heavy_back_kernel, out_shape=[jax.ShapeDtypeStruct((pieces...  8.66 us
  transfers between devices with their start and end apart: 4, of which 2 were waited for; matrix products, arithmetic and copies ran while one was open for 14% of the time, Pallas kernels for 29%

profile of v6, /device:TPU:0, one launch (start us, length us, event | category | flops | bytes accessed | tf_op | source)
XLA Modules:
  0.0 402.6 jit_solution(4238055750103221908)
XLA Ops:
  7.3 2.7 convolution_convert_fusion.12
  10.1 2.6 fusion.57
  12.7 5.9 %collective-permute-start = (bf16[4,128,768]{2,1,0:T(8,128)(2,1)}, bf16[4,128,768]{2,1,0:T(8,128)(2,1)}, u32[]{:S(2)}, u32[]{:S(2)}) collective-permute-start(bf16[4,128,768]{2,1,0:T(8,128)(2,1)} %get-tuple-element.95), channel_id=1, source_target_pairs={{0,1},{1,2},{2,3},{3,4},{4,5},{5,6},{6,7},{8,9},{9,10},{10,11},{11... | collective-permute-start | bytes 2359304 | tf_op jit(solution)/shard_map/ppermute | solution.py:1190
  18.6 1.3 collective-permute-start.1
  20.3 2.0 multiply_reduce_fusion.7
  23.0 0.7 iota_compare_fusion.5
  23.7 2.0 multiply_convert_fusion.3
  26.7 4.3 %convolution_convert_fusion.1 = bf16[1024,2304]{1,0:T(8,128)(2,1)S(1)} fusion(bf16[1024,768]{1,0:T(8,128)(2,1)S(1)} %bitcast.152, bf16[768,2304]{1,0:T(8,128)(2,1)S(1)} %copy-done.28), kind=kOutput, calls=%fused_computation.6 | convolution fusion | flops 3626237952 | bytes 9830400 | tf_op jit(solution)/shard_map/dot_general | solution.py:26
  31.0 24.9 %collective-permute-done = bf16[4,128,768]{2,1,0:T(8,128)(2,1)} collective-permute-done((bf16[4,128,768]{2,1,0:T(8,128)(2,1)}, bf16[4,128,768]{2,1,0:T(8,128)(2,1)}, u32[]{:S(2)}, u32[]{:S(2)}) %collective-permute-start) | collective-permute-done | bytes 786464 | tf_op jit(solution)/shard_map/ppermute | solution.py:1190
  55.9 1.8 multiply_reduce_fusion.6
  57.7 1.6 maximum_convert_fusion
  59.7 2.8 convolution_convert_fusion.2
  62.6 15.9 %light_attention.1 = bf16[4,256,768]{2,1,0:T(8,128)(2,1)S(1)} custom-call(s32[2]{0:T(128)S(1)} %add_convert_fusion.1.ends_ref, bf16[4,256,2304]{2,1,0:T(8,128)(2,1)S(1)} %bitcast.139, bf16[4,256,1536]{2,1,0:T(8,128)(2,1)S(1)} %bitcast.141), custom_call_target="tpu_custom_call" | custom-call | flops 3221225472 | bytes 9437184 | tf_op jit(solution)/shard_map/light_attention/pallas_call | solution.py:152
  78.4 1.1 copy-done.6
  79.6 3.1 fusion.58
  82.6 10.8 %all-gather.2.cloned.1.call-done = bf16[4,512,768]{2,1,0:T(8,128)(2,1)} async-done(((bf16[4,64,768]{2,1,0:T(8,128)(2,1)}), bf16[4,512,768]{2,1,0:T(8,128)(2,1)}) %all-gather.2.cloned.1.call-update) | async-done | bytes 3145744 | tf_op jit(solution)/shard_map/all_gather | solution.py:1202
  93.4 2.7 multiply_reduce_fusion
  96.8 0.8 fusion.1
  97.6 5.2 %convolution_convert_fusion = bf16[2048,1536]{1,0:T(8,128)(2,1)S(1)} fusion(bf16[2048,768]{1,0:T(8,128)(2,1)S(1)} %fusion.1, bf16[768,1536]{1,0:T(8,128)(2,1)S(1)} %copy-done), kind=kOutput, calls=%fused_computation | convolution fusion | flops 4834983936 | bytes 11796480 | tf_op jit(solution)/shard_map/dot_general | solution.py:26
  102.9 4.1 %heavy_attention.1 = bf16[4,64,768]{2,1,0:T(8,128)(2,1)S(1)} custom-call(bf16[4,64,768]{2,1,0:T(8,128)(2,1)S(1)} %bitcast.143, bf16[4,512,1536]{2,1,0:T(8,128)(2,1)S(1)} %bitcast.135, f32[4,1,512]{2,1,0:T(1,128)S(1)} %compare_convert_fusion.live_ref), custom_call_target="tpu_custom_call" | custom-call | flops 1610612736 | bytes 7077888 | tf_op jit(solution)/shard_map/heavy_attention/pallas_call | solution.py:299
  107.8 1.6 multiply_reduce_fusion.5
  109.5 0.7 fusion.4
  111.1 0.9 copy-done.15
  112.8 0.9 pad_maximum_fusion.own_rows
  113.6 38.4 %feed_forward.1 = (bf16[1024,1024]{1,0:T(8,128)(2,1)}, bf16[1024,2048]{1,0:T(8,128)(2,1)}, f32[1024,768]{1,0:T(8,128)}, f32[1024,768]{1,0:T(8,128)}, bf16[2,192,...) custom-call(bf16[1024,768]{1,0:T(8,128)(2,1)} %copy-done.21, ...), custom_call_target="tpu_custom_call" | custom-call | flops 16911433728 | bytes 31457280 | tf_op jit(solution)/shard_map/feed_forward/pallas_call | solution.py:578
  152.1 2.5 fusion.7
  154.7 4.1 %multiply_reduce_fusion.1 = (bf16[768]{0:T(1024)(128)(2,1)}, f32[1024]{0:T(1024)S(1)}, f32[1024,768]{1,0:T(8,128)S(1)}) fusion(f32[1024,768]{1,0:T(8,128)S(1)} %copy-done.11, f32[1024]{0:T(1024)S(1)} %get-tuple-element.105, f32[768]{0:T(1024)S(1)} %convert_element_type.180, f32[768]{0:T(1024)S(1)} %convert_element_type.184, ...), kind=kOutput, calls=%fused_computation.29 | convolution fusion | flops 309262592 | bytes 9758208 | tf_op jit(solution)/shard_map/dot_general | solution.py:26
  158.8 3.5 fusion.55
  162.3 2.6 convolution_convert_fusion.8
  165.9 8.7 %heavy_attention_back.1 = (bf16[4,64,768]{2,1,0:T(8,128)(2,1)S(1)}, bf16[4,512,1536]{2,1,0:T(8,128)(2,1)S(1)}) custom-call(bf16[4,64,768]{2,1,0:T(8,128)(2,1)S(1)} %bitcast.144, bf16[4,512,1536]{2,1,0:T(8,128)(2,1)S(1)} %bitcast.138, f32[4,1,512]{2,1,0:T(1,128)S(1)} %compare_convert_fusion.live_ref, bf16[4,64,768]{2,1,0:T(8,128)(2,1)S(1)} %bitcast.146), custom_call_target="tpu_custom_call" | custom-call | flops 4026531840 | bytes 14155776 | tf_op jit(solution)/shard_map/heavy_attention_back/pallas_call | solution.py:343
  174.6 6.5 %convolution_convert_fusion.5 = bf16[2048,768]{1,0:T(8,128)(2,1)} fusion(bf16[2048,1536]{1,0:T(8,128)(2,1)S(1)} %bitcast.147, bf16[768,1536]{1,0:T(8,128)(2,1)S(1)} %copy-done), kind=kOutput, calls=%fused_computation.18 | convolution fusion | flops 4833411072 | bytes 11796480 | tf_op jit(solution)/shard_map/dot_general | solution.py:26
  183.1 1.6 bitcast_convert_fusion.2
  185.1 1.2 fusion.56
  186.3 0.8 copy-done.20
  187.1 2.5 convolution_convert_fusion.10
  189.6 4.0 %convolution_convert_fusion.3 = bf16[768,2048]{1,0:T(8,128)(2,1)} fusion(bf16[768,768]{1,0:T(8,128)(2,1)S(1)} %bitcast.178, bf16[768,2048]{1,0:T(8,128)(2,1)S(1)} %bitcast.189), kind=kOutput, calls=%fused_computation.16 | convolution fusion | flops 2417491968 | bytes 7471104 | tf_op jit(solution)/shard_map/dot_general | solution.py:26
  193.6 4.9 %convolution_convert_fusion.4 = bf16[768,2048]{1,0:T(8,128)(2,1)} fusion(bf16[1024,768]{1,0:T(8,128)(2,1)S(1)} %copy-done.23, bf16[1024,2048]{1,0:T(8,128)(2,1)S(1)} %copy-done.58), kind=kOutput, calls=%fused_computation.17 | convolution fusion | flops 3222798336 | bytes 8912896 | tf_op jit(solution)/shard_map/dot_general | solution.py:26
  198.5 6.7 %bitcast_convert_fusion = bf16[768,1536]{1,0:T(8,128)(2,1)} fusion(bf16[4,512,1536]{2,1,0:T(8,128)(2,1)S(1)} %bitcast.149, bf16[4,512,768]{2,1,0:T(8,128)(2,1)S(1)} %copy-done.14, f32[768]{0:T(1024)S(1)} %convert_element_type.161, f32[4,512]{1,0:T(4,128)S(1)} %copy-done.47), kind=kOutput, calls=%fused_computation.10 | convolution fusion | flops 4839309312 | bytes 11807744 | tf_op jit(solution)/shard_map/dot_general | solution.py:26
  205.2 100.6 %reduce_gradients.2 = (f32[24,2048]{1,0:T(8,128)}, f32[24,768]{1,0:T(8,128)}, f32[24,8192]{1,0:T(8,128)}, f32[24,768]{1,0:T(8,128)}, f32[24,1536]{1,0:T(8,128)},...) custom-call(bf16[2,2,4,2,24,2048]{5,4,3,2,1,0:T(8,128)(2,1)} %bitcast.166, ...), custom_call_target="tpu_custom_call" | custom-call | flops 20447232 | bytes 327155712 | tf_op jit(solution)/shard_map/reduce_gradients/pallas_call | solution.py:1081
  305.9 1.6 bitcast_convert_fusion.1
  308.4 2.6 convolution_convert_fusion.6
  311.1 3.1 convolution_convert_fusion.7
  314.2 5.6 %fusion.2 = f32[4,256,768]{2,1,0:T(8,128)} fusion(bf16[4,256,2304]{2,1,0:T(8,128)(2,1)S(1)} %bitcast.162, bf16[768,2304]{1,0:T(8,128)(2,1)S(1)} %copy-done.29), kind=kOutput, calls=%fused_computation.14 | convolution fusion | flops 3623878656 | bytes 11403264 | tf_op jit(solution)/shard_map/dot_general | solution.py:26
  319.7 5.6 %multiply_reduce_fusion.2 = (bf16[768]{0:T(1024)(128)(2,1)S(1)}, f32[4,256]{1,0:T(4,128)S(1)}, f32[4,256,768]{2,1,0:T(8,128)}) fusion(bf16[4,256,768]{2,1,0:T(8,128)(2,1)S(1)} %copy-done.9, f32[4,256]{1,0:T(4,128)S(1)} %get-tuple-element.103, f32[768]{0:T(1024)S(1)} %convert_element_type.161, bf16[4,256,768]{2,1,0:T(8,128)(2,1)} %get-tuple-element.60, ...), kind=kOutput, calls=%fused_computation.30 | convolution fusion | flops 210893056 | bytes 10367488 | tf_op jit(solution)/shard_map/pkt,pkd->ptd/dot_general | solution.py:1382
  326.2 60.0 %reduce_gradients.3 = (f32[24,2304]{1,0:T(8,128)}, f32[8,256]{1,0:T(8,128)}, f32[32,768]{1,0:T(8,128)}, f32[24,768]{1,0:T(8,128)}, f32[128,768]{1,0:T(8,128)}) custom-call(bf16[2,2,4,2,8,256]{5,4,3,2,1,0:T(8,128)(2,1)} %bitcast.180, bf16[2,2,4,2,32,768]{5,4,3,2,1,0:T(8,128)(2,1)} %bitcast.172, bf16[2,2,4,2,24,768]{5,4,3,2,1,0:T(8,128)(2,1)} %bitcast.179, ...), custom_call_target="tpu_custom_call" | custom-call | flops 12713984 | bytes 203423744 | tf_op jit(solution)/shard_map/reduce_gradients/pallas_call | solution.py:1081
  386.2 3.0 copy_outputs.1
  389.1 1.3 slice_bitcast_fusion
  390.5 5.0 %subtract_add_fusion = f32[4,256,768]{2,1,0:T(8,128)} fusion(f32[4,256,768]{2,1,0:T(8,128)} %bitcast.154, bf16[4,256,768]{2,1,0:T(8,128)(2,1)} %param.19, f32[4,256,768]{2,1,0:T(8,128)} %get-tuple-element.111, f32[4,256]{1,0:T(4,128)S(1)} %broadcast_multiply_fusion.1, f32[4,256]{1,0:T(4,128)S(1)} %copy-done.44, f32[768]{0:T(1024)S(1)} %convert_element_type.161, ...), kind=kLoop, calls=%fused_computation.31 | loop fusion | flops 5505024 | bytes 11025408 | tf_op jit(solution)/shard_map/add | solution.py:1386
  (176 shorter events, 10.6 us)
Async XLA Ops:
  7.2 90.4 %copy-start = (bf16[768,1536]{1,0:T(8,128)(2,1)S(1)}, bf16[768,1536]{1,0:T(8,128)(2,1)}, u32[]{:S(2)}) copy-start(bf16[768,1536]{1,0:T(8,128)(2,1)} %param.25) | copy-start | bytes 7077892
  7.2 15.8 %copy-start.45 = (s32[4,64]{1,0:T(4,128)S(1)}, s32[4,64]{1,0:T(4,128)}, u32[]{:S(2)}) copy-start(s32[4,64]{1,0:T(4,128)} %param.35) | copy-start | bytes 3076
  7.2 12.7 %copy-start.49 = (bf16[768]{0:T(1024)(128)(2,1)S(1)}, bf16[768]{0:T(1024)(128)(2,1)}, u32[]{:S(2)}) copy-start(bf16[768]{0:T(1024)(128)(2,1)} %param.21) | copy-start | bytes 4612
  7.2 12.7 %copy-start.50 = (bf16[768]{0:T(1024)(128)(2,1)S(1)}, bf16[768]{0:T(1024)(128)(2,1)}, u32[]{:S(2)}) copy-start(bf16[768]{0:T(1024)(128)(2,1)} %param.27) | copy-start | bytes 4612
  7.2 12.7 %copy-start.51 = (bf16[768]{0:T(1024)(128)(2,1)S(1)}, bf16[768]{0:T(1024)(128)(2,1)}, u32[]{:S(2)}) copy-start(bf16[768]{0:T(1024)(128)(2,1)} %param.28) | copy-start | bytes 4612
  7.2 12.7 %copy-start.48 = (s32[4,256]{1,0:T(4,128)S(1)}, s32[4,256]{1,0:T(4,128)}, u32[]{:S(2)}) copy-start(s32[4,256]{1,0:T(4,128)} %param.37) | copy-start | bytes 12292
  7.2 12.8 %copy-start.52 = (s32[4,8]{1,0:T(4,128)S(1)}, s32[4,8]{1,0:T(4,128)}, u32[]{:S(2)}) copy-start(s32[4,8]{1,0:T(4,128)} %param.36) | copy-start | bytes 388
  7.3 15.0 %copy-start.55 = (s32[4,1]{0,1:T(1,128)S(1)}, s32[4,1]{0,1:T(1,128)}, u32[]{:S(2)}) copy-start(s32[4,1]{0,1:T(1,128)} %param.34) | copy-start | bytes 52
  7.3 86.2 %all-gather.2.cloned.1.call-start = ((), (), s32[]{:S(2)}) async-start(), calls=%async_computation.1 | async-start | bytes 3538944 | tf_op jit(solution)/shard_map/all_gather | solution.py:1202
  10.1 309.7 %reduce-scatter.2.cloned.1.call-start = ((), (), s32[]{:S(2)}) async-start(), calls=%async_computation.2 | async-start | bytes 3538944 | tf_op jit(solution)/shard_map/reduce_scatter | solution.py:1338
  12.7 13.0 %copy-start.42 = (s32[4,64]{1,0:T(4,128)S(1)}, s32[4,64]{1,0:T(4,128)}, u32[]{:S(2)}) copy-start(s32[4,64]{1,0:T(4,128)} %param.33) | copy-start | bytes 3076
  12.7 43.2 %collective-permute-start = (bf16[4,128,768]{2,1,0:T(8,128)(2,1)}, bf16[4,128,768]{2,1,0:T(8,128)(2,1)}, u32[]{:S(2)}, u32[]{:S(2)}) collective-permute-start(bf16[4,128,768]{2,1,0:T(8,128)(2,1)} %get-tuple-element.95), channel_id=1, source_target_pairs={{0,1},{1,2},{2,3},{3,4},{4,5},{5,6},{6,7},{8,9},{9,10},{10,11},{11... | collective-permute-start | bytes 2359304 | tf_op jit(solution)/shard_map/ppermute | solution.py:1190
  18.6 37.3 %collective-permute-start.1 = (bf16[4,128,768]{2,1,0:T(8,128)(2,1)}, bf16[4,128,768]{2,1,0:T(8,128)(2,1)}, u32[]{:S(2)}, u32[]{:S(2)}) collective-permute-start(bf16[4,128,768]{2,1,0:T(8,128)(2,1)} %get-tuple-element.96), channel_id=1, source_target_pairs={{1,0},{2,1},{3,2},{4,3},{5,4},{6,5},{7,6},{9,8},{10,9},{11,10},{12... | collective-permute-start | bytes 2359304 | tf_op jit(solution)/shard_map/ppermute | solution.py:1193
  20.3 5.9 %copy-start.26 = (bf16[768,768]{1,0:T(8,128)(2,1)S(1)}, bf16[768,768]{1,0:T(8,128)(2,1)}, u32[]{:S(2)}) copy-start(bf16[768,768]{1,0:T(8,128)(2,1)} %param.24) | copy-start | bytes 3538948
  23.7 2.9 copy-start.28
  25.7 5.2 %copy-start.12 = (bf16[4,256,768]{2,1,0:T(8,128)(2,1)}, bf16[4,256,768]{2,1,0:T(8,128)(2,1)S(1)}, u32[]{:S(2)}) copy-start(bf16[4,256,768]{2,1,0:T(8,128)(2,1)S(1)} %multiply_convert_fusion.3) | copy-start | bytes 4718596
  26.2 4.8 %copy-start.33 = (bf16[4,64,768]{2,1,0:T(8,128)(2,1)}, bf16[4,64,768]{2,1,0:T(8,128)(2,1)S(1)}, u32[]{:S(2)}) copy-start(bf16[4,64,768]{2,1,0:T(8,128)(2,1)S(1)} %convolution_convert_fusion.13) | copy-start | bytes 1179652
  31.0 31.6 %copy-start.3 = (bf16[1024,2304]{1,0:T(8,128)(2,1)}, bf16[1024,2304]{1,0:T(8,128)(2,1)S(1)}, u32[]{:S(2)}) copy-start(bf16[1024,2304]{1,0:T(8,128)(2,1)S(1)} %convolution_convert_fusion.1) | copy-start | bytes 14155780
  62.5 15.9 %copy-start.4 = (bf16[1024,1536]{1,0:T(8,128)(2,1)}, bf16[1024,1536]{1,0:T(8,128)(2,1)S(1)}, u32[]{:S(2)}) copy-start(bf16[1024,1536]{1,0:T(8,128)(2,1)S(1)} %convolution_convert_fusion.2) | copy-start | bytes 9437188
  62.5 17.0 %copy-start.53 = (bf16[768,768]{1,0:T(8,128)(2,1)S(1)}, bf16[768,768]{1,0:T(8,128)(2,1)}, u32[]{:S(2)}) copy-start(bf16[768,768]{1,0:T(8,128)(2,1)} %param.23) | copy-start | bytes 3538948
  93.4 3.4 copy-start.13
  102.8 4.2 %copy-start.2 = (bf16[2048,1536]{1,0:T(8,128)(2,1)}, bf16[2048,1536]{1,0:T(8,128)(2,1)S(1)}, u32[]{:S(2)}) copy-start(bf16[2048,1536]{1,0:T(8,128)(2,1)S(1)} %convolution_convert_fusion) | copy-start | bytes 18874372
  102.8 4.7 %copy-start.8 = (bf16[4,256,768]{2,1,0:T(8,128)(2,1)S(1)}, bf16[4,256,768]{2,1,0:T(8,128)(2,1)}, u32[]{:S(2)}) copy-start(bf16[4,256,768]{2,1,0:T(8,128)(2,1)} %param.19) | copy-start | bytes 4718596
  102.8 4.7 %copy-start.24 = (bf16[768,768]{1,0:T(8,128)(2,1)S(1)}, bf16[768,768]{1,0:T(8,128)(2,1)}, u32[]{:S(2)}) copy-start(bf16[768,768]{1,0:T(8,128)(2,1)} %param.26) | copy-start | bytes 3538948
  102.8 5.0 %copy-start.31 = (f32[1024,768]{1,0:T(8,128)S(1)}, f32[1024,768]{1,0:T(8,128)}, u32[]{:S(2)}) copy-start(f32[1024,768]{1,0:T(8,128)} %fusion.58) | copy-start | bytes 9437188
  154.6 4.1 %copy-start.40 = (f32[1024]{0:T(1024)}, f32[1024]{0:T(1024)S(1)}, u32[]{:S(2)}) copy-start(f32[1024]{0:T(1024)S(1)} %subtract_multiply_fusion) | copy-start | bytes 12292
  154.7 4.1 %copy-start.16 = (bf16[4,256,768]{2,1,0:T(8,128)(2,1)S(1)}, bf16[4,256,768]{2,1,0:T(8,128)(2,1)}, u32[]{:S(2)}) copy-start(bf16[4,256,768]{2,1,0:T(8,128)(2,1)} %param.20) | copy-start | bytes 4718596
  154.7 4.1 %copy-start.30 = (f32[1024,768]{1,0:T(8,128)S(1)}, f32[1024,768]{1,0:T(8,128)}, u32[]{:S(2)}) copy-start(f32[1024,768]{1,0:T(8,128)} %get-tuple-element.49) | copy-start | bytes 9437188
  154.7 11.2 %slice-start = ((s8[6291456]{0:T(1024)(128)(4,1)}), s8[4194304]{0:T(1024)(128)(4,1)S(1)}, s32[]{:S(2)}) async-start(s8[6291456]{0:T(1024)(128)(4,1)} %bitcast.136), calls=%async_computation.3 | async-start | bytes 8388608
  158.8 3.5 copy-start.54
  158.8 7.1 %slice-start.1 = ((s8[6291456]{0:T(1024)(128)(4,1)}), s8[2097152]{0:T(1024)(128)(4,1)S(1)}, s32[]{:S(2)}) async-start(s8[6291456]{0:T(1024)(128)(4,1)} %bitcast.136), calls=%async_computation.4 | async-start | bytes 4194304
  162.3 3.1 copy-start.25
  165.4 9.2 %copy-start.35 = (bf16[4,64,768]{2,1,0:T(8,128)(2,1)}, bf16[4,64,768]{2,1,0:T(8,128)(2,1)S(1)}, u32[]{:S(2)}) copy-start(bf16[4,64,768]{2,1,0:T(8,128)(2,1)S(1)} %convolution_convert_fusion.11) | copy-start | bytes 1179652
  174.6 6.5 %copy-start.5 = (bf16[4,512,1536]{2,1,0:T(8,128)(2,1)}, bf16[4,512,1536]{2,1,0:T(8,128)(2,1)S(1)}, u32[]{:S(2)}) copy-start(bf16[4,512,1536]{2,1,0:T(8,128)(2,1)S(1)} %get-tuple-element.56) | copy-start | bytes 18874372
  187.1 11.4 %slice-start.2 = ((s8[6291456]{0:T(1024)(128)(4,1)}), s8[4194304]{0:T(1024)(128)(4,1)S(1)}, s32[]{:S(2)}) async-start(s8[6291456]{0:T(1024)(128)(4,1)} %bitcast.148), calls=%async_computation.5 | async-start | bytes 8388608
  189.6 4.1 %copy-start.23 = (bf16[1024,768]{1,0:T(8,128)(2,1)S(1)}, bf16[1024,768]{1,0:T(8,128)(2,1)}, u32[]{:S(2)}) copy-start(bf16[1024,768]{1,0:T(8,128)(2,1)} %copy-done.21) | copy-start | bytes 4718596
  189.6 4.1 %copy-start.58 = (bf16[1024,2048]{1,0:T(8,128)(2,1)S(1)}, bf16[1024,2048]{1,0:T(8,128)(2,1)}, u32[]{:S(2)}) copy-start(bf16[1024,2048]{1,0:T(8,128)(2,1)} %get-tuple-element.52) | copy-start | bytes 12582916
  189.6 8.9 %slice-start.3 = ((s8[6291456]{0:T(1024)(128)(4,1)}), s8[2097152]{0:T(1024)(128)(4,1)S(1)}, s32[]{:S(2)}) async-start(s8[6291456]{0:T(1024)(128)(4,1)} %bitcast.148), calls=%async_computation.6 | async-start | bytes 4194304
  193.6 4.9 %copy-start.14 = (bf16[4,512,768]{2,1,0:T(8,128)(2,1)S(1)}, bf16[4,512,768]{2,1,0:T(8,128)(2,1)}, u32[]{:S(2)}) copy-start(bf16[4,512,768]{2,1,0:T(8,128)(2,1)} %all-gather.2.cloned.1.call-done) | copy-start | bytes 9437188
  193.6 4.9 %copy-start.47 = (f32[4,512]{1,0:T(4,128)S(1)}, f32[4,512]{1,0:T(4,128)}, u32[]{:S(2)}) copy-start(f32[4,512]{1,0:T(4,128)} %get-tuple-element.100) | copy-start | bytes 24580
  205.2 100.6 %copy-start.36 = (bf16[4,64,768]{2,1,0:T(8,128)(2,1)S(1)}, bf16[4,64,768]{2,1,0:T(8,128)(2,1)}, u32[]{:S(2)}) copy-start(bf16[4,64,768]{2,1,0:T(8,128)(2,1)} %copy-done.35) | copy-start | bytes 1179652
  308.4 5.7 %slice-start.4 = ((s8[4718592]{0:T(1024)(128)(4,1)}), s8[4194304]{0:T(1024)(128)(4,1)S(1)}, s32[]{:S(2)}) async-start(s8[4718592]{0:T(1024)(128)(4,1)} %bitcast.161), calls=%async_computation.7 | async-start | bytes 8388608
  311.1 3.1 slice-start.5
  311.1 3.1 copy-start.29
  314.1 5.6 %copy-start.9 = (bf16[4,256,768]{2,1,0:T(8,128)(2,1)S(1)}, bf16[4,256,768]{2,1,0:T(8,128)(2,1)}, u32[]{:S(2)}) copy-start(bf16[4,256,768]{2,1,0:T(8,128)(2,1)} %param.19) | copy-start | bytes 4718596
  314.2 5.6 %copy-start.39 = (pred[4,64,256]{1,2,0:T(32,128)(4,1)S(1)}, pred[4,64,256]{1,2,0:T(32,128)(4,1)}, u32[]{:S(2)}) copy-start(pred[4,64,256]{1,2,0:T(32,128)(4,1)} %iota_compare_fusion.5) | copy-start | bytes 196612
  326.2 64.3 %copy-start.44 = (f32[4,256]{1,0:T(4,128)S(1)}, f32[4,256]{1,0:T(4,128)}, u32[]{:S(2)}) copy-start(f32[4,256]{1,0:T(4,128)} %get-tuple-element.102) | copy-start | bytes 12292
  390.5 5.0 %copy-start.1 = (bf16[768,1536]{1,0:T(8,128)(2,1)S(1)}, bf16[768,1536]{1,0:T(8,128)(2,1)}, u32[]{:S(2)}) copy-start(bf16[768,1536]{1,0:T(8,128)(2,1)} %param.25) | copy-start | bytes 7077892
  (22 other events, 45.1 us)
Sparse Core Ops, SparseCore 0:
  10.9 82.5 all-gather.1
  181.3 86.4 reduce-scatter.1
